TPU v7x, 768 devices: a whole 4x8x12 slice. The times are simulated.
768 devices in a mesh: seq: 192 (over y, x_hi, z), tp: 4 (over x_lo, core).
Axes of the slice: x: 4 (x_hi: 2, x_lo: 2; x = x_hi * 2 + x_lo), y: 8, z: 12, core: 2. Of those that a mesh axis runs over, the one named last changes fastest.
Arguments:
- hidden: bfloat16 [49152, 4096], P('seq', 'tp'), may hold values from -6 to 6
- in_proj: bfloat16 [4096, 1024], P('tp'), may hold values from -0.09375 to 0.09375
- norm_gain: float32 [1024], replicated, may hold values from 0.25 to 1.75
- head_weight: bfloat16 [1024, 2048], P(None, 'tp'), may hold values from -0.625 to 0.625
- code_ids: int32 [49152], P('seq'), may hold values from 0 to 2047
- stream_mask: int32 [49152], P('seq'), may hold values from 0 to 1
Outputs:
- hidden_grad: bfloat16 [49152, 4096], P('seq', 'tp')
- weight_grads: float32 [4, 3072, 512], P('tp', 'seq')
All inputs are finite; a program needn't handle non-finite values.
Results may differ from a plain program's by a relative error of at most 0.029.
Values may be sent and summed in bfloat16 or wider, within the bound.
No kernel may reach another device: no remote copies, remote signals or barrier semaphores. Data moves between devices by JAX's collectives and lax.ppermute only.
A program may use at most 64 MiB of HBM per device.

v0:
```python
import jax
import jax.numpy as jnp
from jax import lax
from jax.sharding import PartitionSpec as P

norm_eps = 1e-05
loss_scale = 16.0


def normalize(projected, norm_gain):
    inv_rms = lax.rsqrt(jnp.mean(projected * projected, axis=1, keepdims=True) + norm_eps)
    unit_rows = projected * inv_rms
    normed = (unit_rows * norm_gain[None, :]).astype(jnp.bfloat16)
    return (inv_rms, unit_rows, normed)


def norm_backward(normed_grad, norm_gain, inv_rms, unit_rows):
    scaled_grad = normed_grad * norm_gain[None, :]
    centred = scaled_grad - unit_rows * jnp.mean(scaled_grad * unit_rows, axis=1, keepdims=True)
    return (inv_rms * centred).astype(jnp.bfloat16)


def local(hidden, in_proj, norm_gain, head_weight, code_ids, stream_mask):
    frames = hidden.shape[0]
    vocab_part = head_weight.shape[1]
    partial_x = jnp.dot(hidden, in_proj, preferred_element_type=jnp.float32)
    x_whole = lax.psum(partial_x.astype(jnp.bfloat16), "tp").astype(jnp.float32)
    inv_rms, unit_rows, normed = normalize(x_whole, norm_gain)
    logits = jnp.dot(normed, head_weight, preferred_element_type=jnp.float32)
    exp_logits = jnp.exp(logits)
    exp_total = lax.psum(jnp.sum(exp_logits, axis=1), "tp")
    local_code = code_ids - lax.axis_index("tp") * vocab_part
    columns = lax.broadcasted_iota(jnp.int32, (frames, vocab_part), 1)
    onehot = (columns == local_code[:, None]).astype(jnp.float32)
    weighting = stream_mask.astype(jnp.float32)[:, None]
    dlogit = (weighting * (exp_logits / exp_total[:, None] - onehot)).astype(jnp.bfloat16)
    head_grad = lax.dot_general(
        normed, dlogit, (((0,), (0,)), ((), ())), preferred_element_type=jnp.float32
    )
    partial_grad = lax.dot_general(
        dlogit, head_weight, (((1,), (1,)), ((), ())), preferred_element_type=jnp.float32
    )
    grad_whole = lax.psum(partial_grad.astype(jnp.bfloat16), "tp").astype(jnp.float32)
    row_grad = norm_backward(grad_whole, norm_gain, inv_rms, unit_rows)
    hidden_grad = (
        loss_scale
        * lax.dot_general(
            row_grad, in_proj, (((1,), (1,)), ((), ())), preferred_element_type=jnp.float32
        )
    ).astype(jnp.bfloat16)
    proj_grad = lax.dot_general(
        hidden, row_grad, (((0,), (0,)), ((), ())), preferred_element_type=jnp.float32
    )
    flat_grads = jnp.concatenate([proj_grad.reshape(-1, vocab_part), head_grad], axis=0)
    summed_grads = lax.psum_scatter(flat_grads, "seq", scatter_dimension=0, tiled=True)
    return (hidden_grad, summed_grads[None])


def solution(mesh):
    in_specs = (P("seq", "tp"), P("tp", None), P(), P(None, "tp"), P("seq"), P("seq"))
    out_specs = (P("seq", "tp"), P("tp", "seq", None))
    return jax.shard_map(local, mesh=mesh, in_specs=in_specs, out_specs=out_specs, check_vma=False)
```

profile of v0, /device:TPU:2, one launch (start us, length us, event | category | flops | bytes accessed | tf_op | source)
XLA Modules:
  0.0 1252.5 jit_solution(10812593946052091729)
XLA Ops:
  7.2 0.0 copy-start
  7.2 0.0 copy-start.5
  7.2 0.0 copy-start.6
  7.2 0.0 copy-start.4
  7.2 0.0 all-reduce.3.cloned.1.call-start
  7.3 1.5 copy-done
  8.8 2.5 convolution_convert_fusion.1
  11.3 0.0 all-reduce.3.cloned.1.call-update
  11.3 0.0 all-reduce.5.cloned.1.call-start
  11.4 0.0 copy-done.5
  11.4 0.0 copy-done.6
  11.4 60.6 %all-reduce.3.cloned.1.call-done = bf16[256,1024]{1,0:T(8,128)(2,1)} async-done(((bf16[256,1024]{1,0:T(8,128)(2,1)}), bf16[256,1024]{1,0:T(8,128)(2,1)}) %all-reduce.3.cloned.1.call-update) | async-done | bytes 524304 | tf_op jit(solution)/shard_map/psum | solution.py:27
  72.0 1.2 fusion.9
  73.2 0.0 copy-done.4
  73.3 2.7 fusion.15
  75.9 0.0 copy-start.1
  75.9 7.8 psum.22
  83.7 2.7 convolution_convert_fusion
  86.4 0.0 all-reduce.5.cloned.1.call-update
  86.4 0.0 copy-start.3
  86.5 0.0 reduce-scatter.2.cloned.1.call-start
  86.5 0.0 copy-done.1
  86.5 3.0 fusion.10
  89.5 50.7 %all-reduce.5.cloned.1.call-done = bf16[256,1024]{1,0:T(8,128)(2,1)} async-done(((bf16[256,1024]{1,0:T(8,128)(2,1)}), bf16[256,1024]{1,0:T(8,128)(2,1)}) %all-reduce.5.cloned.1.call-update) | async-done | bytes 524304 | tf_op jit(solution)/shard_map/psum | solution.py:43
  140.3 1.4 fusion.5
  141.6 0.0 copy-done.3
  141.7 3.9 convolution_bitcast_fusion
  145.6 5.3 copy.8
  150.9 5.0 reshape.23
  155.9 6.2 pad_maximum_fusion
  162.1 0.0 copy-start.2
  162.1 0.0 reduce-scatter.2.cloned.1.call-update
  162.1 1.0 copy-done.2
  163.1 1.6 fusion.3
  164.7 1081.2 %reduce-scatter.2.cloned.1.call-done = f32[16,512]{1,0:T(8,128)} async-done(((f32[3072,512]{1,0:T(8,128)}), f32[16,512]{1,0:T(8,128)}) %reduce-scatter.2.cloned.1.call-update) | async-done | bytes 32784 | tf_op jit(solution)/shard_map/reduce_scatter | solution.py:55
  (4 shorter events, 0.0 us)
Async XLA Ops:
  7.2 1.6 copy-start
  7.2 4.2 copy-start.5
  7.2 4.2 copy-start.6
  7.2 66.1 %copy-start.4 = (f32[1024]{0:T(1024)S(1)}, f32[1024]{0:T(1024)}, u32[]{:S(2)}) copy-start(f32[1024]{0:T(1024)} %param.8) | copy-start | bytes 12292
  7.2 64.8 %all-reduce.3.cloned.1.call-start = ((), (), s32[]{:S(2)}) async-start(), calls=%async_computation.1 | async-start | bytes 1048576 | tf_op jit(solution)/shard_map/psum | solution.py:27
  11.3 128.9 %all-reduce.5.cloned.1.call-start = ((), (), s32[]{:S(2)}) async-start(), calls=%async_computation.2 | async-start | bytes 1048576 | tf_op jit(solution)/shard_map/psum | solution.py:43
  75.9 10.6 copy-start.1
  86.4 55.2 %copy-start.3 = (bf16[256,1024]{1,0:T(8,128)(2,1)S(1)}, bf16[256,1024]{1,0:T(8,128)(2,1)}, u32[]{:S(2)}) copy-start(bf16[256,1024]{1,0:T(8,128)(2,1)} %param.6) | copy-start | bytes 1572868
  86.5 1159.5 %reduce-scatter.2.cloned.1.call-start = ((), (), s32[]{:S(2)}) async-start(), calls=%async_computation.3 | async-start | bytes 6324224 | tf_op jit(solution)/shard_map/reduce_scatter | solution.py:55
  162.1 1.0 copy-start.2
Sparse Core Ops, SparseCore 0:
  11.8 60.1 all-reduce.2
  86.6 53.6 all-reduce.4
  162.3 1083.6 reduce-scatter.1
where the time goes:
time: 1250 us
  waiting for transfers between devices  1190 us (95%)
  matrix products  16.5 us (1%)
  between operations  13.9 us (1%)
  local copies, waits for them, and re-layouts  12.9 us (1%)
    reduce_scatter x1, waiting for transfers between devices, local(): lax.psum_scatter(flat_grads, 'seq', scatter_dimension=0, tiled=True)  1080 us
    psum x1, waiting for transfers between devices, local(): x_whole = lax.psum(partial_x.astype(jnp.bfloat16), 'tp').astype(jnp.float32)  60.6 us
    psum x1, waiting for transfers between devices, local(): lax.psum(partial_grad.astype(jnp.bfloat16), 'tp').astype(jnp.float32)  50.7 us
  transfers between devices with their start and end apart: 3, of which 3 were waited for; matrix products, arithmetic and copies ran while one was open for 0% of the time, Pallas kernels for 0%

commit v1 on v0

v1 whole, which is shorter than its diff:
```python
import jax
import jax.numpy as jnp
from jax import lax
from jax.sharding import Mesh
from jax.sharding import PartitionSpec as P

norm_eps = 1e-05
loss_scale = 16.0

AXES = ("yh", "yl", "xh", "zh", "zl", "xl", "core")
SIZES = (4, 2, 2, 6, 2, 2, 2)
SEQ = ("yh", "yl", "xh", "zh", "zl")
TP = ("xl", "core")
NEAR = ("yl", "xh", "zl")
FAR = ("yh", "zh")
N_TP = 4
N_NEAR = 8
N_FAR = 24
BLOCKS = 192
PROJ_BLOCKS = 128
f32 = jnp.float32
bf16 = jnp.bfloat16


def dot(a, b, ca, cb):
    return lax.dot_general(a, b, (((ca,), (cb,)), ((), ())), preferred_element_type=f32)


def local(hidden, in_proj, norm_gain, head_weight, code_ids, stream_mask):
    frames, width = hidden.shape[0], in_proj.shape[1]
    vocab_part = head_weight.shape[1]
    own = frames // N_TP
    tp = lax.axis_index(TP)
    gain = norm_gain[None, :]

    partial_x = dot(hidden, in_proj, 1, 0).astype(bf16)
    pieces = lax.all_to_all(partial_x.reshape(N_TP, own, width), TP, 0, 0)
    x = jnp.sum(pieces.astype(f32), axis=0)
    inv_rms = lax.rsqrt(jnp.mean(x * x, axis=1, keepdims=True) + norm_eps)
    unit_rows = x * inv_rms
    normed = lax.all_gather((unit_rows * gain).astype(bf16), TP, tiled=True)

    exp_logits = jnp.exp(dot(normed, head_weight, 1, 0))
    totals = lax.all_gather(jnp.sum(exp_logits, axis=1), TP)
    exp_total = jnp.sum(totals, axis=0)[:, None]
    columns = lax.broadcasted_iota(jnp.int32, (frames, vocab_part), 1) + tp * vocab_part
    onehot = (columns == code_ids[:, None]).astype(f32)
    weighting = stream_mask.astype(f32)[:, None]
    dlogit = (weighting * (exp_logits / exp_total - onehot)).astype(bf16)

    partial_grad = dot(dlogit, head_weight, 1, 1).astype(bf16)
    pieces = lax.all_to_all(partial_grad.reshape(N_TP, own, width), TP, 0, 0)
    head_grad = dot(normed, dlogit, 0, 0).astype(bf16)
    scaled_grad = jnp.sum(pieces.astype(f32), axis=0) * gain
    centred = scaled_grad - unit_rows * jnp.mean(scaled_grad * unit_rows, axis=1, keepdims=True)
    own_grad = (inv_rms * centred).astype(bf16)
    row_grad = lax.all_to_all(
        jnp.broadcast_to(own_grad[None], (N_TP, own, width)), TP, 0, 0
    ).reshape(frames, width)

    proj_grad = dot(hidden, row_grad, 0, 0).astype(bf16)
    proj_blocks = proj_grad.reshape(PROJ_BLOCKS, 8, width)
    head_blocks = head_grad.reshape(BLOCKS - PROJ_BLOCKS, 2, 8, vocab_part)
    head_blocks = jnp.transpose(head_blocks, (0, 2, 1, 3)).reshape(BLOCKS - PROJ_BLOCKS, 8, width)
    blocks = jnp.concatenate([proj_blocks, head_blocks], axis=0)
    blocks = blocks.reshape(4, 2, 2, 6, 2, 8, width)
    blocks = jnp.transpose(blocks, (1, 2, 4, 0, 3, 5, 6)).reshape(N_NEAR, N_FAR * 8, width)
    near = lax.all_to_all(blocks, NEAR, 0, 0)
    near = jnp.sum(near.astype(f32), axis=0).astype(bf16).reshape(N_FAR, 8, width)
    far = lax.all_to_all(near, FAR, 0, 0)
    summed = jnp.sum(far.astype(f32), axis=0)
    as_proj = summed.reshape(16, vocab_part)
    as_head = jnp.concatenate([summed[:, :vocab_part], summed[:, vocab_part:]], axis=0)
    weight_grads = jnp.where(lax.axis_index(SEQ) < PROJ_BLOCKS, as_proj, as_head)

    hidden_grad = (loss_scale * dot(row_grad, in_proj, 1, 1)).astype(bf16)
    return (hidden_grad, weight_grads[None])


def solution(mesh):
    fine = Mesh(mesh.devices.reshape(SIZES), AXES)
    in_specs = (P(SEQ, TP), P(TP, None), P(), P(None, TP), P(SEQ), P(SEQ))
    out_specs = (P(SEQ, TP), P(TP, SEQ, None))
    return jax.shard_map(local, mesh=fine, in_specs=in_specs, out_specs=out_specs, check_vma=False)
```

time: 1250 us -> 150 us (0.12)
  the two profiles are of different devices: /device:TPU:2 before, /device:TPU:8 now
where the time goes in v1:
time: 150 us; the launch traced here: 149 us
  blocking collectives  73.5 us (49%)
  waiting for transfers between devices  35 us (23%)
  starting transfers between devices  20.3 us (14%)
  matrix products  11.8 us (8%)
  other arithmetic  5.02 us (3%)
  local copies, waits for them, and re-layouts  2.79 us (2%)
    all_to_all x1, blocking collectives, local(): near = lax.all_to_all(blocks, NEAR, 0, 0)  50.6 us
    all_to_all x1, waiting for transfers between devices, local(): far = lax.all_to_all(near, FAR, 0, 0)  20.1 us
    all_to_all x1, starting transfers between devices, local(): far = lax.all_to_all(near, FAR, 0, 0)  13.4 us
    dot_general x6, matrix products, dot(): lax.dot_general(a, b, (((ca,), (cb,)), ((), ())), preferred_element_type=...  11.8 us
    all_to_all x1, blocking collectives, local(): pieces = lax.all_to_all(partial_grad.reshape(N_TP, own, width), TP, 0, 0)  11.2 us
    all_to_all x1, waiting for transfers between devices, local(): pieces = lax.all_to_all(partial_x.reshape(N_TP, own, width), TP, 0, 0)  8.75 us
    all_gather x1, blocking collectives, local(): normed = lax.all_gather((unit_rows * gain).astype(bf16), TP, tiled=True)  6.58 us
    all_to_all x1, waiting for transfers between devices, local(): lax.all_to_all(jnp.broadcast_to(own_grad[None], (N_TP, own, width)), TP,...  6.18 us
  transfers between devices with their start and end apart: 3, of which 3 were waited for; matrix products, arithmetic and copies ran while one was open for 3% of the time, Pallas kernels for 0%

profile of v1, /device:TPU:8, one launch (start us, length us, event | category | flops | bytes accessed | tf_op | source)
XLA Modules:
  0.0 149.2 jit_solution(2022506041073714042)
XLA Ops:
  0.6 0.0 copy-start
  0.6 0.0 copy-start.4
  0.7 0.0 copy-start.3
  0.7 1.6 %copy-done = bf16[1024,1024]{1,0:T(8,128)(2,1)S(1)} copy-done((bf16[1024,1024]{1,0:T(8,128)(2,1)S(1)}, bf16[1024,1024]{1,0:T(8,128)(2,1)}, u32[]{:S(2)}) %copy-start) | copy-done | bytes 2097176
  2.2 2.5 %convolution_convert_fusion.2 = bf16[256,1024]{1,0:T(8,128)(2,1)} fusion(bf16[256,1024]{1,0:T(8,128)(2,1)} %param.6, bf16[1024,1024]{1,0:T(8,128)(2,1)S(1)} %copy-done), kind=kOutput, calls=%fused_computation.5 | convolution fusion | flops 537133056 | bytes 3145728 | tf_op jit(solution)/shard_map/dot_general | solution.py:26
  4.8 3.5 %all-to-all-start = ((bf16[4,64,1024]{2,1,0:T(8,128)(2,1)}), bf16[4,64,1024]{2,1,0:T(8,128)(2,1)S(1)}, u32[]{:S(2)}, u32[]{:S(2)}) async-start(bf16[4,64,1024]{2,1,0:T(8,128)(2,1)} %bitcast), calls=%async_computation | async-start | bytes 1048576 | tf_op jit(solution)/shard_map/all_to_all | solution.py:37
  8.3 0.0 copy-done.4
  8.3 0.0 copy-start.5
  8.3 8.8 %all-to-all-done = bf16[4,64,1024]{2,1,0:T(8,128)(2,1)S(1)} async-done(((bf16[4,64,1024]{2,1,0:T(8,128)(2,1)}), bf16[4,64,1024]{2,1,0:T(8,128)(2,1)S(1)}, u32[]{:S(2)}, u32[]{:S(2)}) %all-to-all-start) | async-done | bytes 524320 | tf_op jit(solution)/shard_map/all_to_all | solution.py:37
  17.1 0.0 copy-start.1
  17.1 0.1 convert_reduce_fusion.1
  17.1 0.1 multiply_reduce_fusion.1
  17.3 0.0 copy-done.3
  17.3 0.1 multiply_convert_fusion.2
  17.4 6.6 %all_gather.9 = bf16[256,1024]{1,0:T(8,128)(2,1)S(1)} all-gather(bf16[64,1024]{1,0:T(8,128)(2,1)S(1)} %multiply_convert_fusion.2), channel_id=1, replica_groups=mesh['yh'=4,'yl'=2,'xh'=2,'zh'=6,'zl'=2,'xl'=2,'core'=2] {'xl','core'}, dimensions={0}, use_global_device_ids=true | all-gather | bytes 655360 | tf_op jit(solution)/shard_map/all_gather | solution.py:41
  24.0 0.0 copy-done.1
  24.0 1.3 fusion.1
  25.2 5.1 %all-gather.1 = f32[4,1,256]{2,1,0:T(1,128)S(1)} all-gather(f32[1,1,256]{2,1,0:T(1,128)S(1)} %bitcast.38), channel_id=2, replica_groups=mesh['yh'=4,'yl'=2,'xh'=2,'zh'=6,'zl'=2,'xl'=2,'core'=2] {'xl','core'}, dimensions={0}, use_global_device_ids=true | all-gather | bytes 5120 | tf_op jit(solution)/shard_map/all_gather | solution.py:44
  30.3 0.0 copy-done.5
  30.3 1.9 %convolution_convert_fusion.1 = bf16[256,1024]{1,0:T(8,128)(2,1)S(1)} fusion(bf16[1024,512]{1,0:T(8,128)(2,1)} %param.9, f32[256,512]{1,0:T(8,128)} %get-tuple-element.5, s32[512]{0:T(512)S(1)} %iota_add_fusion, f32[256]{0:T(256)S(1)} %reduce_sum.78, f32[256]{0:T(256)S(1)} %convert_element_type.50, s32[256]{0:T(256)S(1)} %copy-done.5), kind=kOutput, calls=%fused_computation.4 | convolution fusion | flops 269484032 | bytes 2102272 | tf_op jit(solution)/shard_map/dot_general | solution.py:26
  32.2 11.2 %all_to_all.25 = bf16[4,64,1024]{2,1,0:T(8,128)(2,1)S(1)} all-to-all(bf16[4,64,1024]{2,1,0:T(8,128)(2,1)S(1)} %bitcast.37), channel_id=1, replica_groups=mesh['yh'=4,'yl'=2,'xh'=2,'zh'=6,'zl'=2,'xl'=2,'core'=2] {'xl','core'}, dimensions={0} | all-to-all | bytes 1048576 | tf_op jit(solution)/shard_map/all_to_all | solution.py:52
  43.5 0.1 convert_reduce_fusion
  43.6 0.2 multiply_reduce_fusion
  43.8 0.1 multiply_convert_fusion.1
  43.9 0.9 broadcast_in_dim.2
  44.8 3.5 %all-to-all-start.2 = ((bf16[4,64,1024]{2,1,0:T(8,128)(2,1)}), bf16[4,64,1024]{2,1,0:T(8,128)(2,1)S(1)}, u32[]{:S(2)}, u32[]{:S(2)}) async-start(bf16[4,64,1024]{2,1,0:T(8,128)(2,1)} %broadcast_in_dim.2), calls=%async_computation.2 | async-start | bytes 1048576 | tf_op jit(solution)/shard_map/all_to_all | solution.py:57
  48.2 2.6 %convolution_convert_fusion = bf16[1024,512]{1,0:T(8,128)(2,1)} fusion(bf16[256,1024]{1,0:T(8,128)(2,1)S(1)} %all_gather.9, f32[256,512]{1,0:T(8,128)} %get-tuple-element.5, s32[512]{0:T(512)S(1)} %iota_add_fusion, f32[256]{0:T(256)S(1)} %reduce_sum.78, f32[256]{0:T(256)S(1)} %convert_element_type.50, s32[256]{0:T(256)S(1)} %copy-done.5), kind=kOutput, calls=%fused_computation.2 | convolution fusion | flops 269746176 | bytes 2102272 | tf_op jit(solution)/shard_map/dot_general | solution.py:26
  50.9 6.2 %all-to-all-done.2 = bf16[4,64,1024]{2,1,0:T(8,128)(2,1)S(1)} async-done(((bf16[4,64,1024]{2,1,0:T(8,128)(2,1)}), bf16[4,64,1024]{2,1,0:T(8,128)(2,1)S(1)}, u32[]{:S(2)}, u32[]{:S(2)}) %all-to-all-start.2) | async-done | bytes 524320 | tf_op jit(solution)/shard_map/all_to_all | solution.py:57
  57.1 0.0 copy-start.2
  57.1 1.9 %convert_bitcast_fusion = bf16[128,8,1024]{2,1,0:T(8,128)(2,1)S(1)} fusion(bf16[256,1024]{1,0:T(8,128)(2,1)S(1)} %bitcast.34, bf16[256,1024]{1,0:T(8,128)(2,1)} %param.6), kind=kOutput, calls=%fused_computation.1 | convolution fusion | flops 537919488 | bytes 3145728 | tf_op jit(solution)/shard_map/dot_general | solution.py:26
  58.9 0.0 copy-done.2
  59.0 0.3 pad_maximum_fusion
  59.2 0.3 copy.10
  59.6 50.6 %all_to_all.26 = bf16[8,192,1024]{2,1,0:T(8,128)(2,1)} all-to-all(bf16[8,192,1024]{2,1,0:T(8,128)(2,1)S(1)} %bitcast.33), channel_id=1, replica_groups=mesh['yh'=4,'yl'=2,'xh'=2,'zh'=6,'zl'=2,'xl'=2,'core'=2] {'yl','xh','zl'}, dimensions={0} | all-to-all | bytes 6291456 | tf_op jit(solution)/shard_map/all_to_all | solution.py:68
  110.2 3.3 %reduce_sum.81 = bf16[192,1024]{1,0:T(8,128)(2,1)} reduce(bf16[8,192,1024]{2,1,0:T(8,128)(2,1)} %all_to_all.26, bf16[]{:T(256)} %constant.47.clone.1), dimensions={0}, to_apply=%region_6.0 | reduce | flops 1376256 | bytes 3538946 | tf_op jit(solution)/shard_map/reduce_sum | solution.py:69
  113.5 13.4 %all-to-all-start.4 = ((bf16[24,8,1024]{2,1,0:T(8,128)(2,1)}), bf16[24,8,1024]{2,1,0:T(8,128)(2,1)S(1)}, u32[]{:S(2)}, u32[]{:S(2)}) async-start(bf16[24,8,1024]{2,1,0:T(8,128)(2,1)} %bitcast.12), calls=%async_computation.4 | async-start | bytes 786432 | tf_op jit(solution)/shard_map/all_to_all | solution.py:70
  126.9 1.5 %fusion = bf16[256,1024]{1,0:T(8,128)(2,1)} fusion(bf16[256,1024]{1,0:T(8,128)(2,1)S(1)} %bitcast.35, bf16[1024,1024]{1,0:T(8,128)(2,1)S(1)} %copy-done), kind=kOutput, calls=%fused_computation.6 | convolution fusion | flops 537395200 | bytes 3145728 | tf_op jit(solution)/shard_map/dot_general | solution.py:26
  128.4 20.1 %all-to-all-done.4 = bf16[24,8,1024]{2,1,0:T(8,128)(2,1)S(1)} async-done(((bf16[24,8,1024]{2,1,0:T(8,128)(2,1)}), bf16[24,8,1024]{2,1,0:T(8,128)(2,1)S(1)}, u32[]{:S(2)}, u32[]{:S(2)}) %all-to-all-start.4) | async-done | bytes 393248 | tf_op jit(solution)/shard_map/all_to_all | solution.py:70
  148.5 0.1 convert_reduce_fusion.2
  148.6 0.6 maximum_select_fusion
  (7 shorter events, 0.1 us)
Async XLA Ops:
  0.6 1.6 %copy-start = (bf16[1024,1024]{1,0:T(8,128)(2,1)S(1)}, bf16[1024,1024]{1,0:T(8,128)(2,1)}, u32[]{:S(2)}) copy-start(bf16[1024,1024]{1,0:T(8,128)(2,1)} %param.7) | copy-start | bytes 6291460
  0.6 7.6 %copy-start.4 = (s32[256]{0:T(256)S(1)}, s32[256]{0:T(256)}, u32[]{:S(2)}) copy-start(s32[256]{0:T(256)} %param.11) | copy-start | bytes 3076
  0.7 16.6 %copy-start.3 = (f32[1024]{0:T(1024)S(1)}, f32[1024]{0:T(1024)}, u32[]{:S(2)}) copy-start(f32[1024]{0:T(1024)} %param.8) | copy-start | bytes 12292
  4.8 12.3 %all-to-all-start = ((bf16[4,64,1024]{2,1,0:T(8,128)(2,1)}), bf16[4,64,1024]{2,1,0:T(8,128)(2,1)S(1)}, u32[]{:S(2)}, u32[]{:S(2)}) async-start(bf16[4,64,1024]{2,1,0:T(8,128)(2,1)} %bitcast), calls=%async_computation | async-start | bytes 1048576 | tf_op jit(solution)/shard_map/all_to_all | solution.py:37
  8.3 22.0 %copy-start.5 = (s32[256]{0:T(256)S(1)}, s32[256]{0:T(256)}, u32[]{:S(2)}) copy-start(s32[256]{0:T(256)} %param.10) | copy-start | bytes 3076
  17.1 6.9 %copy-start.1 = (bf16[1024,512]{1,0:T(8,128)(2,1)S(1)}, bf16[1024,512]{1,0:T(8,128)(2,1)}, u32[]{:S(2)}) copy-start(bf16[1024,512]{1,0:T(8,128)(2,1)} %param.9) | copy-start | bytes 3145732
  44.8 12.3 %all-to-all-start.2 = ((bf16[4,64,1024]{2,1,0:T(8,128)(2,1)}), bf16[4,64,1024]{2,1,0:T(8,128)(2,1)S(1)}, u32[]{:S(2)}, u32[]{:S(2)}) async-start(bf16[4,64,1024]{2,1,0:T(8,128)(2,1)} %broadcast_in_dim.2), calls=%async_computation.2 | async-start | bytes 1048576 | tf_op jit(solution)/shard_map/all_to_all | solution.py:57
  57.1 1.9 %copy-start.2 = (bf16[1024,512]{1,0:T(8,128)(2,1)S(1)}, bf16[1024,512]{1,0:T(8,128)(2,1)}, u32[]{:S(2)}) copy-start(bf16[1024,512]{1,0:T(8,128)(2,1)} %convolution_convert_fusion) | copy-start | bytes 3145732
  113.5 35.0 %all-to-all-start.4 = ((bf16[24,8,1024]{2,1,0:T(8,128)(2,1)}), bf16[24,8,1024]{2,1,0:T(8,128)(2,1)S(1)}, u32[]{:S(2)}, u32[]{:S(2)}) async-start(bf16[24,8,1024]{2,1,0:T(8,128)(2,1)} %bitcast.12), calls=%async_computation.4 | async-start | bytes 786432 | tf_op jit(solution)/shard_map/all_to_all | solution.py:70

commit v2 on v1

v2 whole, which is shorter than its diff:
```python
import jax
import jax.numpy as jnp
from jax import lax
from jax.sharding import Mesh
from jax.sharding import PartitionSpec as P

norm_eps = 1e-05
loss_scale = 16.0

AXES = ("yh", "yl", "xh", "zh", "zl", "xl", "core")
SIZES = (4, 2, 2, 6, 2, 2, 2)
SEQ = ("yh", "yl", "xh", "zh", "zl")
TP = ("xl", "core")
NEAR = ("yl", "xh", "zl")
N_TP = 4
N_NEAR = 8
BLOCKS = 192
PROJ_BLOCKS = 128
f32 = jnp.float32
bf16 = jnp.bfloat16


def dot(a, b, ca, cb):
    return lax.dot_general(a, b, (((ca,), (cb,)), ((), ())), preferred_element_type=f32)


def add_up(pieces):
    total = pieces[0].astype(f32)
    for i in range(1, pieces.shape[0]):
        total = total + pieces[i].astype(f32)
    return total


def near_sum(blocks, n_yh):
    blocks = blocks.reshape(n_yh, 2, 2, 6, 2, 8, blocks.shape[-1])
    blocks = jnp.transpose(blocks, (1, 2, 4, 0, 3, 5, 6)).reshape(N_NEAR, n_yh * 6 * 8, -1)
    near = add_up(lax.all_to_all(blocks, NEAR, 0, 0)).astype(bf16)
    return near.reshape(n_yh, 6, 8, near.shape[-1])


def local(hidden, in_proj, norm_gain, head_weight, code_ids, stream_mask):
    frames, width = hidden.shape[0], in_proj.shape[1]
    vocab_part = head_weight.shape[1]
    own = frames // N_TP
    tp = lax.axis_index(TP)
    gain = norm_gain[None, :]

    partial_x = dot(hidden, in_proj, 1, 0).astype(bf16)
    x = add_up(lax.all_to_all(partial_x.reshape(N_TP, own, width), TP, 0, 0))
    inv_rms = lax.rsqrt(jnp.mean(x * x, axis=1, keepdims=True) + norm_eps)
    unit_rows = x * inv_rms
    normed = lax.all_gather((unit_rows * gain).astype(bf16), TP, tiled=True)

    exp_logits = jnp.exp(dot(normed, head_weight, 1, 0))
    totals = lax.all_gather(jnp.sum(exp_logits, axis=1), TP)
    exp_total = jnp.sum(totals, axis=0)[:, None]
    columns = lax.broadcasted_iota(jnp.int32, (frames, vocab_part), 1) + tp * vocab_part
    onehot = (columns == code_ids[:, None]).astype(f32)
    weighting = stream_mask.astype(f32)[:, None]
    dlogit = (weighting * (exp_logits / exp_total - onehot)).astype(bf16)

    partial_grad = dot(dlogit, head_weight, 1, 1).astype(bf16)
    pieces = lax.all_to_all(partial_grad.reshape(N_TP, own, width), TP, 0, 0)

    head_grad = dot(normed, dlogit, 0, 0).astype(bf16)
    head_blocks = head_grad.reshape(BLOCKS - PROJ_BLOCKS, 2, 8, vocab_part)
    head_blocks = jnp.transpose(head_blocks, (0, 2, 1, 3)).reshape(BLOCKS - PROJ_BLOCKS, 8, width)
    head_blocks = jnp.pad(head_blocks, ((PROJ_BLOCKS - 96, 0), (0, 0), (0, 0)))
    head_near = near_sum(head_blocks, 2)

    scaled_grad = add_up(pieces) * gain
    centred = scaled_grad - unit_rows * jnp.mean(scaled_grad * unit_rows, axis=1, keepdims=True)
    row_grad = lax.all_gather((inv_rms * centred).astype(bf16), TP, tiled=True)

    proj_grad = dot(hidden, row_grad, 0, 0).astype(bf16)
    proj_blocks = jnp.pad(proj_grad.reshape(PROJ_BLOCKS, 8, width), ((0, 144 - PROJ_BLOCKS), (0, 0), (0, 0)))
    proj_near = near_sum(proj_blocks, 3)
    hidden_grad = (loss_scale * dot(row_grad, in_proj, 1, 1)).astype(bf16)

    near_place = (lax.axis_index("yl") * 2 + lax.axis_index("xh")) * 12 + lax.axis_index("zl")
    mixed = 96 + near_place + 2 * jnp.arange(6)
    third = jnp.where((mixed < PROJ_BLOCKS)[:, None, None], proj_near[2], head_near[0])
    near = jnp.concatenate([proj_near[:2], third[None], head_near[1:]], axis=0)
    far = add_up(lax.all_to_all(near, "yh", 0, 0)).astype(bf16)
    summed = add_up(lax.all_to_all(far, "zh", 0, 0))
    block = lax.axis_index(SEQ)
    as_proj = summed.reshape(16, vocab_part)
    as_head = jnp.concatenate([summed[:, :vocab_part], summed[:, vocab_part:]], axis=0)
    weight_grads = jnp.where(block < PROJ_BLOCKS, as_proj, as_head)
    return (hidden_grad, weight_grads[None])


def solution(mesh):
    fine = Mesh(mesh.devices.reshape(SIZES), AXES)
    in_specs = (P(SEQ, TP), P(TP, None), P(), P(None, TP), P(SEQ), P(SEQ))
    out_specs = (P(SEQ, TP), P(TP, SEQ, None))
    return jax.shard_map(local, mesh=fine, in_specs=in_specs, out_specs=out_specs, check_vma=False)
```

time: 150 us -> 165 us (1.10)
  the two profiles are of different devices: /device:TPU:8 before, /device:TPU:70 now
where the time goes in v2:
time: 165 us; the launch traced here: 164 us
  waiting for transfers between devices  65.2 us (40%)
  starting transfers between devices  41.9 us (25%)
  blocking collectives  34.1 us (21%)
  matrix products  10.8 us (7%)
  other arithmetic  6.57 us (4%)
  local copies, waits for them, and re-layouts  4.99 us (3%)
    all_to_all x2, waiting for transfers between devices, near_sum(): near = add_up(lax.all_to_all(blocks, NEAR, 0, 0)).astype(bf16)  31.4 us
    all_gather x1, blocking collectives, local(): row_grad = lax.all_gather((inv_rms * centred).astype(bf16), TP, tiled=True)  21.7 us
    all_to_all x2, starting transfers between devices, near_sum(): near = add_up(lax.all_to_all(blocks, NEAR, 0, 0)).astype(bf16)  20.1 us
    all_to_all x1, waiting for transfers between devices, local(): far = add_up(lax.all_to_all(near, 'yh', 0, 0)).astype(bf16)  13.2 us
    dot_general x6, matrix products, dot(): lax.dot_general(a, b, (((ca,), (cb,)), ((), ())), preferred_element_type=...  10.8 us
    all_to_all x1, starting transfers between devices, local(): summed = add_up(lax.all_to_all(far, 'zh', 0, 0))  9.73 us
    all_to_all x1, waiting for transfers between devices, local(): summed = add_up(lax.all_to_all(far, 'zh', 0, 0))  9.42 us
    all_gather x1, blocking collectives, local(): normed = lax.all_gather((unit_rows * gain).astype(bf16), TP, tiled=True)  7.35 us
  transfers between devices with their start and end apart: 6, of which 5 were waited for; matrix products, arithmetic and copies ran while one was open for 6% of the time, Pallas kernels for 0%

profile of v2, /device:TPU:70, one launch (start us, length us, event | category | flops | bytes accessed | tf_op | source)
XLA Modules:
  0.0 164.4 jit_solution(6999499070855689006)
XLA Ops:
  0.6 0.0 copy-start
  0.6 0.0 copy-start.4
  0.7 0.0 copy-start.3
  0.7 1.6 copy-done
  2.2 2.5 %convolution_convert_fusion.2 = bf16[256,1024]{1,0:T(8,128)(2,1)} fusion(bf16[256,1024]{1,0:T(8,128)(2,1)} %param.6, bf16[1024,1024]{1,0:T(8,128)(2,1)S(1)} %copy-done), kind=kOutput, calls=%fused_computation.4 | convolution fusion | flops 537133056 | bytes 3145728 | tf_op jit(solution)/shard_map/dot_general | solution.py:24
  4.8 4.3 %all-to-all-start = ((bf16[4,64,1024]{2,1,0:T(8,128)(2,1)}), bf16[4,64,1024]{2,1,0:T(8,128)(2,1)S(1)}, u32[]{:S(2)}, u32[]{:S(2)}) async-start(bf16[4,64,1024]{2,1,0:T(8,128)(2,1)} %bitcast), calls=%async_computation | async-start | bytes 1048576 | tf_op jit(solution)/shard_map/all_to_all | solution.py:49
  9.0 0.0 copy-start.5
  9.0 0.0 copy-done.4
  9.1 7.2 %all-to-all-done = bf16[4,64,1024]{2,1,0:T(8,128)(2,1)S(1)} async-done(((bf16[4,64,1024]{2,1,0:T(8,128)(2,1)}), bf16[4,64,1024]{2,1,0:T(8,128)(2,1)S(1)}, u32[]{:S(2)}, u32[]{:S(2)}) %all-to-all-start) | async-done | bytes 524320 | tf_op jit(solution)/shard_map/all_to_all | solution.py:49
  16.2 0.2 fusion.1
  16.4 0.0 copy-done.3
  16.4 0.1 multiply_convert_fusion.2
  16.5 7.3 %all_gather.12 = bf16[256,1024]{1,0:T(8,128)(2,1)S(1)} all-gather(bf16[64,1024]{1,0:T(8,128)(2,1)S(1)} %multiply_convert_fusion.2), channel_id=1, replica_groups=mesh['yh'=4,'yl'=2,'xh'=2,'zh'=6,'zl'=2,'xl'=2,'core'=2] {'xl','core'}, dimensions={0}, use_global_device_ids=true | all-gather | bytes 655360 | tf_op jit(solution)/shard_map/all_gather | solution.py:52
  23.9 1.7 %fusion.4 = (f32[256]{0:T(256)S(1)}, f32[256,512]{1,0:T(8,128)S(1)}) fusion(bf16[256,1024]{1,0:T(8,128)(2,1)S(1)} %all_gather.12, bf16[1024,512]{1,0:T(8,128)(2,1)} %param.9), kind=kOutput, calls=%fused_computation.33 | convolution fusion | flops 268566272 | bytes 2098176 | tf_op jit(solution)/shard_map/dot_general | solution.py:24
  25.6 0.0 copy-start.2
  25.6 5.1 %all-gather.1 = f32[4,1,256]{2,1,0:T(1,128)S(1)} all-gather(f32[1,1,256]{2,1,0:T(1,128)S(1)} %bitcast.73), channel_id=2, replica_groups=mesh['yh'=4,'yl'=2,'xh'=2,'zh'=6,'zl'=2,'xl'=2,'core'=2] {'xl','core'}, dimensions={0}, use_global_device_ids=true | all-gather | bytes 5120 | tf_op jit(solution)/shard_map/all_gather | solution.py:55
  30.7 0.0 copy-done.5
  30.7 2.5 %convolution_convert_fusion.1 = bf16[256,1024]{1,0:T(8,128)(2,1)} fusion(bf16[1024,512]{1,0:T(8,128)(2,1)} %param.9, f32[256,512]{1,0:T(8,128)S(1)} %get-tuple-element.7, s32[512]{0:T(512)S(1)} %iota_add_fusion, f32[256]{0:T(256)S(1)} %reduce_sum.38, f32[256]{0:T(256)S(1)} %convert_element_type.267, s32[256]{0:T(256)S(1)} %copy-done.5), kind=kOutput, calls=%fused_computation.3 | convolution fusion | flops 269484032 | bytes 2102272 | tf_op jit(solution)/shard_map/dot_general | solution.py:24
  33.3 0.0 copy-done.2
  33.3 4.3 %all-to-all-start.1 = ((bf16[4,64,1024]{2,1,0:T(8,128)(2,1)}), bf16[4,64,1024]{2,1,0:T(8,128)(2,1)S(1)}, u32[]{:S(2)}, u32[]{:S(2)}) async-start(bf16[4,64,1024]{2,1,0:T(8,128)(2,1)} %bitcast.72), calls=%async_computation.1 | async-start | bytes 1048576 | tf_op jit(solution)/shard_map/all_to_all | solution.py:63
  37.6 1.6 convolution_convert_fusion
  39.2 0.2 pad.9
  39.4 1.3 copy.13
  40.8 4.0 %all-to-all-done.1 = bf16[4,64,1024]{2,1,0:T(8,128)(2,1)S(1)} async-done(((bf16[4,64,1024]{2,1,0:T(8,128)(2,1)}), bf16[4,64,1024]{2,1,0:T(8,128)(2,1)S(1)}, u32[]{:S(2)}, u32[]{:S(2)}) %all-to-all-start.1) | async-done | bytes 524320 | tf_op jit(solution)/shard_map/all_to_all | solution.py:63
  44.8 0.0 copy-start.1
  44.8 13.5 %all-to-all-start.3 = ((bf16[8,96,1024]{2,1,0:T(8,128)(2,1)}), bf16[8,96,1024]{2,1,0:T(8,128)(2,1)}, u32[]{:S(2)}, u32[]{:S(2)}) async-start(bf16[8,96,1024]{2,1,0:T(8,128)(2,1)} %bitcast.68), calls=%async_computation.3 | async-start | bytes 3145728 | tf_op jit(solution)/shard_map/all_to_all | solution.py:37
  58.3 0.2 multiply_reduce_fusion
  58.5 0.1 multiply_convert_fusion.1
  58.7 21.7 %all_gather.15 = bf16[256,1024]{1,0:T(8,128)(2,1)S(1)} all-gather(bf16[64,1024]{1,0:T(8,128)(2,1)S(1)} %multiply_convert_fusion.1), channel_id=1, replica_groups=mesh['yh'=4,'yl'=2,'xh'=2,'zh'=6,'zl'=2,'xl'=2,'core'=2] {'xl','core'}, dimensions={0}, use_global_device_ids=true | all-gather | bytes 655360 | tf_op jit(solution)/shard_map/all_gather | solution.py:73
  80.3 0.0 copy-done.1
  80.3 0.8 convert_bitcast_fusion
  81.1 0.2 pad.8
  81.3 1.7 %copy.12 = bf16[2,2,2,3,6,8,1024]{6,5,4,3,2,1,0:T(8,128)(2,1)} copy(bf16[2,2,2,3,6,8,1024]{6,5,2,4,1,0,3:T(8,128)(2,1)S(1)} %bitcast.67) | data formatting | bytes 4718592 | tf_op jit(solution)/shard_map/transpose | solution.py:36
  83.0 0.0 all-to-all-done.3
  83.0 6.6 %all-to-all-start.2 = ((bf16[8,144,1024]{2,1,0:T(8,128)(2,1)}), bf16[8,144,1024]{2,1,0:T(8,128)(2,1)}, u32[]{:S(2)}, u32[]{:S(2)}) async-start(bf16[8,144,1024]{2,1,0:T(8,128)(2,1)} %bitcast.66), calls=%async_computation.2 | async-start | bytes 4718592 | tf_op jit(solution)/shard_map/all_to_all | solution.py:37
  89.6 1.7 %add_convert_fusion.1 = bf16[1,96,1024]{2,1,0:T(8,128)(2,1)S(1)} fusion(bf16[8,96,1024]{2,1,0:T(8,128)(2,1)} %all-to-all-done.3), kind=kLoop, calls=%fused_computation.10 | loop fusion | flops 1572864 | bytes 1769472 | tf_op jit(solution)/shard_map/convert_element_type | solution.py:37
  91.3 31.3 %all-to-all-done.2 = bf16[8,144,1024]{2,1,0:T(8,128)(2,1)} async-done(((bf16[8,144,1024]{2,1,0:T(8,128)(2,1)}), bf16[8,144,1024]{2,1,0:T(8,128)(2,1)}, u32[]{:S(2)}, u32[]{:S(2)}) %all-to-all-start.2) | async-done | bytes 2359328 | tf_op jit(solution)/shard_map/all_to_all | solution.py:37
  122.7 2.0 %add_convert_fusion = bf16[1,144,1024]{2,1,0:T(8,128)(2,1)S(1)} fusion(bf16[8,144,1024]{2,1,0:T(8,128)(2,1)} %all-to-all-done.2), kind=kLoop, calls=%fused_computation.7 | loop fusion | flops 2359296 | bytes 2654208 | tf_op jit(solution)/shard_map/convert_element_type | solution.py:37
  124.7 0.1 fusion.3
  124.8 0.8 pad_maximum_fusion
  125.6 3.5 %all-to-all-start.4 = ((bf16[4,6,8,1024]{3,2,1,0:T(8,128)(2,1)}), bf16[4,6,8,1024]{3,2,1,0:T(8,128)(2,1)S(1)}, u32[]{:S(2)}, u32[]{:S(2)}) async-start(bf16[4,6,8,1024]{3,2,1,0:T(8,128)(2,1)} %pad_maximum_fusion), calls=%async_computation.4 | async-start | bytes 786432 | tf_op jit(solution)/shard_map/all_to_all | solution.py:84
  129.1 13.2 %all-to-all-done.4 = bf16[4,6,8,1024]{3,2,1,0:T(8,128)(2,1)S(1)} async-done(((bf16[4,6,8,1024]{3,2,1,0:T(8,128)(2,1)}), bf16[4,6,8,1024]{3,2,1,0:T(8,128)(2,1)S(1)}, u32[]{:S(2)}, u32[]{:S(2)}) %all-to-all-start.4) | async-done | bytes 393248 | tf_op jit(solution)/shard_map/all_to_all | solution.py:84
  142.3 0.7 fusion.2
  143.0 9.7 %all-to-all-start.5 = ((bf16[6,8,1024]{2,1,0:T(8,128)(2,1)}), bf16[6,8,1024]{2,1,0:T(8,128)(2,1)S(1)}, u32[]{:S(2)}, u32[]{:S(2)}) async-start(bf16[6,8,1024]{2,1,0:T(8,128)(2,1)} %fusion.2), calls=%async_computation.5 | async-start | bytes 196608 | tf_op jit(solution)/shard_map/all_to_all | solution.py:85
  152.7 1.5 fusion
  154.3 9.4 %all-to-all-done.5 = bf16[6,8,1024]{2,1,0:T(8,128)(2,1)S(1)} async-done(((bf16[6,8,1024]{2,1,0:T(8,128)(2,1)}), bf16[6,8,1024]{2,1,0:T(8,128)(2,1)S(1)}, u32[]{:S(2)}, u32[]{:S(2)}) %all-to-all-start.5) | async-done | bytes 98336 | tf_op jit(solution)/shard_map/all_to_all | solution.py:85
  163.7 0.6 maximum_select_fusion
  (12 shorter events, 0.1 us)
Async XLA Ops:
  0.6 1.6 copy-start
  0.6 8.4 %copy-start.4 = (s32[256]{0:T(256)S(1)}, s32[256]{0:T(256)}, u32[]{:S(2)}) copy-start(s32[256]{0:T(256)} %param.11) | copy-start | bytes 3076
  0.7 15.8 %copy-start.3 = (f32[1024]{0:T(1024)S(1)}, f32[1024]{0:T(1024)}, u32[]{:S(2)}) copy-start(f32[1024]{0:T(1024)} %param.8) | copy-start | bytes 12292
  4.8 11.5 %all-to-all-start = ((bf16[4,64,1024]{2,1,0:T(8,128)(2,1)}), bf16[4,64,1024]{2,1,0:T(8,128)(2,1)S(1)}, u32[]{:S(2)}, u32[]{:S(2)}) async-start(bf16[4,64,1024]{2,1,0:T(8,128)(2,1)} %bitcast), calls=%async_computation | async-start | bytes 1048576 | tf_op jit(solution)/shard_map/all_to_all | solution.py:49
  9.0 21.7 %copy-start.5 = (s32[256]{0:T(256)S(1)}, s32[256]{0:T(256)}, u32[]{:S(2)}) copy-start(s32[256]{0:T(256)} %param.10) | copy-start | bytes 3076
  25.6 7.6 %copy-start.2 = (f32[256,512]{1,0:T(8,128)}, f32[256,512]{1,0:T(8,128)S(1)}, u32[]{:S(2)}) copy-start(f32[256,512]{1,0:T(8,128)S(1)} %get-tuple-element.7) | copy-start | bytes 1572868
  33.3 11.5 %all-to-all-start.1 = ((bf16[4,64,1024]{2,1,0:T(8,128)(2,1)}), bf16[4,64,1024]{2,1,0:T(8,128)(2,1)S(1)}, u32[]{:S(2)}, u32[]{:S(2)}) async-start(bf16[4,64,1024]{2,1,0:T(8,128)(2,1)} %bitcast.72), calls=%async_computation.1 | async-start | bytes 1048576 | tf_op jit(solution)/shard_map/all_to_all | solution.py:63
  44.8 35.5 %copy-start.1 = (bf16[256,1024]{1,0:T(8,128)(2,1)S(1)}, bf16[256,1024]{1,0:T(8,128)(2,1)}, u32[]{:S(2)}) copy-start(bf16[256,1024]{1,0:T(8,128)(2,1)} %param.6) | copy-start | bytes 1572868
  44.8 38.2 %all-to-all-start.3 = ((bf16[8,96,1024]{2,1,0:T(8,128)(2,1)}), bf16[8,96,1024]{2,1,0:T(8,128)(2,1)}, u32[]{:S(2)}, u32[]{:S(2)}) async-start(bf16[8,96,1024]{2,1,0:T(8,128)(2,1)} %bitcast.68), calls=%async_computation.3 | async-start | bytes 3145728 | tf_op jit(solution)/shard_map/all_to_all | solution.py:37
  83.0 39.7 %all-to-all-start.2 = ((bf16[8,144,1024]{2,1,0:T(8,128)(2,1)}), bf16[8,144,1024]{2,1,0:T(8,128)(2,1)}, u32[]{:S(2)}, u32[]{:S(2)}) async-start(bf16[8,144,1024]{2,1,0:T(8,128)(2,1)} %bitcast.66), calls=%async_computation.2 | async-start | bytes 4718592 | tf_op jit(solution)/shard_map/all_to_all | solution.py:37
  125.6 16.7 %all-to-all-start.4 = ((bf16[4,6,8,1024]{3,2,1,0:T(8,128)(2,1)}), bf16[4,6,8,1024]{3,2,1,0:T(8,128)(2,1)S(1)}, u32[]{:S(2)}, u32[]{:S(2)}) async-start(bf16[4,6,8,1024]{3,2,1,0:T(8,128)(2,1)} %pad_maximum_fusion), calls=%async_computation.4 | async-start | bytes 786432 | tf_op jit(solution)/shard_map/all_to_all | solution.py:84
  143.0 20.7 %all-to-all-start.5 = ((bf16[6,8,1024]{2,1,0:T(8,128)(2,1)}), bf16[6,8,1024]{2,1,0:T(8,128)(2,1)S(1)}, u32[]{:S(2)}, u32[]{:S(2)}) async-start(bf16[6,8,1024]{2,1,0:T(8,128)(2,1)} %fusion.2), calls=%async_computation.5 | async-start | bytes 196608 | tf_op jit(solution)/shard_map/all_to_all | solution.py:85

commit v3 on v2

v3 whole, which is shorter than its diff:
```python
import jax
import jax.numpy as jnp
from jax import lax
from jax.sharding import Mesh
from jax.sharding import PartitionSpec as P

norm_eps = 1e-05
loss_scale = 16.0

AXES = ("yh", "yl", "xh", "zh", "zl", "xl", "core")
SIZES = (4, 2, 2, 6, 2, 2, 2)
SEQ = ("yh", "yl", "xh", "zh", "zl")
TP = ("xl", "core")
BLOCKS = 192
PROJ_BLOCKS = 128
HALF = 96
SWAP = [(0, 1), (1, 0)]
f32 = jnp.float32
bf16 = jnp.bfloat16


def dot(a, b, ca, cb):
    return lax.dot_general(a, b, (((ca,), (cb,)), ((), ())), preferred_element_type=f32)


def add_up(pieces):
    total = pieces[0].astype(f32)
    for i in range(1, pieces.shape[0]):
        total = total + pieces[i].astype(f32)
    return total


def tp_sum(partial):
    rows, width = partial.shape
    chip = add_up(lax.all_to_all(partial.reshape(2, rows // 2, width), "core", 0, 0)).astype(bf16)
    return add_up(lax.all_gather(chip, "xl"))


def halve(blocks, axis_name, axis):
    me = lax.axis_index(axis_name)
    sent = lax.dynamic_index_in_dim(blocks, 1 - me, axis, keepdims=False)
    kept = lax.dynamic_index_in_dim(blocks, me, axis, keepdims=False)
    return (kept.astype(f32) + lax.ppermute(sent, axis_name, SWAP).astype(f32)).astype(bf16)


def local(hidden, in_proj, norm_gain, head_weight, code_ids, stream_mask):
    frames, width = hidden.shape[0], in_proj.shape[1]
    vocab_part = head_weight.shape[1]
    tp = lax.axis_index(TP)
    gain = norm_gain[None, :]

    x = tp_sum(dot(hidden, in_proj, 1, 0).astype(bf16))
    inv_rms = lax.rsqrt(jnp.mean(x * x, axis=1, keepdims=True) + norm_eps)
    unit_rows = x * inv_rms
    normed = lax.all_gather((unit_rows * gain).astype(bf16), "core", tiled=True)

    exp_logits = jnp.exp(dot(normed, head_weight, 1, 0))
    totals = lax.all_gather(jnp.sum(exp_logits, axis=1), TP)
    exp_total = jnp.sum(totals, axis=0)[:, None]
    columns = lax.broadcasted_iota(jnp.int32, (frames, vocab_part), 1) + tp * vocab_part
    onehot = (columns == code_ids[:, None]).astype(f32)
    weighting = stream_mask.astype(f32)[:, None]
    dlogit = (weighting * (exp_logits / exp_total - onehot)).astype(bf16)

    scaled_grad = tp_sum(dot(dlogit, head_weight, 1, 1).astype(bf16)) * gain
    head_grad = dot(normed, dlogit, 0, 0).astype(bf16)
    head_blocks = head_grad.reshape(BLOCKS - PROJ_BLOCKS, 2, 8, vocab_part)
    head_blocks = jnp.transpose(head_blocks, (0, 2, 1, 3)).reshape(BLOCKS - PROJ_BLOCKS, 8, width)

    centred = scaled_grad - unit_rows * jnp.mean(scaled_grad * unit_rows, axis=1, keepdims=True)
    row_grad = lax.all_gather((inv_rms * centred).astype(bf16), "core", tiled=True)

    split = HALF * 8
    late = dot(hidden[:, split:], row_grad, 0, 0).astype(bf16).reshape(PROJ_BLOCKS - HALF, 8, width)
    early = dot(hidden[:, :split], row_grad, 0, 0).astype(bf16)
    shape = (2, 2, 2, 6, 2, 8, width)
    late = jnp.concatenate([late, head_blocks], axis=0).reshape(shape)
    early = early.reshape(shape)
    late = halve(late, "yl", 1)
    early = halve(early, "zl", 4)
    late = halve(late, "zl", 3)
    early = halve(early, "yl", 1)
    near = jnp.concatenate([early, late], axis=0).reshape(8, 6 * 8, width)
    mid = add_up(lax.all_to_all(near, ("yh", "xh"), 0, 0)).astype(bf16).reshape(6, 8, width)
    summed = add_up(lax.all_to_all(mid, "zh", 0, 0))
    as_proj = summed.reshape(16, vocab_part)
    as_head = jnp.concatenate([summed[:, :vocab_part], summed[:, vocab_part:]], axis=0)
    weight_grads = jnp.where(lax.axis_index(SEQ) < PROJ_BLOCKS, as_proj, as_head)

    hidden_grad = (loss_scale * dot(row_grad, in_proj, 1, 1)).astype(bf16)
    return (hidden_grad, weight_grads[None])


def solution(mesh):
    fine = Mesh(mesh.devices.reshape(SIZES), AXES)
    in_specs = (P(SEQ, TP), P(TP, None), P(), P(None, TP), P(SEQ), P(SEQ))
    out_specs = (P(SEQ, TP), P(TP, SEQ, None))
    return jax.shard_map(local, mesh=fine, in_specs=in_specs, out_specs=out_specs, check_vma=False)
```

time: 165 us -> 157 us (0.952)
  the two profiles are of different devices: /device:TPU:70 before, /device:TPU:16 now
where the time goes in v3:
time: 157 us; the launch traced here: 156 us
  waiting for transfers between devices  53.1 us (34%)
  starting transfers between devices  46.5 us (30%)
  blocking collectives  27.8 us (18%)
  matrix products  14.1 us (9%)
  other arithmetic  9.22 us (6%)
  local copies, waits for them, and re-layouts  4.92 us (3%)
    all_to_all x1, waiting for transfers between devices, local(): lax.all_to_all(near, ('yh', 'xh'), 0, 0)  21.7 us
    ppermute x4, waiting for transfers between devices, halve(): lax.ppermute(sent, axis_name, SWAP).astype(f32)  20.6 us
    all_gather x2, blocking collectives, tp_sum(): return add_up(lax.all_gather(chip, 'xl'))  18.4 us
    ppermute x4, starting transfers between devices, halve(): lax.ppermute(sent, axis_name, SWAP).astype(f32)  15.5 us
    dot_general x7, matrix products, dot(): lax.dot_general(a, b, (((ca,), (cb,)), ((), ())), preferred_element_type=...  14.1 us
    all_to_all x1, starting transfers between devices, local(): summed = add_up(lax.all_to_all(mid, 'zh', 0, 0))  13.1 us
    all_to_all x1, starting transfers between devices, local(): lax.all_to_all(near, ('yh', 'xh'), 0, 0)  10.7 us
    all_to_all x1, waiting for transfers between devices, local(): summed = add_up(lax.all_to_all(mid, 'zh', 0, 0))  9.07 us
  transfers between devices with their start and end apart: 8, of which 6 were waited for; matrix products, arithmetic and copies ran while one was open for 6% of the time, Pallas kernels for 0%

profile of v3, /device:TPU:16, one launch (start us, length us, event | category | flops | bytes accessed | tf_op | source)
XLA Modules:
  0.0 156.5 jit_solution(3493224593762520505)
XLA Ops:
  0.6 0.0 copy-start
  0.6 1.6 %copy-done = bf16[1024,1024]{1,0:T(8,128)(2,1)S(1)} copy-done((bf16[1024,1024]{1,0:T(8,128)(2,1)S(1)}, bf16[1024,1024]{1,0:T(8,128)(2,1)}, u32[]{:S(2)}) %copy-start) | copy-done | bytes 2097176
  2.2 2.5 %convolution_convert_fusion.4 = bf16[256,1024]{1,0:T(8,128)(2,1)} fusion(bf16[256,1024]{1,0:T(8,128)(2,1)} %param.6, bf16[1024,1024]{1,0:T(8,128)(2,1)S(1)} %copy-done), kind=kOutput, calls=%fused_computation.10 | convolution fusion | flops 537133056 | bytes 3145728 | tf_op jit(solution)/shard_map/dot_general | solution.py:23
  4.8 0.0 copy-start.3
  4.8 3.6 %all-to-all-start = ((bf16[2,128,1024]{2,1,0:T(8,128)(2,1)}), bf16[2,128,1024]{2,1,0:T(8,128)(2,1)S(1)}, u32[]{:S(2)}, u32[]{:S(2)}) async-start(bf16[2,128,1024]{2,1,0:T(8,128)(2,1)} %bitcast), calls=%async_computation | async-start | bytes 1048576 | tf_op jit(solution)/shard_map/all_to_all | solution.py:35
  8.4 1.7 %all-to-all-done = bf16[2,128,1024]{2,1,0:T(8,128)(2,1)S(1)} async-done(((bf16[2,128,1024]{2,1,0:T(8,128)(2,1)}), bf16[2,128,1024]{2,1,0:T(8,128)(2,1)S(1)}, u32[]{:S(2)}, u32[]{:S(2)}) %all-to-all-start) | async-done | bytes 524320 | tf_op jit(solution)/shard_map/all_to_all | solution.py:35
  10.1 0.1 add_convert_fusion.1
  10.2 9.0 %all_gather.20 = bf16[2,128,1024]{2,1,0:T(8,128)(2,1)S(1)} all-gather(bf16[1,128,1024]{2,1,0:T(8,128)(2,1)S(1)} %add_convert_fusion.1), channel_id=1, replica_groups=mesh['yh'=4,'yl'=2,'xh'=2,'zh'=6,'zl'=2,'xl'=2,'core'=2] {'xl'}, dimensions={0}, use_global_device_ids=true | all-gather | bytes 786432 | tf_op jit(solution)/shard_map/all_gather | solution.py:36
  19.2 0.2 fusion.6
  19.4 0.0 copy-done.3
  19.4 0.1 multiply_convert_fusion.2
  19.5 0.0 copy-start.4
  19.5 0.0 copy-start.5
  19.6 2.2 %all_gather.21 = bf16[256,1024]{1,0:T(8,128)(2,1)S(1)} all-gather(bf16[128,1024]{1,0:T(8,128)(2,1)S(1)} %multiply_convert_fusion.2), channel_id=1, replica_groups=mesh['yh'=4,'yl'=2,'xh'=2,'zh'=6,'zl'=2,'xl'=2,'core'=2] {'core'}, dimensions={0}, use_global_device_ids=true | all-gather | bytes 786432 | tf_op jit(solution)/shard_map/all_gather | solution.py:55
  21.7 0.0 copy-start.1
  21.7 2.7 %fusion.10 = (f32[256]{0:T(256)S(1)}, f32[256,512]{1,0:T(8,128)}) fusion(bf16[256,1024]{1,0:T(8,128)(2,1)S(1)} %all_gather.21, bf16[1024,512]{1,0:T(8,128)(2,1)} %param.9), kind=kOutput, calls=%fused_computation.48 | convolution fusion | flops 268566272 | bytes 2098176 | tf_op jit(solution)/shard_map/dot_general | solution.py:23
  24.4 5.1 %all-gather.1 = f32[4,1,256]{2,1,0:T(1,128)S(1)} all-gather(f32[1,1,256]{2,1,0:T(1,128)S(1)} %bitcast.81), channel_id=2, replica_groups=mesh['yh'=4,'yl'=2,'xh'=2,'zh'=6,'zl'=2,'xl'=2,'core'=2] {'xl','core'}, dimensions={0}, use_global_device_ids=true | all-gather | bytes 5120 | tf_op jit(solution)/shard_map/all_gather | solution.py:58
  29.5 0.0 copy-done.4
  29.5 0.0 copy-done.5
  29.5 2.7 %convolution_convert_fusion.3 = bf16[256,1024]{1,0:T(8,128)(2,1)} fusion(bf16[1024,512]{1,0:T(8,128)(2,1)} %param.9, f32[256,512]{1,0:T(8,128)} %get-tuple-element.7, s32[512]{0:T(512)S(1)} %iota_add_fusion, f32[256]{0:T(256)S(1)} %reduce_sum.38, f32[256]{0:T(256)S(1)} %convert_element_type.275, s32[256]{0:T(256)S(1)} %copy-done.5), kind=kOutput, calls=%fused_computation.9 | convolution fusion | flops 269484032 | bytes 2102272 | tf_op jit(solution)/shard_map/dot_general | solution.py:23
  32.2 0.0 copy-done.1
  32.2 3.5 %all-to-all-start.1 = ((bf16[2,128,1024]{2,1,0:T(8,128)(2,1)}), bf16[2,128,1024]{2,1,0:T(8,128)(2,1)S(1)}, u32[]{:S(2)}, u32[]{:S(2)}) async-start(bf16[2,128,1024]{2,1,0:T(8,128)(2,1)} %bitcast.80), calls=%async_computation.1 | async-start | bytes 1048576 | tf_op jit(solution)/shard_map/all_to_all | solution.py:35
  35.7 2.8 %convolution_convert_fusion.1 = bf16[1024,512]{1,0:T(8,128)(2,1)} fusion(bf16[256,1024]{1,0:T(8,128)(2,1)} %copy-done.1, f32[256,512]{1,0:T(8,128)} %get-tuple-element.7, s32[512]{0:T(512)S(1)} %iota_add_fusion, f32[256]{0:T(256)S(1)} %reduce_sum.38, f32[256]{0:T(256)S(1)} %convert_element_type.275, s32[256]{0:T(256)S(1)} %copy-done.5), kind=kOutput, calls=%fused_computation.6 | convolution fusion | flops 269746176 | bytes 2102272 | tf_op jit(solution)/shard_map/dot_general | solution.py:23
  38.5 0.0 all-to-all-done.1
  38.5 0.1 add_convert_fusion
  38.5 9.4 %all_gather.24 = bf16[2,128,1024]{2,1,0:T(8,128)(2,1)S(1)} all-gather(bf16[1,128,1024]{2,1,0:T(8,128)(2,1)S(1)} %add_convert_fusion), channel_id=1, replica_groups=mesh['yh'=4,'yl'=2,'xh'=2,'zh'=6,'zl'=2,'xl'=2,'core'=2] {'xl'}, dimensions={0}, use_global_device_ids=true | all-gather | bytes 786432 | tf_op jit(solution)/shard_map/all_gather | solution.py:36
  47.9 0.3 multiply_reduce_fusion
  48.2 0.2 multiply_convert_fusion
  48.4 2.2 %all_gather.25 = bf16[256,1024]{1,0:T(8,128)(2,1)S(1)} all-gather(bf16[128,1024]{1,0:T(8,128)(2,1)S(1)} %multiply_convert_fusion), channel_id=1, replica_groups=mesh['yh'=4,'yl'=2,'xh'=2,'zh'=6,'zl'=2,'xl'=2,'core'=2] {'core'}, dimensions={0}, use_global_device_ids=true | all-gather | bytes 786432 | tf_op jit(solution)/shard_map/all_gather | solution.py:71
  50.6 1.2 fusion.3
  51.9 2.5 %pad_maximum_fusion = bf16[96,8,1024]{2,1,0:T(8,128)(2,1)} fusion(bf16[64,8,1024]{2,1,0:T(8,128)(2,1)} %bitcast.79, bf16[32,8,1024]{2,1,0:T(8,128)(2,1)S(1)} %fusion.3), kind=kLoop, calls=%fused_computation.1 | loop fusion | flops 786432 | bytes 3145728 | tf_op jit(solution)/shard_map/concatenate | solution.py:77
  54.4 0.0 copy-start.2
  54.4 2.2 %dynamic-slice_bitcast_fusion = bf16[2,2,6,2,8,1024]{5,4,3,2,1,0:T(8,128)(2,1)} fusion(bf16[2,2,2,6,2,8,1024]{6,5,4,3,2,1,0:T(8,128)(2,1)} %bitcast.75, s32[]{:T(128)S(6)} %select_n.39), kind=kLoop, calls=%fused_computation.21 | loop fusion | bytes 1572868 | tf_op jit(solution)/shard_map/jit(dynamic_index_in_dim)/squeeze | solution.py:41
  56.5 3.5 %collective-permute-start.2 = (bf16[2,2,6,2,8,1024]{5,4,3,2,1,0:T(8,128)(2,1)}, bf16[2,2,6,2,8,1024]{5,4,3,2,1,0:T(8,128)(2,1)}, u32[]{:S(2)}, u32[]{:S(2)}) collective-permute-start(bf16[2,2,6,2,8,1024]{5,4,3,2,1,0:T(8,128)(2,1)} %dynamic-slice_bitcast_fusion), channel_id=1, source_target_pairs={{0,96},{96,0},{1,97},{97,1},{2,98},{98,2},{3,99},{99,3},{4,100},{1... | collective-permute-start | bytes 2359304 | tf_op jit(solution)/shard_map/ppermute | solution.py:43
  60.0 0.0 copy-done.2
  60.0 0.6 convolution_convert_fusion
  60.7 0.1 constant_dynamic-slice_fusion.1
  60.8 0.9 copy.17
  61.7 4.3 %collective-permute-start = (bf16[2,2,2,6,8,1024]{5,4,3,2,0,1:T(8,128)(2,1)}, bf16[2,2,2,6,8,1024]{5,4,3,2,0,1:T(8,128)(2,1)}, u32[]{:S(2)}, u32[]{:S(2)}) collective-permute-start(bf16[2,2,2,6,8,1024]{5,4,3,2,0,1:T(8,128)(2,1)} %bitcast.74), channel_id=1, source_target_pairs={{0,4},{4,0},{1,5},{5,1},{2,6},{6,2},{3,7},{7,3},{8,12},{12,8},{9,1... | collective-permute-start | bytes 2359304 | tf_op jit(solution)/shard_map/ppermute | solution.py:43
  66.0 12.3 %collective-permute-done.2 = bf16[2,2,6,2,8,1024]{5,4,3,2,1,0:T(8,128)(2,1)} collective-permute-done((bf16[2,2,6,2,8,1024]{5,4,3,2,1,0:T(8,128)(2,1)}, bf16[2,2,6,2,8,1024]{5,4,3,2,1,0:T(8,128)(2,1)}, u32[]{:S(2)}, u32[]{:S(2)}) %collective-permute-start.2) | collective-permute-done | bytes 786464 | tf_op jit(solution)/shard_map/ppermute | solution.py:43
  78.3 1.7 %fusion = bf16[2,2,6,2,8,1024]{5,4,3,2,1,0:T(8,128)(2,1)S(1)} fusion(bf16[2,2,6,2,8,1024]{5,4,3,2,1,0:T(8,128)(2,1)} %collective-permute-done.2, bf16[2,2,2,6,2,8,1024]{6,5,4,3,2,1,0:T(8,128)(2,1)} %bitcast.76, s32[]{:T(128)S(6)} %select_n.38), kind=kLoop, calls=%fused_computation.3 | loop fusion | flops 1572864 | bytes 2359300 | tf_op jit(solution)/shard_map/convert_element_type | solution.py:43
  80.0 4.3 %collective-permute-start.3 = (bf16[2,2,6,8,1024]{4,3,2,1,0:T(8,128)(2,1)S(1)}, bf16[2,2,6,8,1024]{4,3,2,1,0:T(8,128)(2,1)S(1)}, u32[]{:S(2)}, u32[]{:S(2)}) collective-permute-start(bf16[2,2,6,8,1024]{4,3,2,1,0:T(8,128)(2,1)S(1)} %dynamic-slice_bitcast_fusion.1), channel_id=1, source_target_pairs={{0,4},{4,0},{1,5},{5,1},{2,6},{6,2},{3,7},{7,3},{8,12},{12,8},{9,1... | collective-permute-start | bytes 1179656 | tf_op jit(solution)/shard_map/ppermute | solution.py:43
  84.3 0.0 collective-permute-done
  84.3 1.4 fusion.1
  85.8 3.5 %collective-permute-start.1 = (bf16[2,2,6,8,1024]{4,3,2,1,0:T(8,128)(2,1)S(1)}, bf16[2,2,6,8,1024]{4,3,2,1,0:T(8,128)(2,1)S(1)}, u32[]{:S(2)}, u32[]{:S(2)}) collective-permute-start(bf16[2,2,6,8,1024]{4,3,2,1,0:T(8,128)(2,1)S(1)} %dynamic-slice_bitcast_fusion.2), channel_id=1, source_target_pairs={{0,96},{96,0},{1,97},{97,1},{2,98},{98,2},{3,99},{99,3},{4,100},{1... | collective-permute-start | bytes 1179656 | tf_op jit(solution)/shard_map/ppermute | solution.py:43
  89.3 3.6 %collective-permute-done.3 = bf16[2,2,6,8,1024]{4,3,2,1,0:T(8,128)(2,1)S(1)} collective-permute-done((bf16[2,2,6,8,1024]{4,3,2,1,0:T(8,128)(2,1)S(1)}, bf16[2,2,6,8,1024]{4,3,2,1,0:T(8,128)(2,1)S(1)}, u32[]{:S(2)}, u32[]{:S(2)}) %collective-permute-start.3) | collective-permute-done | bytes 393248 | tf_op jit(solution)/shard_map/ppermute | solution.py:43
  92.9 0.1 fusion.4
  93.1 4.7 %collective-permute-done.1 = bf16[2,2,6,8,1024]{4,3,2,1,0:T(8,128)(2,1)S(1)} collective-permute-done((bf16[2,2,6,8,1024]{4,3,2,1,0:T(8,128)(2,1)S(1)}, bf16[2,2,6,8,1024]{4,3,2,1,0:T(8,128)(2,1)S(1)}, u32[]{:S(2)}, u32[]{:S(2)}) %collective-permute-start.1) | collective-permute-done | bytes 393248 | tf_op jit(solution)/shard_map/ppermute | solution.py:43
  97.8 0.1 fusion.5
  97.9 1.0 pad_maximum_fusion.1
  98.9 10.7 %all-to-all-start.2 = ((bf16[8,48,1024]{2,1,0:T(8,128)(2,1)}), bf16[8,48,1024]{2,1,0:T(8,128)(2,1)S(1)}, u32[]{:S(2)}, u32[]{:S(2)}) async-start(bf16[8,48,1024]{2,1,0:T(8,128)(2,1)} %bitcast.78), calls=%async_computation.2 | async-start | bytes 1572864 | tf_op jit(solution)/shard_map/all_to_all | solution.py:84
  109.6 21.7 %all-to-all-done.2 = bf16[8,48,1024]{2,1,0:T(8,128)(2,1)S(1)} async-done(((bf16[8,48,1024]{2,1,0:T(8,128)(2,1)}), bf16[8,48,1024]{2,1,0:T(8,128)(2,1)S(1)}, u32[]{:S(2)}, u32[]{:S(2)}) %all-to-all-start.2) | async-done | bytes 786464 | tf_op jit(solution)/shard_map/all_to_all | solution.py:84
  131.3 0.8 fusion.9
  132.0 13.1 %all-to-all-start.3 = ((bf16[6,8,1024]{2,1,0:T(8,128)(2,1)}), bf16[6,8,1024]{2,1,0:T(8,128)(2,1)S(1)}, u32[]{:S(2)}, u32[]{:S(2)}) async-start(bf16[6,8,1024]{2,1,0:T(8,128)(2,1)} %fusion.9), calls=%async_computation.3 | async-start | bytes 196608 | tf_op jit(solution)/shard_map/all_to_all | solution.py:85
  145.2 1.5 fusion.2
  146.7 9.1 %all-to-all-done.3 = bf16[6,8,1024]{2,1,0:T(8,128)(2,1)S(1)} async-done(((bf16[6,8,1024]{2,1,0:T(8,128)(2,1)}), bf16[6,8,1024]{2,1,0:T(8,128)(2,1)S(1)}, u32[]{:S(2)}, u32[]{:S(2)}) %all-to-all-start.3) | async-done | bytes 98336 | tf_op jit(solution)/shard_map/all_to_all | solution.py:85
  155.8 0.6 maximum_select_fusion
  (11 shorter events, 0.2 us)
Async XLA Ops:
  0.6 1.6 %copy-start = (bf16[1024,1024]{1,0:T(8,128)(2,1)S(1)}, bf16[1024,1024]{1,0:T(8,128)(2,1)}, u32[]{:S(2)}) copy-start(bf16[1024,1024]{1,0:T(8,128)(2,1)} %param.7) | copy-start | bytes 6291460
  4.8 14.6 %copy-start.3 = (f32[1024]{0:T(1024)S(1)}, f32[1024]{0:T(1024)}, u32[]{:S(2)}) copy-start(f32[1024]{0:T(1024)} %param.8) | copy-start | bytes 12292
  4.8 5.4 %all-to-all-start = ((bf16[2,128,1024]{2,1,0:T(8,128)(2,1)}), bf16[2,128,1024]{2,1,0:T(8,128)(2,1)S(1)}, u32[]{:S(2)}, u32[]{:S(2)}) async-start(bf16[2,128,1024]{2,1,0:T(8,128)(2,1)} %bitcast), calls=%async_computation | async-start | bytes 1048576 | tf_op jit(solution)/shard_map/all_to_all | solution.py:35
  19.5 9.9 %copy-start.4 = (s32[256]{0:T(256)S(1)}, s32[256]{0:T(256)}, u32[]{:S(2)}) copy-start(s32[256]{0:T(256)} %param.11) | copy-start | bytes 3076
  19.5 9.9 %copy-start.5 = (s32[256]{0:T(256)S(1)}, s32[256]{0:T(256)}, u32[]{:S(2)}) copy-start(s32[256]{0:T(256)} %param.10) | copy-start | bytes 3076
  21.7 10.5 %copy-start.1 = (bf16[256,1024]{1,0:T(8,128)(2,1)}, bf16[256,1024]{1,0:T(8,128)(2,1)S(1)}, u32[]{:S(2)}) copy-start(bf16[256,1024]{1,0:T(8,128)(2,1)S(1)} %all_gather.21) | copy-start | bytes 1572868
  32.2 6.3 %all-to-all-start.1 = ((bf16[2,128,1024]{2,1,0:T(8,128)(2,1)}), bf16[2,128,1024]{2,1,0:T(8,128)(2,1)S(1)}, u32[]{:S(2)}, u32[]{:S(2)}) async-start(bf16[2,128,1024]{2,1,0:T(8,128)(2,1)} %bitcast.80), calls=%async_computation.1 | async-start | bytes 1048576 | tf_op jit(solution)/shard_map/all_to_all | solution.py:35
  54.4 5.7 %copy-start.2 = (bf16[256,1024]{1,0:T(8,128)(2,1)S(1)}, bf16[256,1024]{1,0:T(8,128)(2,1)}, u32[]{:S(2)}) copy-start(bf16[256,1024]{1,0:T(8,128)(2,1)} %param.6) | copy-start | bytes 1572868
  56.5 21.8 %collective-permute-start.2 = (bf16[2,2,6,2,8,1024]{5,4,3,2,1,0:T(8,128)(2,1)}, bf16[2,2,6,2,8,1024]{5,4,3,2,1,0:T(8,128)(2,1)}, u32[]{:S(2)}, u32[]{:S(2)}) collective-permute-start(bf16[2,2,6,2,8,1024]{5,4,3,2,1,0:T(8,128)(2,1)} %dynamic-slice_bitcast_fusion), channel_id=1, source_target_pairs={{0,96},{96,0},{1,97},{97,1},{2,98},{98,2},{3,99},{99,3},{4,100},{1... | collective-permute-start | bytes 2359304 | tf_op jit(solution)/shard_map/ppermute | solution.py:43
  61.7 22.6 %collective-permute-start = (bf16[2,2,2,6,8,1024]{5,4,3,2,0,1:T(8,128)(2,1)}, bf16[2,2,2,6,8,1024]{5,4,3,2,0,1:T(8,128)(2,1)}, u32[]{:S(2)}, u32[]{:S(2)}) collective-permute-start(bf16[2,2,2,6,8,1024]{5,4,3,2,0,1:T(8,128)(2,1)} %bitcast.74), channel_id=1, source_target_pairs={{0,4},{4,0},{1,5},{5,1},{2,6},{6,2},{3,7},{7,3},{8,12},{12,8},{9,1... | collective-permute-start | bytes 2359304 | tf_op jit(solution)/shard_map/ppermute | solution.py:43
  80.0 12.9 %collective-permute-start.3 = (bf16[2,2,6,8,1024]{4,3,2,1,0:T(8,128)(2,1)S(1)}, bf16[2,2,6,8,1024]{4,3,2,1,0:T(8,128)(2,1)S(1)}, u32[]{:S(2)}, u32[]{:S(2)}) collective-permute-start(bf16[2,2,6,8,1024]{4,3,2,1,0:T(8,128)(2,1)S(1)} %dynamic-slice_bitcast_fusion.1), channel_id=1, source_target_pairs={{0,4},{4,0},{1,5},{5,1},{2,6},{6,2},{3,7},{7,3},{8,12},{12,8},{9,1... | collective-permute-start | bytes 1179656 | tf_op jit(solution)/shard_map/ppermute | solution.py:43
  85.8 11.9 %collective-permute-start.1 = (bf16[2,2,6,8,1024]{4,3,2,1,0:T(8,128)(2,1)S(1)}, bf16[2,2,6,8,1024]{4,3,2,1,0:T(8,128)(2,1)S(1)}, u32[]{:S(2)}, u32[]{:S(2)}) collective-permute-start(bf16[2,2,6,8,1024]{4,3,2,1,0:T(8,128)(2,1)S(1)} %dynamic-slice_bitcast_fusion.2), channel_id=1, source_target_pairs={{0,96},{96,0},{1,97},{97,1},{2,98},{98,2},{3,99},{99,3},{4,100},{1... | collective-permute-start | bytes 1179656 | tf_op jit(solution)/shard_map/ppermute | solution.py:43
  98.9 32.4 %all-to-all-start.2 = ((bf16[8,48,1024]{2,1,0:T(8,128)(2,1)}), bf16[8,48,1024]{2,1,0:T(8,128)(2,1)S(1)}, u32[]{:S(2)}, u32[]{:S(2)}) async-start(bf16[8,48,1024]{2,1,0:T(8,128)(2,1)} %bitcast.78), calls=%async_computation.2 | async-start | bytes 1572864 | tf_op jit(solution)/shard_map/all_to_all | solution.py:84
  132.0 23.8 %all-to-all-start.3 = ((bf16[6,8,1024]{2,1,0:T(8,128)(2,1)}), bf16[6,8,1024]{2,1,0:T(8,128)(2,1)S(1)}, u32[]{:S(2)}, u32[]{:S(2)}) async-start(bf16[6,8,1024]{2,1,0:T(8,128)(2,1)} %fusion.9), calls=%async_computation.3 | async-start | bytes 196608 | tf_op jit(solution)/shard_map/all_to_all | solution.py:85

commit v4 on v3

v4 whole, which is shorter than its diff:
```python
import jax
import jax.numpy as jnp
from jax import lax
from jax.experimental import pallas as pl
from jax.experimental.pallas import tpu as pltpu
from jax.sharding import Mesh
from jax.sharding import PartitionSpec as P

norm_eps = 1e-05
loss_scale = 16.0

AXES = ("yh", "yl", "xh", "zh", "zl", "xl", "core")
SIZES = (4, 2, 2, 6, 2, 2, 2)
SEQ = ("yh", "yl", "xh", "zh", "zl")
TP = ("xl", "core")
NEAR = ("yl", "xh", "zl")
FAR = ("yh", "zh")
N_NEAR = 8
N_FAR = 24
BLOCKS = 192
PROJ_BLOCKS = 128
VMEM_BYTES = 20 << 20
SWAP = [(0, 1), (1, 0)]
f32 = jnp.float32
bf16 = jnp.bfloat16


def dot(a, b, ca, cb):
    return lax.dot_general(a, b, (((ca,), (cb,)), ((), ())), preferred_element_type=f32)


def add_up(pieces):
    total = pieces[0].astype(f32)
    for i in range(1, pieces.shape[0]):
        total = total + pieces[i].astype(f32)
    return total


def near_far(block):
    y, x, z = block // 24, block // 12 % 2, block % 12
    return (y % 2 * 2 + x) * 2 + z % 2, y // 2 * 6 + z // 2


def rows_product(half_ref, a_ref, b_ref, out_ref):
    rows = out_ref.shape[0]
    start = pl.multiple_of(half_ref[0] * rows, rows)
    out_ref[...] = dot(a_ref[pl.ds(start, rows), :], b_ref[...], 1, 0).astype(out_ref.dtype)


def exp_rows(normed_ref, head_ref, exp_ref, sum_ref):
    exp_logits = jnp.exp(dot(normed_ref[...], head_ref[...], 1, 0))
    exp_ref[...] = exp_logits
    sum_ref[...] = jnp.sum(exp_logits, axis=1, keepdims=True)


def dlogit_rows(first, exp_ref, totals_ref, code_ref, mask_ref, rows):
    window = pl.ds(first, rows)
    exp_logits = exp_ref[window, :]
    columns = lax.broadcasted_iota(jnp.int32, exp_logits.shape, 1)
    onehot = (columns == code_ref[window, :]).astype(f32)
    return (mask_ref[window, :] * (exp_logits / totals_ref[window, :] - onehot)).astype(bf16)


def sent_grad(half_ref, exp_ref, totals_ref, code_ref, mask_ref, head_ref, out_ref):
    rows = out_ref.shape[0]
    start = pl.multiple_of(half_ref[0] * rows, rows)
    dlogit = dlogit_rows(start, exp_ref, totals_ref, code_ref, mask_ref, rows)
    out_ref[...] = dot(dlogit, head_ref[...], 1, 1).astype(out_ref.dtype)


def kept_grad(half_ref, exp_ref, totals_ref, code_ref, mask_ref, head_ref, normed_ref, out_ref, blocks_ref):
    rows = out_ref.shape[0]
    start = pl.multiple_of(half_ref[0] * rows, rows)
    dlogit = dlogit_rows(start, exp_ref, totals_ref, code_ref, mask_ref, rows)
    out_ref[...] = dot(dlogit, head_ref[...], 1, 1)
    whole = dlogit_rows(0, exp_ref, totals_ref, code_ref, mask_ref, exp_ref.shape[0])
    grad = dot(normed_ref[...], whole, 0, 0).astype(bf16)
    part = grad.shape[1]
    for i in range(blocks_ref.shape[0]):
        blocks_ref[i, :, :part] = grad[16 * i : 16 * i + 8]
        blocks_ref[i, :, part:] = grad[16 * i + 8 : 16 * i + 16]


def grad_blocks(hidden_ref, grad_ref, head_ref, out_ref):
    step = 16
    for first in range(0, PROJ_BLOCKS, step):
        part = dot(hidden_ref[:, 8 * first : 8 * (first + step)], grad_ref[...], 0, 0).astype(bf16)
        for i in range(step):
            near, far = near_far(first + i)
            out_ref[near, 8 * far : 8 * far + 8, :] = part[8 * i : 8 * i + 8]
    for block in range(PROJ_BLOCKS, BLOCKS):
        near, far = near_far(block)
        out_ref[near, 8 * far : 8 * far + 8, :] = head_ref[block - PROJ_BLOCKS]


def near_sum(pieces_ref, out_ref):
    out_ref[...] = add_up(pieces_ref).astype(out_ref.dtype)


def far_sum(is_proj_ref, pieces_ref, out_ref):
    total = add_up(pieces_ref)
    part = out_ref.shape[2]
    left, right = total[:, :part], total[:, part:]

    @pl.when(is_proj_ref[0] == 1)
    def _():
        out_ref[:, 0, :] = left
        out_ref[:, 1, :] = right

    @pl.when(is_proj_ref[0] == 0)
    def _():
        for row in range(4):
            out_ref[row] = left[2 * row : 2 * row + 2]
            out_ref[4 + row] = right[2 * row : 2 * row + 2]


def in_vmem(kernel, outs, n_in, scalars=0):
    vmem = pl.BlockSpec(memory_space=pltpu.VMEM)
    smem = pl.BlockSpec(memory_space=pltpu.SMEM)
    return pl.pallas_call(
        kernel,
        out_shape=outs,
        in_specs=[smem] * scalars + [vmem] * n_in,
        out_specs=jax.tree.map(lambda _: vmem, outs),
        compiler_params=pltpu.CompilerParams(vmem_limit_bytes=VMEM_BYTES),
    )


def shape(dims, dtype):
    return jax.ShapeDtypeStruct(dims, dtype)


def local(hidden, in_proj, norm_gain, head_weight, code_ids, stream_mask):
    frames, width = hidden.shape[0], in_proj.shape[1]
    vocab_part = head_weight.shape[1]
    half = frames // 2
    tp = lax.axis_index(TP)
    gain = norm_gain[None, :]
    mine = lax.axis_index("core").reshape(1)
    other = 1 - mine
    code = (code_ids - tp * vocab_part)[:, None]
    mask = stream_mask.astype(f32)[:, None]

    def tp_sum(sent, kept):
        chip = (kept + lax.ppermute(sent, "core", SWAP).astype(f32)).astype(bf16)
        return add_up(lax.all_gather(chip, "xl"))

    sent = in_vmem(rows_product, shape((half, width), bf16), 2, 1)(other, hidden, in_proj)
    kept = in_vmem(rows_product, shape((half, width), f32), 2, 1)(mine, hidden, in_proj)
    x = tp_sum(sent, kept)
    inv_rms = lax.rsqrt(jnp.mean(x * x, axis=1, keepdims=True) + norm_eps)
    unit_rows = x * inv_rms
    normed = lax.all_gather((unit_rows * gain).astype(bf16), "core", tiled=True)

    exp_logits, sums = in_vmem(
        exp_rows, [shape((frames, vocab_part), f32), shape((frames, 1), f32)], 2
    )(normed, head_weight)
    exp_total = jnp.sum(lax.all_gather(sums[:, 0], TP), axis=0)[:, None]

    rest = (exp_logits, exp_total, code, mask, head_weight)
    sent = in_vmem(sent_grad, shape((half, width), bf16), 5, 1)(other, *rest)
    kept, head_blocks = in_vmem(
        kept_grad,
        [shape((half, width), f32), shape((BLOCKS - PROJ_BLOCKS, 8, width), bf16)],
        6,
        1,
    )(mine, *rest, normed)
    scaled_grad = tp_sum(sent, kept) * gain
    centred = scaled_grad - unit_rows * jnp.mean(scaled_grad * unit_rows, axis=1, keepdims=True)
    row_grad = lax.all_gather((inv_rms * centred).astype(bf16), "core", tiled=True)

    blocks = in_vmem(grad_blocks, shape((N_NEAR, N_FAR * 8, width), bf16), 3)(hidden, row_grad, head_blocks)
    pieces = lax.all_to_all(blocks, NEAR, 0, 0)
    rows = 32
    near = pl.pallas_call(
        near_sum,
        out_shape=shape((N_FAR * 8, width), bf16),
        grid=(N_FAR * 8 // rows,),
        in_specs=[pl.BlockSpec((N_NEAR, rows, width), lambda i: (0, i, 0))],
        out_specs=pl.BlockSpec((rows, width), lambda i: (i, 0)),
        compiler_params=pltpu.CompilerParams(vmem_limit_bytes=VMEM_BYTES),
    )(pieces)
    far = lax.all_to_all(near.reshape(N_FAR, 8, width), FAR, 0, 0)
    is_proj = (lax.axis_index(SEQ) < PROJ_BLOCKS).astype(jnp.int32).reshape(1)
    weight_grads = in_vmem(far_sum, shape((8, 2, vocab_part), f32), 1, 1)(is_proj, far).reshape(16, vocab_part)

    hidden_grad = (loss_scale * dot(row_grad, in_proj, 1, 1)).astype(bf16)
    return (hidden_grad, weight_grads[None])


def solution(mesh):
    fine = Mesh(mesh.devices.reshape(SIZES), AXES)
    in_specs = (P(SEQ, TP), P(TP, None), P(), P(None, TP), P(SEQ), P(SEQ))
    out_specs = (P(SEQ, TP), P(TP, SEQ, None))
    return jax.shard_map(local, mesh=fine, in_specs=in_specs, out_specs=out_specs, check_vma=False)
```

time: 157 us -> 140 us (0.89)
  blocking collectives: 27.8 us -> 77 us
  waiting for transfers between devices: 53.1 us -> 19.6 us
  starting transfers between devices: 46.5 us -> 23.4 us
  matrix products: 14.1 us -> 1.54 us
  Pallas kernels: 0 us -> 6.57 us
  other arithmetic: 9.22 us -> 3.29 us
  local copies, waits for them, and re-layouts: 4.92 us -> 7.66 us
    all_to_all x0 -> x1, blocking collectives: none -> 46.5 us  [local(): pieces = lax.all_to_all(blocks, NEAR, 0, 0)]
    ppermute x4 -> x2, waiting for transfers between devices: 20.6 us -> 0.6 us  [tp_sum(): chip = (kept + lax.ppermute(sent, 'core', SWAP).astype(f32)).astype(bf16)]
    all_to_all x4 -> x1, waiting for transfers between devices: 32.5 us -> 19 us  [local(): far = lax.all_to_all(near.reshape(N_FAR, 8, width), FAR, 0, 0)]
    dot_general x7 -> x1, matrix products: 14.1 us -> 1.54 us  [dot(): lax.dot_general(a, b, (((ca,), (cb,)), ((), ())), preferred_element_type=...]
    all_to_all x4 -> x1, starting transfers between devices: 31 us -> 19 us  [local(): far = lax.all_to_all(near.reshape(N_FAR, 8, width), FAR, 0, 0)]
    ppermute x4 -> x2, starting transfers between devices: 15.5 us -> 4.43 us  [tp_sum(): chip = (kept + lax.ppermute(sent, 'core', SWAP).astype(f32)).astype(bf16)]
    pallas_call x0 -> x8, Pallas kernels: none -> 6.57 us  [the longest x1 2.33 us: local(): pl.pallas_call(near_sum, out_shape=shape((N_FAR * 8, width), bf16), grid=...]
    unnamed x12 -> x32, local copies, waits for them, and re-layouts: 1.61 us -> 6.6 us
  transfers between devices with their start and end apart: 8 -> 3, of which waited for: 6 -> 3; matrix products, arithmetic and copies ran while one was open for 6% -> 1% of each run, Pallas kernels for 0% -> 1%
where the time goes in v4:
time: 140 us
  blocking collectives  77 us (55%)
  starting transfers between devices  23.4 us (17%)
  waiting for transfers between devices  19.6 us (14%)
  local copies, waits for them, and re-layouts  7.66 us (5%)
  Pallas kernels  6.57 us (5%)
  other arithmetic  3.29 us (2%)
  matrix products  1.54 us (1%)
    all_to_all x1, blocking collectives, local(): pieces = lax.all_to_all(blocks, NEAR, 0, 0)  46.5 us
    all_to_all x1, starting transfers between devices, local(): far = lax.all_to_all(near.reshape(N_FAR, 8, width), FAR, 0, 0)  19 us
    all_to_all x1, waiting for transfers between devices, local(): far = lax.all_to_all(near.reshape(N_FAR, 8, width), FAR, 0, 0)  19 us
    all_gather x2, blocking collectives, tp_sum(): return add_up(lax.all_gather(chip, 'xl'))  18.5 us
    all_gather x1, blocking collectives, local(): exp_total = jnp.sum(lax.all_gather(sums[:, 0], TP), axis=0)[:, None]  7.6 us
    unnamed x32, local copies, waits for them, and re-layouts  6.6 us
    ppermute x2, starting transfers between devices, tp_sum(): chip = (kept + lax.ppermute(sent, 'core', SWAP).astype(f32)).astype(bf16)  4.43 us
  transfers between devices with their start and end apart: 3, of which 3 were waited for; matrix products, arithmetic and copies ran while one was open for 1% of the time, Pallas kernels for 1%

profile of v4, /device:TPU:16, one launch (start us, length us, event | category | flops | bytes accessed | tf_op | source)
XLA Modules:
  0.0 139.9 jit_solution(6949424567331499059)
XLA Ops:
  0.6 0.0 copy-start.1
  0.6 1.6 %copy-done.1 = bf16[1024,1024]{1,0:T(8,128)(2,1)S(1)} copy-done((bf16[1024,1024]{1,0:T(8,128)(2,1)S(1)}, bf16[1024,1024]{1,0:T(8,128)(2,1)}, u32[]{:S(2)}) %copy-start.1) | copy-done | bytes 2097176
  2.2 0.0 copy-start.5
  2.2 1.0 copy-done.5
  3.3 0.0 copy-start.2
  3.3 0.0 copy-start.6
  3.3 1.2 shard_map.78
  4.4 0.0 copy-start.14
  4.4 0.0 copy-start.15
  4.4 2.0 %collective-permute-start = (bf16[128,1024]{1,0:T(8,128)(2,1)}, bf16[128,1024]{1,0:T(8,128)(2,1)}, u32[]{:S(2)}, u32[]{:S(2)}) collective-permute-start(bf16[128,1024]{1,0:T(8,128)(2,1)} %shard_map.78), channel_id=1, source_target_pairs={{0,1},{1,0},{2,3},{3,2},{4,5},{5,4},{6,7},{7,6},{8,9},{9,8},{10,11... | collective-permute-start | bytes 786440 | tf_op jit(solution)/shard_map/ppermute | solution.py:145
  6.5 0.0 copy-done.2
  6.5 0.0 copy-done.6
  6.5 0.4 shard_map.77
  7.0 0.0 copy-start.10
  7.0 0.8 copy-done.10
  7.8 0.0 copy-start.13
  7.8 0.0 copy-done.14
  7.8 0.0 copy-start
  7.8 0.1 copy.10.mask_ref
  7.9 0.0 copy-done.15
  7.9 0.1 copy.9.code_ref
  8.1 0.3 collective-permute-done
  8.3 1.2 add_convert_fusion.1
  9.5 9.2 %all-gather = bf16[256,1024]{1,0:T(8,128)(2,1)S(1)} all-gather(bf16[128,1024]{1,0:T(8,128)(2,1)S(1)} %add_convert_fusion.1), channel_id=2, replica_groups=mesh['yh'=4,'yl'=2,'xh'=2,'zh'=6,'zl'=2,'xl'=2,'core'=2] {'xl'}, dimensions={0}, use_global_device_ids=true | all-gather | bytes 786432 | tf_op jit(solution)/shard_map/all_gather | solution.py:146
  18.6 0.0 copy-start.11
  18.7 0.2 multiply_reduce_fusion.1
  18.8 0.0 copy-done.13
  18.8 0.1 multiply_convert_fusion.1
  19.0 0.5 copy-done.11
  19.4 2.2 %all_gather.23.normed_ref = bf16[256,1024]{1,0:T(8,128)(2,1)S(1)} all-gather(bf16[128,1024]{1,0:T(8,128)(2,1)S(1)} %multiply_convert_fusion.1), channel_id=1, replica_groups=mesh['yh'=4,'yl'=2,'xh'=2,'zh'=6,'zl'=2,'xl'=2,'core'=2] {'core'}, dimensions={0}, use_global_device_ids=true | all-gather | bytes 786432 | tf_op jit(solution)/shard_map/all_gather | solution.py:153
  21.6 0.0 copy-done
  21.6 0.5 shard_map.79
  22.1 0.0 copy-start.3
  22.1 0.8 copy-done.3
  22.9 0.0 copy-start.8
  22.9 0.8 copy-done.8
  23.7 7.6 %all-gather.1 = f32[1024,1]{1,0:T(8,128)} all-gather(f32[256,1]{1,0:T(8,128)S(1)} %get-tuple-element.7), channel_id=3, replica_groups=mesh['yh'=4,'yl'=2,'xh'=2,'zh'=6,'zl'=2,'xl'=2,'core'=2] {'xl','core'}, dimensions={0}, use_global_device_ids=true | all-gather | bytes 5120 | tf_op jit(solution)/shard_map/all_gather | solution.py:158
  31.3 1.2 reduce
  32.6 0.1 copy.8.totals_ref
  32.8 0.0 copy-start.4
  32.8 0.0 copy-start.9
  32.8 1.1 copy-done.9
  33.9 0.5 shard_map.81
  34.4 0.0 copy-start.12
  34.4 2.4 %collective-permute-start.1 = (bf16[128,1024]{1,0:T(8,128)(2,1)S(1)}, bf16[128,1024]{1,0:T(8,128)(2,1)S(1)}, u32[]{:S(2)}, u32[]{:S(2)}) collective-permute-start(bf16[128,1024]{1,0:T(8,128)(2,1)S(1)} %shard_map.81), channel_id=1, source_target_pairs={{0,1},{1,0},{2,3},{3,2},{4,5},{5,4},{6,7},{7,6},{8,9},{9,8},{10,11... | collective-permute-start | bytes 786440 | tf_op jit(solution)/shard_map/ppermute | solution.py:145
  36.8 0.0 copy-done.4
  36.8 0.8 shard_map.80
  37.6 0.3 collective-permute-done.1
  37.9 0.1 add_convert_fusion
  38.0 0.0 copy-start.7
  38.0 9.4 %all-gather.2 = bf16[256,1024]{1,0:T(8,128)(2,1)S(1)} all-gather(bf16[128,1024]{1,0:T(8,128)(2,1)S(1)} %add_convert_fusion), channel_id=4, replica_groups=mesh['yh'=4,'yl'=2,'xh'=2,'zh'=6,'zl'=2,'xl'=2,'core'=2] {'xl'}, dimensions={0}, use_global_device_ids=true | all-gather | bytes 786432 | tf_op jit(solution)/shard_map/all_gather | solution.py:146
  47.4 0.0 copy-done.12
  47.4 0.3 multiply_reduce_fusion
  47.7 0.2 multiply_convert_fusion
  47.9 2.2 %all_gather.27.grad_ref = bf16[256,1024]{1,0:T(8,128)(2,1)S(1)} all-gather(bf16[128,1024]{1,0:T(8,128)(2,1)S(1)} %multiply_convert_fusion), channel_id=1, replica_groups=mesh['yh'=4,'yl'=2,'xh'=2,'zh'=6,'zl'=2,'xl'=2,'core'=2] {'core'}, dimensions={0}, use_global_device_ids=true | all-gather | bytes 786432 | tf_op jit(solution)/shard_map/all_gather | solution.py:170
  50.1 0.0 copy-done.7
  50.1 0.8 shard_map.82
  50.8 46.5 %all_to_all.10.pieces_ref = bf16[8,192,1024]{2,1,0:T(8,128)(2,1)S(1)} all-to-all(bf16[8,192,1024]{2,1,0:T(8,128)(2,1)S(1)} %shard_map.82), channel_id=1, replica_groups=mesh['yh'=4,'yl'=2,'xh'=2,'zh'=6,'zl'=2,'xl'=2,'core'=2] {'yl','xh','zl'}, dimensions={0} | all-to-all | bytes 6291456 | tf_op jit(solution)/shard_map/all_to_all | solution.py:173
  97.3 2.3 %shard_map.83 = bf16[192,1024]{1,0:T(8,128)(2,1)} custom-call(bf16[8,192,1024]{2,1,0:T(8,128)(2,1)S(1)} %all_to_all.10.pieces_ref), custom_call_target="tpu_custom_call" | custom-call | tf_op jit(solution)/shard_map/pallas_call | solution.py:175
  99.7 19.0 %all-to-all-start.1 = ((bf16[24,8,1024]{2,1,0:T(8,128)(2,1)}), bf16[24,8,1024]{2,1,0:T(8,128)(2,1)S(1)}, u32[]{:S(2)}, u32[]{:S(2)}) async-start(bf16[24,8,1024]{2,1,0:T(8,128)(2,1)} %bitcast.5), calls=%async_computation.1 | async-start | bytes 786432 | tf_op jit(solution)/shard_map/all_to_all | solution.py:183
  118.7 1.5 %fusion = bf16[256,1024]{1,0:T(8,128)(2,1)} fusion(bf16[256,1024]{1,0:T(8,128)(2,1)S(1)} %all_gather.27.grad_ref, bf16[1024,1024]{1,0:T(8,128)(2,1)S(1)} %copy-done.2), kind=kOutput, calls=%fused_computation.1 | convolution fusion | flops 537395200 | bytes 3145728 | tf_op jit(solution)/shard_map/dot_general | solution.py:29
  120.2 19.0 %all-to-all-done.1.pieces_ref = bf16[24,8,1024]{2,1,0:T(8,128)(2,1)S(1)} async-done(((bf16[24,8,1024]{2,1,0:T(8,128)(2,1)}), bf16[24,8,1024]{2,1,0:T(8,128)(2,1)S(1)}, u32[]{:S(2)}, u32[]{:S(2)}) %all-to-all-start.1) | async-done | bytes 393248 | tf_op jit(solution)/shard_map/all_to_all | solution.py:183
  139.2 0.1 shard_map.84
  139.3 0.6 broadcast_in_dim_reshape.3
  (6 shorter events, 0.1 us)
Async XLA Ops:
  0.6 1.6 %copy-start.1 = (bf16[1024,1024]{1,0:T(8,128)(2,1)S(1)}, bf16[1024,1024]{1,0:T(8,128)(2,1)}, u32[]{:S(2)}) copy-start(bf16[1024,1024]{1,0:T(8,128)(2,1)} %b_ref.3) | copy-start | bytes 6291460
  2.2 1.0 copy-start.5
  3.3 3.2 %copy-start.2 = (bf16[1024,1024]{1,0:T(8,128)(2,1)S(1)}, bf16[1024,1024]{1,0:T(8,128)(2,1)}, u32[]{:S(2)}) copy-start(bf16[1024,1024]{1,0:T(8,128)(2,1)} %b_ref.3) | copy-start | bytes 6291460
  3.3 3.2 %copy-start.6 = (bf16[256,1024]{1,0:T(8,128)(2,1)S(1)}, bf16[256,1024]{1,0:T(8,128)(2,1)}, u32[]{:S(2)}) copy-start(bf16[256,1024]{1,0:T(8,128)(2,1)} %hidden_ref.1) | copy-start | bytes 1572868
  4.4 3.3 %copy-start.14 = (s32[256]{0:T(256)S(1)}, s32[256]{0:T(256)}, u32[]{:S(2)}) copy-start(s32[256]{0:T(256)} %param.11) | copy-start | bytes 3076
  4.4 3.5 %copy-start.15 = (s32[256]{0:T(256)S(1)}, s32[256]{0:T(256)}, u32[]{:S(2)}) copy-start(s32[256]{0:T(256)} %param.10) | copy-start | bytes 3076
  4.4 3.9 %collective-permute-start = (bf16[128,1024]{1,0:T(8,128)(2,1)}, bf16[128,1024]{1,0:T(8,128)(2,1)}, u32[]{:S(2)}, u32[]{:S(2)}) collective-permute-start(bf16[128,1024]{1,0:T(8,128)(2,1)} %shard_map.78), channel_id=1, source_target_pairs={{0,1},{1,0},{2,3},{3,2},{4,5},{5,4},{6,7},{7,6},{8,9},{9,8},{10,11... | collective-permute-start | bytes 786440 | tf_op jit(solution)/shard_map/ppermute | solution.py:145
  7.0 0.8 copy-start.10
  7.8 11.1 %copy-start.13 = (f32[1024]{0:T(1024)S(1)}, f32[1024]{0:T(1024)}, u32[]{:S(2)}) copy-start(f32[1024]{0:T(1024)} %param.8) | copy-start | bytes 12292
  7.8 13.8 %copy-start = (bf16[1024,512]{1,0:T(8,128)(2,1)S(1)}, bf16[1024,512]{1,0:T(8,128)(2,1)}, u32[]{:S(2)}) copy-start(bf16[1024,512]{1,0:T(8,128)(2,1)} %head_ref.5) | copy-start | bytes 3145732
  18.6 0.8 copy-start.11
  22.1 0.8 copy-start.3
  22.9 0.8 copy-start.8
  32.8 4.0 %copy-start.4 = (bf16[256,1024]{1,0:T(8,128)(2,1)S(1)}, bf16[256,1024]{1,0:T(8,128)(2,1)}, u32[]{:S(2)}) copy-start(bf16[256,1024]{1,0:T(8,128)(2,1)} %copy-done.3) | copy-start | bytes 1572868
  32.8 1.1 copy-start.9
  34.4 13.0 %copy-start.12 = (bf16[256,1024]{1,0:T(8,128)(2,1)S(1)}, bf16[256,1024]{1,0:T(8,128)(2,1)}, u32[]{:S(2)}) copy-start(bf16[256,1024]{1,0:T(8,128)(2,1)} %copy-done.11) | copy-start | bytes 1572868
  34.4 3.6 %collective-permute-start.1 = (bf16[128,1024]{1,0:T(8,128)(2,1)S(1)}, bf16[128,1024]{1,0:T(8,128)(2,1)S(1)}, u32[]{:S(2)}, u32[]{:S(2)}) collective-permute-start(bf16[128,1024]{1,0:T(8,128)(2,1)S(1)} %shard_map.81), channel_id=1, source_target_pairs={{0,1},{1,0},{2,3},{3,2},{4,5},{5,4},{6,7},{7,6},{8,9},{9,8},{10,11... | collective-permute-start | bytes 786440 | tf_op jit(solution)/shard_map/ppermute | solution.py:145
  38.0 12.1 %copy-start.7 = (bf16[256,1024]{1,0:T(8,128)(2,1)S(1)}, bf16[256,1024]{1,0:T(8,128)(2,1)}, u32[]{:S(2)}) copy-start(bf16[256,1024]{1,0:T(8,128)(2,1)} %hidden_ref.1) | copy-start | bytes 1572868
  99.7 39.5 %all-to-all-start.1 = ((bf16[24,8,1024]{2,1,0:T(8,128)(2,1)}), bf16[24,8,1024]{2,1,0:T(8,128)(2,1)S(1)}, u32[]{:S(2)}, u32[]{:S(2)}) async-start(bf16[24,8,1024]{2,1,0:T(8,128)(2,1)} %bitcast.5), calls=%async_computation.1 | async-start | bytes 786432 | tf_op jit(solution)/shard_map/all_to_all | solution.py:183

commit v5 on v4

--- a/solution.py
+++ b/solution.py
@@ -41,24 +41,70 @@
     return (y % 2 * 2 + x) * 2 + z % 2, y // 2 * 6 + z // 2
 
 
-def rows_product(half_ref, a_ref, b_ref, out_ref):
+def rows_product_sum(half_ref, a_ref, b_ref, other_ref, out_ref):
     rows = out_ref.shape[0]
     start = pl.multiple_of(half_ref[0] * rows, rows)
-    out_ref[...] = dot(a_ref[pl.ds(start, rows), :], b_ref[...], 1, 0).astype(out_ref.dtype)
+    kept = dot(a_ref[pl.ds(start, rows), :], b_ref[...], 1, 0)
+    out_ref[...] = (kept + other_ref[...].astype(f32)).astype(out_ref.dtype)
+
+
+def streamed_product(half_ref, a_hbm, b_hbm, out_ref, a_ref, b_ref, sems):
+    rows, steps = out_ref.shape[0], b_ref.shape[0]
+    start = pl.multiple_of(half_ref[0] * rows, rows)
+    depth = b_ref.shape[1]
+    copies = [pltpu.make_async_copy(a_hbm.at[pl.ds(start, rows), :], a_ref, sems.at[steps])]
+    for i in range(steps):
+        copies.append(pltpu.make_async_copy(b_hbm.at[i * depth : (i + 1) * depth, :], b_ref.at[i], sems.at[i]))
+    for copy in copies:
+        copy.start()
+    copies[0].wait()
+    total = None
+    for i in range(steps):
+        copies[1 + i].wait()
+        part = dot(a_ref[:, i * depth : (i + 1) * depth], b_ref[i], 1, 0)
+        total = part if total is None else total + part
+    out_ref[...] = total.astype(out_ref.dtype)
+
+
+def hidden_rows(grad_ref, b_hbm, out_ref, b_ref, sems):
+    steps, depth = b_ref.shape[0], b_ref.shape[1]
+    copies = [
+        pltpu.make_async_copy(b_hbm.at[i * depth : (i + 1) * depth, :], b_ref.at[i], sems.at[i]) for i in range(steps)
+    ]
+    for copy in copies:
+        copy.start()
+    for i in range(steps):
+        copies[i].wait()
+        part = loss_scale * dot(grad_ref[...], b_ref[i], 1, 1)
+        out_ref[:, i * depth : (i + 1) * depth] = part.astype(out_ref.dtype)
 
 
 def exp_rows(normed_ref, head_ref, exp_ref, sum_ref):
     exp_logits = jnp.exp(dot(normed_ref[...], head_ref[...], 1, 0))
     exp_ref[...] = exp_logits
-    sum_ref[...] = jnp.sum(exp_logits, axis=1, keepdims=True)
+    ones = jnp.ones((8, exp_logits.shape[1]), f32)
+    sums = lax.dot_general(
+        ones, exp_logits, (((1,), (1,)), ((), ())), precision=lax.Precision.HIGHEST, preferred_element_type=f32
+    )
+    sum_ref[...] = sums[:1]
+
+
+def spread(rows):
+    ones = jnp.ones((rows.shape[0], 128), f32)
+    return lax.dot_general(
+        rows, ones, (((0,), (0,)), ((), ())), precision=lax.Precision.HIGHEST, preferred_element_type=f32
+    )
 
 
 def dlogit_rows(first, exp_ref, totals_ref, code_ref, mask_ref, rows):
     window = pl.ds(first, rows)
-    exp_logits = exp_ref[window, :]
-    columns = lax.broadcasted_iota(jnp.int32, exp_logits.shape, 1)
-    onehot = (columns == code_ref[window, :]).astype(f32)
-    return (mask_ref[window, :] * (exp_logits / totals_ref[window, :] - onehot)).astype(bf16)
+    total, code, mask = (spread(ref[:, window]) for ref in (totals_ref, code_ref, mask_ref))
+    parts = []
+    for start in range(0, exp_ref.shape[1], 128):
+        columns = (lax.broadcasted_iota(jnp.int32, (rows, 128), 1) + start).astype(f32)
+        onehot = (columns == code).astype(f32)
+        parts.append((mask * (exp_ref[window, start : start + 128] / total - onehot)).astype(bf16))
+    return jnp.concatenate(parts, axis=1)
 
 
 def sent_grad(half_ref, exp_ref, totals_ref, code_ref, mask_ref, head_ref, out_ref):
@@ -93,25 +139,30 @@
         out_ref[near, 8 * far : 8 * far + 8, :] = head_ref[block - PROJ_BLOCKS]
 
 
+def chip_sum(kept_ref, other_ref, out_ref):
+    out_ref[...] = (kept_ref[...] + other_ref[...].astype(f32)).astype(out_ref.dtype)
+
+
 def near_sum(pieces_ref, out_ref):
-    out_ref[...] = add_up(pieces_ref).astype(out_ref.dtype)
+    step = 16
+    for first in range(0, out_ref.shape[0], step):
+        out_ref[first : first + step] = add_up(pieces_ref.at[:, first : first + step]).astype(out_ref.dtype)
 
 
 def far_sum(is_proj_ref, pieces_ref, out_ref):
     total = add_up(pieces_ref)
-    part = out_ref.shape[2]
-    left, right = total[:, :part], total[:, part:]
+    rows, part = total.shape[0], out_ref.shape[1]
 
     @pl.when(is_proj_ref[0] == 1)
     def _():
-        out_ref[:, 0, :] = left
-        out_ref[:, 1, :] = right
+        for row in range(rows):
+            out_ref[2 * row : 2 * row + 1, :] = total[row : row + 1, :part]
+            out_ref[2 * row + 1 : 2 * row + 2, :] = total[row : row + 1, part:]
 
     @pl.when(is_proj_ref[0] == 0)
     def _():
-        for row in range(4):
-            out_ref[row] = left[2 * row : 2 * row + 2]
-            out_ref[4 + row] = right[2 * row : 2 * row + 2]
+        out_ref[:rows, :] = total[:, :part]
+        out_ref[rows:, :] = total[:, part:]
 
 
 def in_vmem(kernel, outs, n_in, scalars=0):
@@ -138,26 +189,36 @@
     gain = norm_gain[None, :]
     mine = lax.axis_index("core").reshape(1)
     other = 1 - mine
-    code = (code_ids - tp * vocab_part)[:, None]
-    mask = stream_mask.astype(f32)[:, None]
-
-    def tp_sum(sent, kept):
-        chip = (kept + lax.ppermute(sent, "core", SWAP).astype(f32)).astype(bf16)
-        return add_up(lax.all_gather(chip, "xl"))
-
-    sent = in_vmem(rows_product, shape((half, width), bf16), 2, 1)(other, hidden, in_proj)
-    kept = in_vmem(rows_product, shape((half, width), f32), 2, 1)(mine, hidden, in_proj)
-    x = tp_sum(sent, kept)
+    code = (code_ids - tp * vocab_part).astype(f32)[None, :]
+    mask = stream_mask.astype(f32)[None, :]
+
+    steps, inner = 4, hidden.shape[1]
+    sent = pl.pallas_call(
+        streamed_product,
+        out_shape=shape((half, width), bf16),
+        in_specs=[pl.BlockSpec(memory_space=pltpu.SMEM)] + [pl.BlockSpec(memory_space=pltpu.HBM)] * 2,
+        out_specs=pl.BlockSpec(memory_space=pltpu.VMEM),
+        scratch_shapes=[
+            pltpu.VMEM((half, inner), bf16),
+            pltpu.VMEM((steps, inner // steps, width), bf16),
+            pltpu.SemaphoreType.DMA((steps + 1,)),
+        ],
+        compiler_params=pltpu.CompilerParams(vmem_limit_bytes=VMEM_BYTES),
+    )(other, *(pltpu.with_memory_space_constraint(array, pltpu.HBM) for array in (hidden, in_proj)))
+    chip = in_vmem(rows_product_sum, shape((half, width), bf16), 3, 1)(
+        mine, hidden, in_proj, lax.ppermute(sent, "core", SWAP)
+    )
+    x = add_up(lax.all_gather(chip, "xl"))
     inv_rms = lax.rsqrt(jnp.mean(x * x, axis=1, keepdims=True) + norm_eps)
     unit_rows = x * inv_rms
     normed = lax.all_gather((unit_rows * gain).astype(bf16), "core", tiled=True)
 
     exp_logits, sums = in_vmem(
-        exp_rows, [shape((frames, vocab_part), f32), shape((frames, 1), f32)], 2
+        exp_rows, [shape((frames, vocab_part), f32), shape((1, frames), f32)], 2
     )(normed, head_weight)
-    exp_total = jnp.sum(lax.all_gather(sums[:, 0], TP), axis=0)[:, None]
-
-    rest = (exp_logits, exp_total, code, mask, head_weight)
+    totals = lax.all_gather(sums, TP, tiled=True)
+
+    rest = (exp_logits, totals, code, mask, head_weight)
     sent = in_vmem(sent_grad, shape((half, width), bf16), 5, 1)(other, *rest)
     kept, head_blocks = in_vmem(
         kept_grad,
@@ -165,26 +226,32 @@
         6,
         1,
     )(mine, *rest, normed)
-    scaled_grad = tp_sum(sent, kept) * gain
+    chip = in_vmem(chip_sum, shape((half, width), bf16), 2)(kept, lax.ppermute(sent, "core", SWAP))
+    scaled_grad = add_up(lax.all_gather(chip, "xl")) * gain
     centred = scaled_grad - unit_rows * jnp.mean(scaled_grad * unit_rows, axis=1, keepdims=True)
     row_grad = lax.all_gather((inv_rms * centred).astype(bf16), "core", tiled=True)
 
     blocks = in_vmem(grad_blocks, shape((N_NEAR, N_FAR * 8, width), bf16), 3)(hidden, row_grad, head_blocks)
     pieces = lax.all_to_all(blocks, NEAR, 0, 0)
-    rows = 32
-    near = pl.pallas_call(
-        near_sum,
-        out_shape=shape((N_FAR * 8, width), bf16),
-        grid=(N_FAR * 8 // rows,),
-        in_specs=[pl.BlockSpec((N_NEAR, rows, width), lambda i: (0, i, 0))],
-        out_specs=pl.BlockSpec((rows, width), lambda i: (i, 0)),
-        compiler_params=pltpu.CompilerParams(vmem_limit_bytes=VMEM_BYTES),
-    )(pieces)
+    near = in_vmem(near_sum, shape((N_FAR * 8, width), bf16), 1)(pieces)
     far = lax.all_to_all(near.reshape(N_FAR, 8, width), FAR, 0, 0)
     is_proj = (lax.axis_index(SEQ) < PROJ_BLOCKS).astype(jnp.int32).reshape(1)
-    weight_grads = in_vmem(far_sum, shape((8, 2, vocab_part), f32), 1, 1)(is_proj, far).reshape(16, vocab_part)
-
-    hidden_grad = (loss_scale * dot(row_grad, in_proj, 1, 1)).astype(bf16)
+    weight_grads = in_vmem(far_sum, shape((16, vocab_part), f32), 1, 1)(is_proj, far)
+
+    hidden_grad = pl.pallas_call(
+        hidden_rows,
+        out_shape=shape((frames, inner), bf16),
+        in_specs=[pl.BlockSpec(memory_space=pltpu.VMEM), pl.BlockSpec(memory_space=pltpu.HBM)],
+        out_specs=pl.BlockSpec(memory_space=pltpu.VMEM),
+        scratch_shapes=[
+            pltpu.VMEM((steps, inner // steps, width), bf16),
+            pltpu.SemaphoreType.DMA((steps,)),
+        ],
+        compiler_params=pltpu.CompilerParams(vmem_limit_bytes=VMEM_BYTES),
+        cost_estimate=pl.CostEstimate(
+            flops=2 * frames * inner * width, transcendentals=0, bytes_accessed=2 * width * (inner + 2 * frames)
+        ),
+    )(row_grad, pltpu.with_memory_space_constraint(in_proj, pltpu.HBM))
     return (hidden_grad, weight_grads[None])
 
 

time: 140 us -> 133 us (0.950)
  Pallas kernels: 6.57 us -> 13.4 us
  local copies, waits for them, and re-layouts: 7.66 us -> 1.07 us
  blocking collectives: 77 us -> 74.3 us
  waiting for transfers between devices: 19.6 us -> 17.1 us
  matrix products: 1.54 us -> 0 us
    pallas_call x5 -> x7, Pallas kernels: 4.53 us -> 10.1 us  [the longest x1 3.69 us: local(): pl.pallas_call(hidden_rows, out_shape=shape((frames, inner), bf16), in_sp...]
    unnamed x32 -> x11, local copies, waits for them, and re-layouts: 6.6 us -> 1.07 us
    all_gather x3, blocking collectives: 26.1 us -> 23.3 us  [the longest x1 9.13 us: local(): x = add_up(lax.all_gather(chip, 'xl'))]
    all_to_all x1, waiting for transfers between devices: 19 us -> 16.8 us  [local(): far = lax.all_to_all(near.reshape(N_FAR, 8, width), FAR, 0, 0)]
    dot_general x1 -> x0, matrix products: 1.54 us -> none  [dot(): lax.dot_general(a, b, (((ca,), (cb,)), ((), ())), preferred_element_type=...]
  transfers between devices with their start and end apart: 3 -> 3, of which waited for: 3 -> 2; matrix products, arithmetic and copies ran while one was open for 1% -> 1% of each run, Pallas kernels for 1% -> 4%
where the time goes in v5:
time: 133 us; the launch traced here: 132 us
  blocking collectives  74.3 us (56%)
  starting transfers between devices  23.4 us (18%)
  waiting for transfers between devices  17.1 us (13%)
  Pallas kernels  13.4 us (10%)
  other arithmetic  2.16 us (2%)
    all_to_all x1, blocking collectives, local(): pieces = lax.all_to_all(blocks, NEAR, 0, 0)  46.6 us
    all_to_all x1, starting transfers between devices, local(): far = lax.all_to_all(near.reshape(N_FAR, 8, width), FAR, 0, 0)  19 us
    all_to_all x1, waiting for transfers between devices, local(): far = lax.all_to_all(near.reshape(N_FAR, 8, width), FAR, 0, 0)  16.8 us
    all_gather x1, blocking collectives, local(): x = add_up(lax.all_gather(chip, 'xl'))  9.13 us
    all_gather x1, blocking collectives, local(): scaled_grad = add_up(lax.all_gather(chip, 'xl')) * gain  9.09 us
    all_gather x1, blocking collectives, local(): totals = lax.all_gather(sums, TP, tiled=True)  5.09 us
    ppermute x2, starting transfers between devices, local(): lax.ppermute(sent, 'core', SWAP)  4.41 us
    pallas_call x1, Pallas kernels, local(): pl.pallas_call(hidden_rows, out_shape=shape((frames, inner), bf16), in_sp...  3.69 us
  transfers between devices with their start and end apart: 3, of which 2 were waited for; matrix products, arithmetic and copies ran while one was open for 1% of the time, Pallas kernels for 4%

profile of v5, /device:TPU:16, one launch (start us, length us, event | category | flops | bytes accessed | tf_op | source)
XLA Modules:
  0.0 132.2 jit_solution(8336008476496619765)
XLA Ops:
  0.6 0.0 copy-start
  0.6 0.0 copy-start.4
  0.7 2.0 %shard_map.77 = bf16[128,1024]{1,0:T(8,128)(2,1)S(1)} custom-call(s32[1]{0:T(128)S(6)} %sub.12.half_ref, bf16[256,1024]{1,0:T(8,128)(2,1)} %hidden_ref.1, bf16[1024,1024]{1,0:T(8,128)(2,1)} %b_hbm.3), custom_call_target="tpu_custom_call" | custom-call | tf_op jit(solution)/shard_map/pallas_call | solution.py:196
  2.7 0.0 copy-start.1
  2.7 2.1 %collective-permute-start = (bf16[128,1024]{1,0:T(8,128)(2,1)S(1)}, bf16[128,1024]{1,0:T(8,128)(2,1)}, u32[]{:S(2)}, u32[]{:S(2)}) collective-permute-start(bf16[128,1024]{1,0:T(8,128)(2,1)S(1)} %shard_map.77), channel_id=1, source_target_pairs={{0,1},{1,0},{2,3},{3,2},{4,5},{5,4},{6,7},{7,6},{8,9},{9,8},{10,11... | collective-permute-start | bytes 786440 | tf_op jit(solution)/shard_map/ppermute | solution.py:209
  4.8 0.7 convert_element_type.33
  5.5 0.7 subtract_convert_fusion
  6.1 0.3 collective-permute-done.other_ref
  6.4 0.0 copy-done
  6.4 0.0 copy-start.2
  6.4 1.0 copy-done.2
  7.4 1.4 %shard_map.78 = bf16[128,1024]{1,0:T(8,128)(2,1)S(1)} custom-call(s32[1]{0:T(128)} %bitcast.half_ref, bf16[256,1024]{1,0:T(8,128)(2,1)S(1)} %copy-done.2, bf16[1024,1024]{1,0:T(8,128)(2,1)S(1)} %copy-done, bf16[128,1024]{1,0:T(8,128)(2,1)} %collective-permute-done.other_ref), custom_call_target="tpu_custom_call" | custom-call | tf_op jit(solution)/shard_map/pallas_call | solution.py:208
  8.8 9.1 %all-gather = bf16[256,1024]{1,0:T(8,128)(2,1)S(1)} all-gather(bf16[128,1024]{1,0:T(8,128)(2,1)S(1)} %shard_map.78), channel_id=2, replica_groups=mesh['yh'=4,'yl'=2,'xh'=2,'zh'=6,'zl'=2,'xl'=2,'core'=2] {'xl'}, dimensions={0}, use_global_device_ids=true | all-gather | bytes 786432 | tf_op jit(solution)/shard_map/all_gather | solution.py:211
  18.0 0.2 multiply_reduce_fusion.1
  18.2 0.0 copy-done.4
  18.2 0.1 multiply_convert_fusion.1
  18.3 2.2 %all_gather.23.normed_ref = bf16[256,1024]{1,0:T(8,128)(2,1)S(1)} all-gather(bf16[128,1024]{1,0:T(8,128)(2,1)S(1)} %multiply_convert_fusion.1), channel_id=1, replica_groups=mesh['yh'=4,'yl'=2,'xh'=2,'zh'=6,'zl'=2,'xl'=2,'core'=2] {'core'}, dimensions={0}, use_global_device_ids=true | all-gather | bytes 786432 | tf_op jit(solution)/shard_map/all_gather | solution.py:214
  20.5 0.0 copy-done.1
  20.5 1.1 shard_map.79
  21.5 5.1 %all-gather.2 = f32[4,1,256]{2,1,0:T(1,128)S(1)} all-gather(f32[1,1,256]{2,1,0:T(1,128)S(1)} %bitcast.16), channel_id=1, replica_groups=mesh['yh'=4,'yl'=2,'xh'=2,'zh'=6,'zl'=2,'xl'=2,'core'=2] {'xl','core'}, dimensions={0}, use_global_device_ids=true | all-gather | bytes 5120 | tf_op jit(solution)/shard_map/all_gather | solution.py:219
  26.6 0.9 shard_map.81
  27.5 0.0 copy-start.3
  27.5 2.4 %collective-permute-start.1 = (bf16[128,1024]{1,0:T(8,128)(2,1)S(1)}, bf16[128,1024]{1,0:T(8,128)(2,1)S(1)}, u32[]{:S(2)}, u32[]{:S(2)}) collective-permute-start(bf16[128,1024]{1,0:T(8,128)(2,1)S(1)} %shard_map.81), channel_id=1, source_target_pairs={{0,1},{1,0},{2,3},{3,2},{4,5},{5,4},{6,7},{7,6},{8,9},{9,8},{10,11... | collective-permute-start | bytes 786440 | tf_op jit(solution)/shard_map/ppermute | solution.py:229
  29.9 1.7 %shard_map.80 = (f32[128,1024]{1,0:T(8,128)S(1)}, bf16[64,8,1024]{2,1,0:T(8,128)(2,1)S(1)}) custom-call(s32[1]{0:T(128)} %bitcast.half_ref, f32[256,512]{1,0:T(8,128)S(1)} %get-tuple-element.6.exp_ref, f32[4,256]{1,0:T(4,128)S(1)} %bitcast.11, f32[1,256]{1,0:T(1,128)S(1)} %bitcast.15, f32[1,256]{1,0:T(1,128)S(1)} %bitcast.13, ...), custom_call_target="tpu_custom_call" | custom-call | tf_op jit(solution)/shard_map/pallas_call | solution.py:223
  31.6 0.0 collective-permute-done.1.other_ref
  31.6 0.1 shard_map.82
  31.7 9.1 %all-gather.1 = bf16[256,1024]{1,0:T(8,128)(2,1)S(1)} all-gather(bf16[128,1024]{1,0:T(8,128)(2,1)S(1)} %shard_map.82), channel_id=3, replica_groups=mesh['yh'=4,'yl'=2,'xh'=2,'zh'=6,'zl'=2,'xl'=2,'core'=2] {'xl'}, dimensions={0}, use_global_device_ids=true | all-gather | bytes 786432 | tf_op jit(solution)/shard_map/all_gather | solution.py:230
  40.8 0.3 multiply_reduce_fusion
  41.0 0.2 multiply_convert_fusion
  41.3 2.2 %all_gather.27.grad_ref = bf16[256,1024]{1,0:T(8,128)(2,1)S(1)} all-gather(bf16[128,1024]{1,0:T(8,128)(2,1)S(1)} %multiply_convert_fusion), channel_id=1, replica_groups=mesh['yh'=4,'yl'=2,'xh'=2,'zh'=6,'zl'=2,'xl'=2,'core'=2] {'core'}, dimensions={0}, use_global_device_ids=true | all-gather | bytes 786432 | tf_op jit(solution)/shard_map/all_gather | solution.py:232
  43.5 0.0 copy-done.3
  43.5 0.8 shard_map.84
  44.2 46.6 %all_to_all.10.pieces_ref = bf16[8,192,1024]{2,1,0:T(8,128)(2,1)S(1)} all-to-all(bf16[8,192,1024]{2,1,0:T(8,128)(2,1)S(1)} %shard_map.84), channel_id=1, replica_groups=mesh['yh'=4,'yl'=2,'xh'=2,'zh'=6,'zl'=2,'xl'=2,'core'=2] {'yl','xh','zl'}, dimensions={0} | all-to-all | bytes 6291456 | tf_op jit(solution)/shard_map/all_to_all | solution.py:235
  90.8 1.1 shard_map.85
  91.9 19.0 %all-to-all-start.1 = ((bf16[24,8,1024]{2,1,0:T(8,128)(2,1)}), bf16[24,8,1024]{2,1,0:T(8,128)(2,1)S(1)}, u32[]{:S(2)}, u32[]{:S(2)}) async-start(bf16[24,8,1024]{2,1,0:T(8,128)(2,1)} %bitcast.5), calls=%async_computation.1 | async-start | bytes 786432 | tf_op jit(solution)/shard_map/all_to_all | solution.py:237
  111.0 3.7 %shard_map.83 = bf16[256,1024]{1,0:T(8,128)(2,1)} custom-call(bf16[256,1024]{1,0:T(8,128)(2,1)S(1)} %all_gather.27.grad_ref, bf16[1024,1024]{1,0:T(8,128)(2,1)} %b_hbm.3), custom_call_target="tpu_custom_call" | custom-call | flops 536870912 | bytes 3145728 | tf_op jit(solution)/shard_map/pallas_call | solution.py:241
  114.7 16.8 %all-to-all-done.1.pieces_ref = bf16[24,8,1024]{2,1,0:T(8,128)(2,1)S(1)} async-done(((bf16[24,8,1024]{2,1,0:T(8,128)(2,1)}), bf16[24,8,1024]{2,1,0:T(8,128)(2,1)S(1)}, u32[]{:S(2)}, u32[]{:S(2)}) %all-to-all-start.1) | async-done | bytes 393248 | tf_op jit(solution)/shard_map/all_to_all | solution.py:237
  131.5 0.7 shard_map.86
  (3 shorter events, 0.0 us)
Async XLA Ops:
  0.6 5.8 %copy-start = (bf16[1024,1024]{1,0:T(8,128)(2,1)S(1)}, bf16[1024,1024]{1,0:T(8,128)(2,1)}, u32[]{:S(2)}) copy-start(bf16[1024,1024]{1,0:T(8,128)(2,1)} %b_hbm.3) | copy-start | bytes 6291460
  0.6 17.5 %copy-start.4 = (f32[1024]{0:T(1024)S(1)}, f32[1024]{0:T(1024)}, u32[]{:S(2)}) copy-start(f32[1024]{0:T(1024)} %param.8) | copy-start | bytes 12292
  2.7 17.8 %copy-start.1 = (bf16[1024,512]{1,0:T(8,128)(2,1)S(1)}, bf16[1024,512]{1,0:T(8,128)(2,1)}, u32[]{:S(2)}) copy-start(bf16[1024,512]{1,0:T(8,128)(2,1)} %head_ref.5) | copy-start | bytes 3145732
  2.7 3.7 %collective-permute-start = (bf16[128,1024]{1,0:T(8,128)(2,1)S(1)}, bf16[128,1024]{1,0:T(8,128)(2,1)}, u32[]{:S(2)}, u32[]{:S(2)}) collective-permute-start(bf16[128,1024]{1,0:T(8,128)(2,1)S(1)} %shard_map.77), channel_id=1, source_target_pairs={{0,1},{1,0},{2,3},{3,2},{4,5},{5,4},{6,7},{7,6},{8,9},{9,8},{10,11... | collective-permute-start | bytes 786440 | tf_op jit(solution)/shard_map/ppermute | solution.py:209
  6.4 1.0 copy-start.2
  27.5 15.9 %copy-start.3 = (bf16[256,1024]{1,0:T(8,128)(2,1)S(1)}, bf16[256,1024]{1,0:T(8,128)(2,1)}, u32[]{:S(2)}) copy-start(bf16[256,1024]{1,0:T(8,128)(2,1)} %hidden_ref.1) | copy-start | bytes 1572868
  27.5 4.1 %collective-permute-start.1 = (bf16[128,1024]{1,0:T(8,128)(2,1)S(1)}, bf16[128,1024]{1,0:T(8,128)(2,1)S(1)}, u32[]{:S(2)}, u32[]{:S(2)}) collective-permute-start(bf16[128,1024]{1,0:T(8,128)(2,1)S(1)} %shard_map.81), channel_id=1, source_target_pairs={{0,1},{1,0},{2,3},{3,2},{4,5},{5,4},{6,7},{7,6},{8,9},{9,8},{10,11... | collective-permute-start | bytes 786440 | tf_op jit(solution)/shard_map/ppermute | solution.py:229
  91.9 39.5 %all-to-all-start.1 = ((bf16[24,8,1024]{2,1,0:T(8,128)(2,1)}), bf16[24,8,1024]{2,1,0:T(8,128)(2,1)S(1)}, u32[]{:S(2)}, u32[]{:S(2)}) async-start(bf16[24,8,1024]{2,1,0:T(8,128)(2,1)} %bitcast.5), calls=%async_computation.1 | async-start | bytes 786432 | tf_op jit(solution)/shard_map/all_to_all | solution.py:237

commit v6 on v5

--- a/solution.py
+++ b/solution.py
@@ -13,8 +13,8 @@
 SIZES = (4, 2, 2, 6, 2, 2, 2)
 SEQ = ("yh", "yl", "xh", "zh", "zl")
 TP = ("xl", "core")
-NEAR = ("yl", "xh", "zl")
-FAR = ("yh", "zh")
+NEAR = ("xh", "yl", "zl")
+FAR = ("zh", "yh")
 N_NEAR = 8
 N_FAR = 24
 BLOCKS = 192
@@ -38,32 +38,29 @@
 
 def near_far(block):
     y, x, z = block // 24, block // 12 % 2, block % 12
-    return (y % 2 * 2 + x) * 2 + z % 2, y // 2 * 6 + z // 2
-
-
-def rows_product_sum(half_ref, a_ref, b_ref, other_ref, out_ref):
-    rows = out_ref.shape[0]
-    start = pl.multiple_of(half_ref[0] * rows, rows)
-    kept = dot(a_ref[pl.ds(start, rows), :], b_ref[...], 1, 0)
-    out_ref[...] = (kept + other_ref[...].astype(f32)).astype(out_ref.dtype)
-
-
-def streamed_product(half_ref, a_hbm, b_hbm, out_ref, a_ref, b_ref, sems):
-    rows, steps = out_ref.shape[0], b_ref.shape[0]
-    start = pl.multiple_of(half_ref[0] * rows, rows)
-    depth = b_ref.shape[1]
-    copies = [pltpu.make_async_copy(a_hbm.at[pl.ds(start, rows), :], a_ref, sems.at[steps])]
+    return (x * 2 + y % 2) * 2 + z % 2, z // 2 * 4 + y // 2
+
+
+def streamed_product(half_ref, a_hbm, b_hbm, sent_ref, kept_ref, a_ref, b_ref, sems):
+    rows, steps, depth = sent_ref.shape[0], b_ref.shape[0], b_ref.shape[1]
+    copies = [pltpu.make_async_copy(a_hbm, a_ref, sems.at[steps])]
     for i in range(steps):
         copies.append(pltpu.make_async_copy(b_hbm.at[i * depth : (i + 1) * depth, :], b_ref.at[i], sems.at[i]))
     for copy in copies:
         copy.start()
     copies[0].wait()
-    total = None
+    mine = pl.ds(pl.multiple_of(half_ref[0] * rows, rows), rows)
+    other = pl.ds(pl.multiple_of((1 - half_ref[0]) * rows, rows), rows)
+    sent = kept = None
     for i in range(steps):
         copies[1 + i].wait()
-        part = dot(a_ref[:, i * depth : (i + 1) * depth], b_ref[i], 1, 0)
-        total = part if total is None else total + part
-    out_ref[...] = total.astype(out_ref.dtype)
+        columns = slice(i * depth, (i + 1) * depth)
+        sent_part = dot(a_ref[other, columns], b_ref[i], 1, 0)
+        kept_part = dot(a_ref[mine, columns], b_ref[i], 1, 0)
+        sent = sent_part if i == 0 else sent + sent_part
+        kept = kept_part if i == 0 else kept + kept_part
+    sent_ref[...] = sent.astype(sent_ref.dtype)
+    kept_ref[...] = kept
 
 
 def hidden_rows(grad_ref, b_hbm, out_ref, b_ref, sems):
@@ -82,9 +79,11 @@
 def exp_rows(normed_ref, head_ref, exp_ref, sum_ref):
     exp_logits = jnp.exp(dot(normed_ref[...], head_ref[...], 1, 0))
     exp_ref[...] = exp_logits
-    ones = jnp.ones((8, exp_logits.shape[1]), f32)
+    groups = exp_logits[:, :128]
+    for start in range(128, exp_logits.shape[1], 128):
+        groups = groups + exp_logits[:, start : start + 128]
     sums = lax.dot_general(
-        ones, exp_logits, (((1,), (1,)), ((), ())), precision=lax.Precision.HIGHEST, preferred_element_type=f32
+        jnp.ones((8, 128), f32), groups, (((1,), (1,)), ((), ())), precision=lax.Precision.HIGHEST, preferred_element_type=f32
     )
     sum_ref[...] = sums[:1]
 
@@ -98,12 +97,13 @@
 
 def dlogit_rows(first, exp_ref, totals_ref, code_ref, mask_ref, rows):
     window = pl.ds(first, rows)
-    total, code, mask = (spread(ref[:, window]) for ref in (totals_ref, code_ref, mask_ref))
+    total, code, weight = (spread(ref[:, window]) for ref in (totals_ref, code_ref, mask_ref))
+    scale = weight / total
     parts = []
     for start in range(0, exp_ref.shape[1], 128):
         columns = (lax.broadcasted_iota(jnp.int32, (rows, 128), 1) + start).astype(f32)
-        onehot = (columns == code).astype(f32)
-        parts.append((mask * (exp_ref[window, start : start + 128] / total - onehot)).astype(bf16))
+        onehot = jnp.where(columns == code, weight, 0.0)
+        parts.append((scale * exp_ref[window, start : start + 128] - onehot).astype(bf16))
     return jnp.concatenate(parts, axis=1)
 
 
@@ -193,21 +193,19 @@
     mask = stream_mask.astype(f32)[None, :]
 
     steps, inner = 4, hidden.shape[1]
-    sent = pl.pallas_call(
+    sent, kept = pl.pallas_call(
         streamed_product,
-        out_shape=shape((half, width), bf16),
+        out_shape=[shape((half, width), bf16), shape((half, width), f32)],
         in_specs=[pl.BlockSpec(memory_space=pltpu.SMEM)] + [pl.BlockSpec(memory_space=pltpu.HBM)] * 2,
-        out_specs=pl.BlockSpec(memory_space=pltpu.VMEM),
+        out_specs=[pl.BlockSpec(memory_space=pltpu.VMEM)] * 2,
         scratch_shapes=[
-            pltpu.VMEM((half, inner), bf16),
+            pltpu.VMEM((frames, inner), bf16),
             pltpu.VMEM((steps, inner // steps, width), bf16),
             pltpu.SemaphoreType.DMA((steps + 1,)),
         ],
         compiler_params=pltpu.CompilerParams(vmem_limit_bytes=VMEM_BYTES),
-    )(other, *(pltpu.with_memory_space_constraint(array, pltpu.HBM) for array in (hidden, in_proj)))
-    chip = in_vmem(rows_product_sum, shape((half, width), bf16), 3, 1)(
-        mine, hidden, in_proj, lax.ppermute(sent, "core", SWAP)
-    )
+    )(mine, *(pltpu.with_memory_space_constraint(array, pltpu.HBM) for array in (hidden, in_proj)))
+    chip = in_vmem(chip_sum, shape((half, width), bf16), 2)(kept, lax.ppermute(sent, "core", SWAP))
     x = add_up(lax.all_gather(chip, "xl"))
     inv_rms = lax.rsqrt(jnp.mean(x * x, axis=1, keepdims=True) + norm_eps)
     unit_rows = x * inv_rms

time: 133 us -> 132 us (level)
  the two profiles are of different devices: /device:TPU:16 before, /device:TPU:2 now
where the time goes in v6:
time: 132 us
  blocking collectives  78 us (59%)
  waiting for transfers between devices  20.2 us (15%)
  starting transfers between devices  18.6 us (14%)
  Pallas kernels  12.1 us (9%)
  other arithmetic  2.18 us (2%)
    all_to_all x1, blocking collectives, local(): pieces = lax.all_to_all(blocks, NEAR, 0, 0)  42.4 us
    all_to_all x1, waiting for transfers between devices, local(): far = lax.all_to_all(near.reshape(N_FAR, 8, width), FAR, 0, 0)  20.1 us
    all_gather x1, blocking collectives, local(): x = add_up(lax.all_gather(chip, 'xl'))  17.1 us
    all_to_all x1, starting transfers between devices, local(): far = lax.all_to_all(near.reshape(N_FAR, 8, width), FAR, 0, 0)  14.3 us
    all_gather x1, blocking collectives, local(): scaled_grad = add_up(lax.all_gather(chip, 'xl')) * gain  9.09 us
    all_gather x1, blocking collectives, local(): totals = lax.all_gather(sums, TP, tiled=True)  5.08 us
    ppermute x2, starting transfers between devices, local(): lax.ppermute(sent, 'core', SWAP)  4.27 us
    pallas_call x1, Pallas kernels, local(): pl.pallas_call(hidden_rows, out_shape=shape((frames, inner), bf16), in_sp...  3.69 us
  transfers between devices with their start and end apart: 3, of which 2 were waited for; matrix products, arithmetic and copies ran while one was open for 1% of the time, Pallas kernels for 4%

profile of v6, /device:TPU:2, one launch (start us, length us, event | category | flops | bytes accessed | tf_op | source)
XLA Modules:
  0.0 131.9 jit_solution(8793131394322954377)
XLA Ops:
  0.6 0.0 copy-start.2
  0.6 0.0 copy-start
  0.7 2.3 %shard_map.77 = (bf16[128,1024]{1,0:T(8,128)(2,1)S(1)}, f32[128,1024]{1,0:T(8,128)S(1)}) custom-call(s32[1]{0:T(128)} %bitcast.half_ref, bf16[256,1024]{1,0:T(8,128)(2,1)} %hidden_ref.1, bf16[1024,1024]{1,0:T(8,128)(2,1)} %b_hbm.3), custom_call_target="tpu_custom_call" | custom-call | tf_op jit(solution)/shard_map/pallas_call | solution.py:196
  3.0 1.9 %collective-permute-start = (bf16[128,1024]{1,0:T(8,128)(2,1)S(1)}, bf16[128,1024]{1,0:T(8,128)(2,1)S(1)}, u32[]{:S(2)}, u32[]{:S(2)}) collective-permute-start(bf16[128,1024]{1,0:T(8,128)(2,1)S(1)} %get-tuple-element.9), channel_id=1, source_target_pairs={{0,1},{1,0},{2,3},{3,2},{4,5},{5,4},{6,7},{7,6},{8,9},{9,8},{10,11... | collective-permute-start | bytes 786440 | tf_op jit(solution)/shard_map/ppermute | solution.py:208
  4.9 0.7 convert_element_type.33
  5.6 0.7 subtract_convert_fusion
  6.3 0.1 collective-permute-done.other_ref
  6.5 17.1 %all-gather = bf16[256,1024]{1,0:T(8,128)(2,1)S(1)} all-gather(bf16[128,1024]{1,0:T(8,128)(2,1)S(1)} %shard_map.78), channel_id=2, replica_groups=mesh['yh'=4,'yl'=2,'xh'=2,'zh'=6,'zl'=2,'xl'=2,'core'=2] {'xl'}, dimensions={0}, use_global_device_ids=true | all-gather | bytes 786432 | tf_op jit(solution)/shard_map/all_gather | solution.py:209
  23.5 0.2 multiply_reduce_fusion.1
  23.7 0.0 copy-done.2
  23.7 0.1 multiply_convert_fusion.1
  23.8 2.2 %all_gather.23.normed_ref = bf16[256,1024]{1,0:T(8,128)(2,1)S(1)} all-gather(bf16[128,1024]{1,0:T(8,128)(2,1)S(1)} %multiply_convert_fusion.1), channel_id=1, replica_groups=mesh['yh'=4,'yl'=2,'xh'=2,'zh'=6,'zl'=2,'xl'=2,'core'=2] {'core'}, dimensions={0}, use_global_device_ids=true | all-gather | bytes 786432 | tf_op jit(solution)/shard_map/all_gather | solution.py:212
  26.0 0.0 copy-done
  26.0 0.8 shard_map.79
  26.8 5.1 %all-gather.2 = f32[4,1,256]{2,1,0:T(1,128)S(1)} all-gather(f32[1,1,256]{2,1,0:T(1,128)S(1)} %bitcast.16), channel_id=1, replica_groups=mesh['yh'=4,'yl'=2,'xh'=2,'zh'=6,'zl'=2,'xl'=2,'core'=2] {'xl','core'}, dimensions={0}, use_global_device_ids=true | all-gather | bytes 5120 | tf_op jit(solution)/shard_map/all_gather | solution.py:217
  31.9 0.9 shard_map.81
  32.8 0.0 copy-start.1
  32.8 2.4 %collective-permute-start.1 = (bf16[128,1024]{1,0:T(8,128)(2,1)S(1)}, bf16[128,1024]{1,0:T(8,128)(2,1)S(1)}, u32[]{:S(2)}, u32[]{:S(2)}) collective-permute-start(bf16[128,1024]{1,0:T(8,128)(2,1)S(1)} %shard_map.81), channel_id=1, source_target_pairs={{0,1},{1,0},{2,3},{3,2},{4,5},{5,4},{6,7},{7,6},{8,9},{9,8},{10,11... | collective-permute-start | bytes 786440 | tf_op jit(solution)/shard_map/ppermute | solution.py:227
  35.1 1.8 %shard_map.80 = (f32[128,1024]{1,0:T(8,128)S(1)}, bf16[64,8,1024]{2,1,0:T(8,128)(2,1)S(1)}) custom-call(s32[1]{0:T(128)} %bitcast.half_ref, f32[256,512]{1,0:T(8,128)S(1)} %get-tuple-element.10.exp_ref, f32[4,256]{1,0:T(4,128)S(1)} %bitcast.11, f32[1,256]{1,0:T(1,128)S(1)} %bitcast.15, f32[1,256]{1,0:T(1,128)S(1)} %bitcast.13, ...), custom_call_target="tpu_custom_call" | custom-call | tf_op jit(solution)/shard_map/pallas_call | solution.py:221
  36.9 0.0 collective-permute-done.1.other_ref
  36.9 0.1 shard_map.82
  37.0 9.1 %all-gather.1 = bf16[256,1024]{1,0:T(8,128)(2,1)S(1)} all-gather(bf16[128,1024]{1,0:T(8,128)(2,1)S(1)} %shard_map.82), channel_id=3, replica_groups=mesh['yh'=4,'yl'=2,'xh'=2,'zh'=6,'zl'=2,'xl'=2,'core'=2] {'xl'}, dimensions={0}, use_global_device_ids=true | all-gather | bytes 786432 | tf_op jit(solution)/shard_map/all_gather | solution.py:228
  46.1 0.3 multiply_reduce_fusion
  46.3 0.2 multiply_convert_fusion
  46.6 2.2 %all_gather.27.grad_ref = bf16[256,1024]{1,0:T(8,128)(2,1)S(1)} all-gather(bf16[128,1024]{1,0:T(8,128)(2,1)S(1)} %multiply_convert_fusion), channel_id=1, replica_groups=mesh['yh'=4,'yl'=2,'xh'=2,'zh'=6,'zl'=2,'xl'=2,'core'=2] {'core'}, dimensions={0}, use_global_device_ids=true | all-gather | bytes 786432 | tf_op jit(solution)/shard_map/all_gather | solution.py:230
  48.8 0.0 copy-done.1
  48.8 0.8 shard_map.84
  49.5 42.4 %all_to_all.10.pieces_ref = bf16[8,192,1024]{2,1,0:T(8,128)(2,1)S(1)} all-to-all(bf16[8,192,1024]{2,1,0:T(8,128)(2,1)S(1)} %shard_map.84), channel_id=1, replica_groups=mesh['yh'=4,'yl'=2,'xh'=2,'zh'=6,'zl'=2,'xl'=2,'core'=2] {'xh','yl','zl'}, dimensions={0} | all-to-all | bytes 6291456 | tf_op jit(solution)/shard_map/all_to_all | solution.py:233
  91.9 1.1 shard_map.85
  93.1 14.3 %all-to-all-start.1 = ((bf16[24,8,1024]{2,1,0:T(8,128)(2,1)}), bf16[24,8,1024]{2,1,0:T(8,128)(2,1)S(1)}, u32[]{:S(2)}, u32[]{:S(2)}) async-start(bf16[24,8,1024]{2,1,0:T(8,128)(2,1)} %bitcast.5), calls=%async_computation.1 | async-start | bytes 786432 | tf_op jit(solution)/shard_map/all_to_all | solution.py:235
  107.4 3.7 %shard_map.83 = bf16[256,1024]{1,0:T(8,128)(2,1)} custom-call(bf16[256,1024]{1,0:T(8,128)(2,1)S(1)} %all_gather.27.grad_ref, bf16[1024,1024]{1,0:T(8,128)(2,1)} %b_hbm.3), custom_call_target="tpu_custom_call" | custom-call | flops 536870912 | bytes 3145728 | tf_op jit(solution)/shard_map/pallas_call | solution.py:239
  111.1 20.1 %all-to-all-done.1.pieces_ref = bf16[24,8,1024]{2,1,0:T(8,128)(2,1)S(1)} async-done(((bf16[24,8,1024]{2,1,0:T(8,128)(2,1)}), bf16[24,8,1024]{2,1,0:T(8,128)(2,1)S(1)}, u32[]{:S(2)}, u32[]{:S(2)}) %all-to-all-start.1) | async-done | bytes 393248 | tf_op jit(solution)/shard_map/all_to_all | solution.py:235
  131.2 0.7 shard_map.86
  (4 shorter events, 0.1 us)
Async XLA Ops:
  0.6 23.1 %copy-start.2 = (f32[1024]{0:T(1024)S(1)}, f32[1024]{0:T(1024)}, u32[]{:S(2)}) copy-start(f32[1024]{0:T(1024)} %param.8) | copy-start | bytes 12292
  0.6 25.4 %copy-start = (bf16[1024,512]{1,0:T(8,128)(2,1)S(1)}, bf16[1024,512]{1,0:T(8,128)(2,1)}, u32[]{:S(2)}) copy-start(bf16[1024,512]{1,0:T(8,128)(2,1)} %head_ref.5) | copy-start | bytes 3145732
  3.0 3.4 %collective-permute-start = (bf16[128,1024]{1,0:T(8,128)(2,1)S(1)}, bf16[128,1024]{1,0:T(8,128)(2,1)S(1)}, u32[]{:S(2)}, u32[]{:S(2)}) collective-permute-start(bf16[128,1024]{1,0:T(8,128)(2,1)S(1)} %get-tuple-element.9), channel_id=1, source_target_pairs={{0,1},{1,0},{2,3},{3,2},{4,5},{5,4},{6,7},{7,6},{8,9},{9,8},{10,11... | collective-permute-start | bytes 786440 | tf_op jit(solution)/shard_map/ppermute | solution.py:208
  32.8 16.0 %copy-start.1 = (bf16[256,1024]{1,0:T(8,128)(2,1)S(1)}, bf16[256,1024]{1,0:T(8,128)(2,1)}, u32[]{:S(2)}) copy-start(bf16[256,1024]{1,0:T(8,128)(2,1)} %hidden_ref.1) | copy-start | bytes 1572868
  32.8 4.1 %collective-permute-start.1 = (bf16[128,1024]{1,0:T(8,128)(2,1)S(1)}, bf16[128,1024]{1,0:T(8,128)(2,1)S(1)}, u32[]{:S(2)}, u32[]{:S(2)}) collective-permute-start(bf16[128,1024]{1,0:T(8,128)(2,1)S(1)} %shard_map.81), channel_id=1, source_target_pairs={{0,1},{1,0},{2,3},{3,2},{4,5},{5,4},{6,7},{7,6},{8,9},{9,8},{10,11... | collective-permute-start | bytes 786440 | tf_op jit(solution)/shard_map/ppermute | solution.py:227
  93.1 38.1 %all-to-all-start.1 = ((bf16[24,8,1024]{2,1,0:T(8,128)(2,1)}), bf16[24,8,1024]{2,1,0:T(8,128)(2,1)S(1)}, u32[]{:S(2)}, u32[]{:S(2)}) async-start(bf16[24,8,1024]{2,1,0:T(8,128)(2,1)} %bitcast.5), calls=%async_computation.1 | async-start | bytes 786432 | tf_op jit(solution)/shard_map/all_to_all | solution.py:235

commit v7 on v6

--- a/solution.py
+++ b/solution.py
@@ -19,6 +19,8 @@
 N_FAR = 24
 BLOCKS = 192
 PROJ_BLOCKS = 128
+LATE_BLOCKS = 144
+EARLY = ("yl", "zl")
 VMEM_BYTES = 20 << 20
 SWAP = [(0, 1), (1, 0)]
 f32 = jnp.float32
@@ -36,9 +38,9 @@
     return total
 
 
-def near_far(block):
+def place(block):
     y, x, z = block // 24, block // 12 % 2, block % 12
-    return (x * 2 + y % 2) * 2 + z % 2, z // 2 * 4 + y // 2
+    return y // 2, y % 2, x, z // 2, z % 2
 
 
 def streamed_product(half_ref, a_hbm, b_hbm, sent_ref, kept_ref, a_ref, b_ref, sems):
@@ -114,7 +116,7 @@
     out_ref[...] = dot(dlogit, head_ref[...], 1, 1).astype(out_ref.dtype)
 
 
-def kept_grad(half_ref, exp_ref, totals_ref, code_ref, mask_ref, head_ref, normed_ref, out_ref, blocks_ref):
+def kept_grad(half_ref, exp_ref, totals_ref, code_ref, mask_ref, head_ref, normed_ref, out_ref, late_ref, early_ref):
     rows = out_ref.shape[0]
     start = pl.multiple_of(half_ref[0] * rows, rows)
     dlogit = dlogit_rows(start, exp_ref, totals_ref, code_ref, mask_ref, rows)
@@ -122,31 +124,49 @@
     whole = dlogit_rows(0, exp_ref, totals_ref, code_ref, mask_ref, exp_ref.shape[0])
     grad = dot(normed_ref[...], whole, 0, 0).astype(bf16)
     part = grad.shape[1]
-    for i in range(blocks_ref.shape[0]):
-        blocks_ref[i, :, :part] = grad[16 * i : 16 * i + 8]
-        blocks_ref[i, :, part:] = grad[16 * i + 8 : 16 * i + 16]
+    for i in range(BLOCKS - PROJ_BLOCKS):
+        top, bottom = grad[16 * i : 16 * i + 8], grad[16 * i + 8 : 16 * i + 16]
+        if PROJ_BLOCKS + i < LATE_BLOCKS:
+            late_ref[i, :, :part] = top
+            late_ref[i, :, part:] = bottom
+        else:
+            _, yl, xh, zh, zl = place(PROJ_BLOCKS + i)
+            row = 8 * (xh * 6 + zh)
+            early_ref[2 * yl + zl, row : row + 8, :part] = top
+            early_ref[2 * yl + zl, row : row + 8, part:] = bottom
 
 
 def grad_blocks(hidden_ref, grad_ref, head_ref, out_ref):
     step = 16
-    for first in range(0, PROJ_BLOCKS, step):
-        part = dot(hidden_ref[:, 8 * first : 8 * (first + step)], grad_ref[...], 0, 0).astype(bf16)
+    for first in range(0, LATE_BLOCKS, step):
+        if first < PROJ_BLOCKS:
+            part = dot(hidden_ref[:, 8 * first : 8 * (first + step)], grad_ref[...], 0, 0).astype(bf16)
         for i in range(step):
-            near, far = near_far(first + i)
-            out_ref[near, 8 * far : 8 * far + 8, :] = part[8 * i : 8 * i + 8]
-    for block in range(PROJ_BLOCKS, BLOCKS):
-        near, far = near_far(block)
-        out_ref[near, 8 * far : 8 * far + 8, :] = head_ref[block - PROJ_BLOCKS]
+            yh, yl, xh, zh, zl = place(first + i)
+            row = 8 * (zh * 3 + yh)
+            block = part[8 * i : 8 * i + 8] if first < PROJ_BLOCKS else head_ref[i]
+            out_ref[(xh * 2 + yl) * 2 + zl, row : row + 8, :] = block
+
+
+def early_sum(half_ref, pieces_ref, sent_ref, kept_ref):
+    rows = sent_ref.shape[0]
+    mine = pl.ds(pl.multiple_of(half_ref[0] * rows, rows), rows)
+    other = pl.ds(pl.multiple_of((1 - half_ref[0]) * rows, rows), rows)
+    sent_ref[...] = add_up(pieces_ref.at[:, other]).astype(sent_ref.dtype)
+    kept_ref[...] = add_up(pieces_ref.at[:, mine])
 
 
 def chip_sum(kept_ref, other_ref, out_ref):
     out_ref[...] = (kept_ref[...] + other_ref[...].astype(f32)).astype(out_ref.dtype)
 
 
-def near_sum(pieces_ref, out_ref):
-    step = 16
-    for first in range(0, out_ref.shape[0], step):
-        out_ref[first : first + step] = add_up(pieces_ref.at[:, first : first + step]).astype(out_ref.dtype)
+def near_sum(pieces_ref, kept_ref, other_ref, out_ref):
+    for zh in range(6):
+        window = slice(24 * zh, 24 * zh + 24)
+        out_ref[32 * zh : 32 * zh + 24] = add_up(pieces_ref.at[:, window]).astype(out_ref.dtype)
+        window = slice(8 * zh, 8 * zh + 8)
+        early = kept_ref[window] + other_ref[window].astype(f32)
+        out_ref[32 * zh + 24 : 32 * zh + 32] = early.astype(out_ref.dtype)
 
 
 def far_sum(is_proj_ref, pieces_ref, out_ref):
@@ -218,20 +238,33 @@
 
     rest = (exp_logits, totals, code, mask, head_weight)
     sent = in_vmem(sent_grad, shape((half, width), bf16), 5, 1)(other, *rest)
-    kept, head_blocks = in_vmem(
+    exp_logits, sent = lax.optimization_barrier((exp_logits, sent))
+    rest = (exp_logits, *rest[1:])
+    kept, late_head, early = in_vmem(
         kept_grad,
-        [shape((half, width), f32), shape((BLOCKS - PROJ_BLOCKS, 8, width), bf16)],
+        [
+            shape((half, width), f32),
+            shape((LATE_BLOCKS - PROJ_BLOCKS, 8, width), bf16),
+            shape((4, 96, width), bf16),
+        ],
         6,
         1,
     )(mine, *rest, normed)
+    early = lax.all_to_all(early, EARLY, 0, 0)
     chip = in_vmem(chip_sum, shape((half, width), bf16), 2)(kept, lax.ppermute(sent, "core", SWAP))
     scaled_grad = add_up(lax.all_gather(chip, "xl")) * gain
     centred = scaled_grad - unit_rows * jnp.mean(scaled_grad * unit_rows, axis=1, keepdims=True)
     row_grad = lax.all_gather((inv_rms * centred).astype(bf16), "core", tiled=True)
 
-    blocks = in_vmem(grad_blocks, shape((N_NEAR, N_FAR * 8, width), bf16), 3)(hidden, row_grad, head_blocks)
+    blocks = in_vmem(grad_blocks, shape((N_NEAR, LATE_BLOCKS, width), bf16), 3)(hidden, row_grad, late_head)
+    early_out = [shape((48, width), bf16), shape((48, width), f32)]
+    early_sent, early_kept = in_vmem(early_sum, early_out, 1, 1)(lax.axis_index("xh").reshape(1), early)
+    blocks, early_sent = lax.optimization_barrier((blocks, early_sent))
     pieces = lax.all_to_all(blocks, NEAR, 0, 0)
-    near = in_vmem(near_sum, shape((N_FAR * 8, width), bf16), 1)(pieces)
+    early_other = lax.ppermute(early_sent, "xh", SWAP)
+    near = in_vmem(near_sum, shape((N_FAR * 8, width), bf16), 3)(
+        pieces, early_kept, early_other
+    )
     far = lax.all_to_all(near.reshape(N_FAR, 8, width), FAR, 0, 0)
     is_proj = (lax.axis_index(SEQ) < PROJ_BLOCKS).astype(jnp.int32).reshape(1)
     weight_grads = in_vmem(far_sum, shape((16, vocab_part), f32), 1, 1)(is_proj, far)

time: 132 us -> 133 us (level)
  the two profiles are of different devices: /device:TPU:2 before, /device:TPU:8 now
where the time goes in v7:
time: 133 us
  waiting for transfers between devices  49.9 us (38%)
  starting transfers between devices  39.5 us (30%)
  blocking collectives  27.6 us (21%)
  Pallas kernels  14.3 us (11%)
    ppermute x1, waiting for transfers between devices, local(): early_other = lax.ppermute(early_sent, 'xh', SWAP)  26.1 us
    all_to_all x1, waiting for transfers between devices, local(): far = lax.all_to_all(near.reshape(N_FAR, 8, width), FAR, 0, 0)  20.8 us
    all_to_all x1, starting transfers between devices, local(): far = lax.all_to_all(near.reshape(N_FAR, 8, width), FAR, 0, 0)  13.5 us
    all_to_all x1, starting transfers between devices, local(): early = lax.all_to_all(early, EARLY, 0, 0)  12.9 us
    all_gather x1, blocking collectives, local(): scaled_grad = add_up(lax.all_gather(chip, 'xl')) * gain  9.16 us
    all_gather x1, blocking collectives, local(): x = add_up(lax.all_gather(chip, 'xl'))  9.02 us
    all_gather x1, blocking collectives, local(): totals = lax.all_gather(sums, TP, tiled=True)  5.08 us
    ppermute x1, starting transfers between devices, local(): early_other = lax.ppermute(early_sent, 'xh', SWAP)  4.87 us
  transfers between devices with their start and end apart: 6, of which 4 were waited for; matrix products, arithmetic and copies ran while one was open for 0% of the time, Pallas kernels for 4%

profile of v7, /device:TPU:8, one launch (start us, length us, event | category | flops | bytes accessed | tf_op | source)
XLA Modules:
  0.0 132.9 jit_solution(4577402873618031862)
XLA Ops:
  0.6 0.0 copy-start.3
  0.6 0.0 copy-start.4
  0.7 0.0 copy-start.2
  0.7 2.3 %shard_map.77 = (bf16[128,1024]{1,0:T(8,128)(2,1)S(1)}, f32[128,1024]{1,0:T(8,128)S(1)}) custom-call(s32[1]{0:T(128)} %bitcast.half_ref, bf16[256,1024]{1,0:T(8,128)(2,1)} %hidden_ref.1, bf16[1024,1024]{1,0:T(8,128)(2,1)} %b_hbm.3), custom_call_target="tpu_custom_call" | custom-call | tf_op jit(solution)/shard_map/pallas_call | solution.py:216
  2.9 0.0 copy-start
  2.9 2.1 %collective-permute-start = (bf16[128,1024]{1,0:T(8,128)(2,1)S(1)}, bf16[128,1024]{1,0:T(8,128)(2,1)S(1)}, u32[]{:S(2)}, u32[]{:S(2)}) collective-permute-start(bf16[128,1024]{1,0:T(8,128)(2,1)S(1)} %get-tuple-element.16), channel_id=1, source_target_pairs={{0,1},{1,0},{2,3},{3,2},{4,5},{5,4},{6,7},{7,6},{8,9},{9,8},{10,11... | collective-permute-start | bytes 786440 | tf_op jit(solution)/shard_map/ppermute | solution.py:228
  5.0 0.0 copy-done.3
  5.0 0.0 copy-done.4
  5.1 1.4 %collective-permute-done.other_ref = bf16[128,1024]{1,0:T(8,128)(2,1)S(1)} collective-permute-done((bf16[128,1024]{1,0:T(8,128)(2,1)S(1)}, bf16[128,1024]{1,0:T(8,128)(2,1)S(1)}, u32[]{:S(2)}, u32[]{:S(2)}) %collective-permute-start) | collective-permute-done | bytes 262176 | tf_op jit(solution)/shard_map/ppermute | solution.py:228
  6.6 9.0 %all-gather = bf16[256,1024]{1,0:T(8,128)(2,1)S(1)} all-gather(bf16[128,1024]{1,0:T(8,128)(2,1)S(1)} %shard_map.78), channel_id=2, replica_groups=mesh['yh'=4,'yl'=2,'xh'=2,'zh'=6,'zl'=2,'xl'=2,'core'=2] {'xl'}, dimensions={0}, use_global_device_ids=true | all-gather | bytes 786432 | tf_op jit(solution)/shard_map/all_gather | solution.py:229
  15.6 0.2 multiply_reduce_fusion.1
  15.8 0.0 copy-done.2
  15.8 0.1 multiply_convert_fusion.1
  15.9 2.2 %all_gather.23.normed_ref = bf16[256,1024]{1,0:T(8,128)(2,1)S(1)} all-gather(bf16[128,1024]{1,0:T(8,128)(2,1)S(1)} %multiply_convert_fusion.1), channel_id=1, replica_groups=mesh['yh'=4,'yl'=2,'xh'=2,'zh'=6,'zl'=2,'xl'=2,'core'=2] {'core'}, dimensions={0}, use_global_device_ids=true | all-gather | bytes 786432 | tf_op jit(solution)/shard_map/all_gather | solution.py:232
  18.1 0.0 copy-done
  18.1 0.8 shard_map.79
  18.8 5.1 %all-gather.2 = f32[4,1,256]{2,1,0:T(1,128)S(1)} all-gather(f32[1,1,256]{2,1,0:T(1,128)S(1)} %bitcast.17), channel_id=1, replica_groups=mesh['yh'=4,'yl'=2,'xh'=2,'zh'=6,'zl'=2,'xl'=2,'core'=2] {'xl','core'}, dimensions={0}, use_global_device_ids=true | all-gather | bytes 5120 | tf_op jit(solution)/shard_map/all_gather | solution.py:237
  23.9 0.9 shard_map.80
  24.8 2.6 %shard_map.81 = (f32[128,1024]{1,0:T(8,128)S(1)}, bf16[16,8,1024]{2,1,0:T(8,128)(2,1)S(1)}, bf16[4,96,1024]{2,1,0:T(8,128)(2,1)}) custom-call(s32[1]{0:T(128)} %bitcast.half_ref, f32[256,512]{1,0:T(8,128)S(1)} %get-tuple-element.19.exp_ref, f32[4,256]{1,0:T(4,128)S(1)} %bitcast.12, f32[1,256]{1,0:T(1,128)S(1)} %bitcast.16, f32[1,256]{1,0:T(1,128)S(1)} %bitcast.14, ...), custom_call_target="tpu_custom_call" | custom-call | tf_op jit(solution)/shard_map/pallas_call | solution.py:243
  27.4 12.9 %all-to-all-start = ((bf16[4,96,1024]{2,1,0:T(8,128)(2,1)}), bf16[4,96,1024]{2,1,0:T(8,128)(2,1)S(1)}, u32[]{:S(2)}, u32[]{:S(2)}) async-start(bf16[4,96,1024]{2,1,0:T(8,128)(2,1)} %get-tuple-element.23), calls=%async_computation | async-start | bytes 1572864 | tf_op jit(solution)/shard_map/all_to_all | solution.py:253
  40.3 1.9 %collective-permute-start.1 = (bf16[128,1024]{1,0:T(8,128)(2,1)S(1)}, bf16[128,1024]{1,0:T(8,128)(2,1)S(1)}, u32[]{:S(2)}, u32[]{:S(2)}) collective-permute-start(bf16[128,1024]{1,0:T(8,128)(2,1)S(1)} %shard_map.80), channel_id=1, source_target_pairs={{0,1},{1,0},{2,3},{3,2},{4,5},{5,4},{6,7},{7,6},{8,9},{9,8},{10,11... | collective-permute-start | bytes 786440 | tf_op jit(solution)/shard_map/ppermute | solution.py:254
  42.3 1.5 %collective-permute-done.1.other_ref = bf16[128,1024]{1,0:T(8,128)(2,1)S(1)} collective-permute-done((bf16[128,1024]{1,0:T(8,128)(2,1)S(1)}, bf16[128,1024]{1,0:T(8,128)(2,1)S(1)}, u32[]{:S(2)}, u32[]{:S(2)}) %collective-permute-start.1) | collective-permute-done | bytes 262176 | tf_op jit(solution)/shard_map/ppermute | solution.py:254
  43.8 0.0 copy-start.1
  43.8 9.2 %all-gather.1 = bf16[256,1024]{1,0:T(8,128)(2,1)S(1)} all-gather(bf16[128,1024]{1,0:T(8,128)(2,1)S(1)} %shard_map.82), channel_id=3, replica_groups=mesh['yh'=4,'yl'=2,'xh'=2,'zh'=6,'zl'=2,'xl'=2,'core'=2] {'xl'}, dimensions={0}, use_global_device_ids=true | all-gather | bytes 786432 | tf_op jit(solution)/shard_map/all_gather | solution.py:255
  53.0 0.3 multiply_reduce_fusion
  53.2 0.2 multiply_convert_fusion
  53.5 2.2 %all_gather.27.grad_ref = bf16[256,1024]{1,0:T(8,128)(2,1)S(1)} all-gather(bf16[128,1024]{1,0:T(8,128)(2,1)S(1)} %multiply_convert_fusion), channel_id=1, replica_groups=mesh['yh'=4,'yl'=2,'xh'=2,'zh'=6,'zl'=2,'xl'=2,'core'=2] {'core'}, dimensions={0}, use_global_device_ids=true | all-gather | bytes 786432 | tf_op jit(solution)/shard_map/all_gather | solution.py:257
  55.7 0.0 copy-done.1
  55.7 2.2 %shard_map.84 = bf16[8,144,1024]{2,1,0:T(8,128)(2,1)} custom-call(bf16[256,1024]{1,0:T(8,128)(2,1)S(1)} %copy-done.1, bf16[256,1024]{1,0:T(8,128)(2,1)S(1)} %all_gather.27.grad_ref, bf16[16,8,1024]{2,1,0:T(8,128)(2,1)S(1)} %get-tuple-element.22.head_ref), custom_call_target="tpu_custom_call" | custom-call | tf_op jit(solution)/shard_map/pallas_call | solution.py:259
  57.8 0.0 all-to-all-done.pieces_ref
  57.8 0.1 shard_map.85
  57.9 4.2 %all-to-all-start.1 = ((bf16[8,144,1024]{2,1,0:T(8,128)(2,1)}), bf16[8,144,1024]{2,1,0:T(8,128)(2,1)S(1)}, u32[]{:S(2)}, u32[]{:S(2)}) async-start(bf16[8,144,1024]{2,1,0:T(8,128)(2,1)} %shard_map.84), calls=%async_computation.1 | async-start | bytes 4718592 | tf_op jit(solution)/shard_map/all_to_all | solution.py:263
  62.1 4.9 %collective-permute-start.2 = (bf16[48,1024]{1,0:T(8,128)(2,1)S(1)}, bf16[48,1024]{1,0:T(8,128)(2,1)S(1)}, u32[]{:S(2)}, u32[]{:S(2)}) collective-permute-start(bf16[48,1024]{1,0:T(8,128)(2,1)S(1)} %get-tuple-element.27), channel_id=1, source_target_pairs={{0,48},{48,0},{1,49},{49,1},{2,50},{50,2},{3,51},{51,3},{4,52},{52... | collective-permute-start | bytes 294920 | tf_op jit(solution)/shard_map/ppermute | solution.py:264
  67.0 26.1 %collective-permute-done.2.other_ref = bf16[48,1024]{1,0:T(8,128)(2,1)S(1)} collective-permute-done((bf16[48,1024]{1,0:T(8,128)(2,1)S(1)}, bf16[48,1024]{1,0:T(8,128)(2,1)S(1)}, u32[]{:S(2)}, u32[]{:S(2)}) %collective-permute-start.2) | collective-permute-done | bytes 98336 | tf_op jit(solution)/shard_map/ppermute | solution.py:264
  93.1 0.0 all-to-all-done.1.pieces_ref
  93.1 1.1 shard_map.86
  94.2 13.5 %all-to-all-start.2 = ((bf16[24,8,1024]{2,1,0:T(8,128)(2,1)}), bf16[24,8,1024]{2,1,0:T(8,128)(2,1)S(1)}, u32[]{:S(2)}, u32[]{:S(2)}) async-start(bf16[24,8,1024]{2,1,0:T(8,128)(2,1)} %bitcast.6), calls=%async_computation.2 | async-start | bytes 786432 | tf_op jit(solution)/shard_map/all_to_all | solution.py:268
  107.7 3.7 %shard_map.83 = bf16[256,1024]{1,0:T(8,128)(2,1)} custom-call(bf16[256,1024]{1,0:T(8,128)(2,1)S(1)} %all_gather.27.grad_ref, bf16[1024,1024]{1,0:T(8,128)(2,1)} %b_hbm.3), custom_call_target="tpu_custom_call" | custom-call | flops 536870912 | bytes 3145728 | tf_op jit(solution)/shard_map/pallas_call | solution.py:272
  111.4 20.8 %all-to-all-done.2.pieces_ref = bf16[24,8,1024]{2,1,0:T(8,128)(2,1)S(1)} async-done(((bf16[24,8,1024]{2,1,0:T(8,128)(2,1)}), bf16[24,8,1024]{2,1,0:T(8,128)(2,1)S(1)}, u32[]{:S(2)}, u32[]{:S(2)}) %all-to-all-start.2) | async-done | bytes 393248 | tf_op jit(solution)/shard_map/all_to_all | solution.py:268
  132.2 0.7 shard_map.87
  (7 shorter events, 0.1 us)
Async XLA Ops:
  0.6 4.4 %copy-start.3 = (s32[256]{0:T(256)S(1)}, s32[256]{0:T(256)}, u32[]{:S(2)}) copy-start(s32[256]{0:T(256)} %param.11) | copy-start | bytes 3076
  0.6 4.4 %copy-start.4 = (s32[256]{0:T(256)S(1)}, s32[256]{0:T(256)}, u32[]{:S(2)}) copy-start(s32[256]{0:T(256)} %param.10) | copy-start | bytes 3076
  0.7 15.1 %copy-start.2 = (f32[1024]{0:T(1024)S(1)}, f32[1024]{0:T(1024)}, u32[]{:S(2)}) copy-start(f32[1024]{0:T(1024)} %param.8) | copy-start | bytes 12292
  2.9 15.1 %copy-start = (bf16[1024,512]{1,0:T(8,128)(2,1)S(1)}, bf16[1024,512]{1,0:T(8,128)(2,1)}, u32[]{:S(2)}) copy-start(bf16[1024,512]{1,0:T(8,128)(2,1)} %head_ref.5) | copy-start | bytes 3145732
  2.9 3.6 %collective-permute-start = (bf16[128,1024]{1,0:T(8,128)(2,1)S(1)}, bf16[128,1024]{1,0:T(8,128)(2,1)S(1)}, u32[]{:S(2)}, u32[]{:S(2)}) collective-permute-start(bf16[128,1024]{1,0:T(8,128)(2,1)S(1)} %get-tuple-element.16), channel_id=1, source_target_pairs={{0,1},{1,0},{2,3},{3,2},{4,5},{5,4},{6,7},{7,6},{8,9},{9,8},{10,11... | collective-permute-start | bytes 786440 | tf_op jit(solution)/shard_map/ppermute | solution.py:228
  27.4 30.4 %all-to-all-start = ((bf16[4,96,1024]{2,1,0:T(8,128)(2,1)}), bf16[4,96,1024]{2,1,0:T(8,128)(2,1)S(1)}, u32[]{:S(2)}, u32[]{:S(2)}) async-start(bf16[4,96,1024]{2,1,0:T(8,128)(2,1)} %get-tuple-element.23), calls=%async_computation | async-start | bytes 1572864 | tf_op jit(solution)/shard_map/all_to_all | solution.py:253
  40.3 3.4 %collective-permute-start.1 = (bf16[128,1024]{1,0:T(8,128)(2,1)S(1)}, bf16[128,1024]{1,0:T(8,128)(2,1)S(1)}, u32[]{:S(2)}, u32[]{:S(2)}) collective-permute-start(bf16[128,1024]{1,0:T(8,128)(2,1)S(1)} %shard_map.80), channel_id=1, source_target_pairs={{0,1},{1,0},{2,3},{3,2},{4,5},{5,4},{6,7},{7,6},{8,9},{9,8},{10,11... | collective-permute-start | bytes 786440 | tf_op jit(solution)/shard_map/ppermute | solution.py:254
  43.8 11.9 %copy-start.1 = (bf16[256,1024]{1,0:T(8,128)(2,1)S(1)}, bf16[256,1024]{1,0:T(8,128)(2,1)}, u32[]{:S(2)}) copy-start(bf16[256,1024]{1,0:T(8,128)(2,1)} %hidden_ref.1) | copy-start | bytes 1572868
  57.9 35.2 %all-to-all-start.1 = ((bf16[8,144,1024]{2,1,0:T(8,128)(2,1)}), bf16[8,144,1024]{2,1,0:T(8,128)(2,1)S(1)}, u32[]{:S(2)}, u32[]{:S(2)}) async-start(bf16[8,144,1024]{2,1,0:T(8,128)(2,1)} %shard_map.84), calls=%async_computation.1 | async-start | bytes 4718592 | tf_op jit(solution)/shard_map/all_to_all | solution.py:263
  62.1 31.0 %collective-permute-start.2 = (bf16[48,1024]{1,0:T(8,128)(2,1)S(1)}, bf16[48,1024]{1,0:T(8,128)(2,1)S(1)}, u32[]{:S(2)}, u32[]{:S(2)}) collective-permute-start(bf16[48,1024]{1,0:T(8,128)(2,1)S(1)} %get-tuple-element.27), channel_id=1, source_target_pairs={{0,48},{48,0},{1,49},{49,1},{2,50},{50,2},{3,51},{51,3},{4,52},{52... | collective-permute-start | bytes 294920 | tf_op jit(solution)/shard_map/ppermute | solution.py:264
  94.2 38.0 %all-to-all-start.2 = ((bf16[24,8,1024]{2,1,0:T(8,128)(2,1)}), bf16[24,8,1024]{2,1,0:T(8,128)(2,1)S(1)}, u32[]{:S(2)}, u32[]{:S(2)}) async-start(bf16[24,8,1024]{2,1,0:T(8,128)(2,1)} %bitcast.6), calls=%async_computation.2 | async-start | bytes 786432 | tf_op jit(solution)/shard_map/all_to_all | solution.py:268

commit v8 on v7

--- a/solution.py
+++ b/solution.py
@@ -250,8 +250,9 @@
         6,
         1,
     )(mine, *rest, normed)
+    early, swapped = lax.optimization_barrier((early, lax.ppermute(sent, "core", SWAP)))
     early = lax.all_to_all(early, EARLY, 0, 0)
-    chip = in_vmem(chip_sum, shape((half, width), bf16), 2)(kept, lax.ppermute(sent, "core", SWAP))
+    chip = in_vmem(chip_sum, shape((half, width), bf16), 2)(kept, swapped)
     scaled_grad = add_up(lax.all_gather(chip, "xl")) * gain
     centred = scaled_grad - unit_rows * jnp.mean(scaled_grad * unit_rows, axis=1, keepdims=True)
     row_grad = lax.all_gather((inv_rms * centred).astype(bf16), "core", tiled=True)

time: 133 us -> 132 us (level)
  waiting for transfers between devices: 49.9 us -> 48.4 us
    ppermute x2, waiting for transfers between devices: 2.92 us -> 1.45 us  [local(): lax.ppermute(sent, 'core', SWAP)]
  transfers between devices with their start and end apart: 6 -> 6, of which waited for: 4 -> 3; matrix products, arithmetic and copies ran while one was open for 0% -> 0% of each run, Pallas kernels for 4% -> 6%
where the time goes in v8:
time: 132 us
  waiting for transfers between devices  48.4 us (37%)
  starting transfers between devices  39.7 us (30%)
  blocking collectives  27.4 us (21%)
  Pallas kernels  14.3 us (11%)
    ppermute x1, waiting for transfers between devices, local(): early_other = lax.ppermute(early_sent, 'xh', SWAP)  26.1 us
    all_to_all x1, waiting for transfers between devices, local(): far = lax.all_to_all(near.reshape(N_FAR, 8, width), FAR, 0, 0)  20.9 us
    all_to_all x1, starting transfers between devices, local(): far = lax.all_to_all(near.reshape(N_FAR, 8, width), FAR, 0, 0)  13.5 us
    all_to_all x1, starting transfers between devices, local(): early = lax.all_to_all(early, EARLY, 0, 0)  12.9 us
    all_gather x1, blocking collectives, local(): x = add_up(lax.all_gather(chip, 'xl'))  9.02 us
    all_gather x1, blocking collectives, local(): scaled_grad = add_up(lax.all_gather(chip, 'xl')) * gain  8.94 us
    all_gather x1, blocking collectives, local(): totals = lax.all_gather(sums, TP, tiled=True)  5.08 us
    ppermute x1, starting transfers between devices, local(): early_other = lax.ppermute(early_sent, 'xh', SWAP)  4.87 us
  transfers between devices with their start and end apart: 6, of which 3 were waited for; matrix products, arithmetic and copies ran while one was open for 0% of the time, Pallas kernels for 6%

profile of v8, /device:TPU:8, one launch (start us, length us, event | category | flops | bytes accessed | tf_op | source)
XLA Modules:
  0.0 131.6 jit_solution(3675408169323886615)
XLA Ops:
  0.6 0.0 copy-start.3
  0.6 0.0 copy-start.4
  0.7 0.0 copy-start.2
  0.7 2.3 %shard_map.77 = (bf16[128,1024]{1,0:T(8,128)(2,1)S(1)}, f32[128,1024]{1,0:T(8,128)S(1)}) custom-call(s32[1]{0:T(128)} %bitcast.half_ref, bf16[256,1024]{1,0:T(8,128)(2,1)} %hidden_ref.1, bf16[1024,1024]{1,0:T(8,128)(2,1)} %b_hbm.3), custom_call_target="tpu_custom_call" | custom-call | tf_op jit(solution)/shard_map/pallas_call | solution.py:216
  2.9 0.0 copy-start
  2.9 2.1 %collective-permute-start = (bf16[128,1024]{1,0:T(8,128)(2,1)S(1)}, bf16[128,1024]{1,0:T(8,128)(2,1)S(1)}, u32[]{:S(2)}, u32[]{:S(2)}) collective-permute-start(bf16[128,1024]{1,0:T(8,128)(2,1)S(1)} %get-tuple-element.18), channel_id=1, source_target_pairs={{0,1},{1,0},{2,3},{3,2},{4,5},{5,4},{6,7},{7,6},{8,9},{9,8},{10,11... | collective-permute-start | bytes 786440 | tf_op jit(solution)/shard_map/ppermute | solution.py:228
  5.0 0.0 copy-done.3
  5.0 0.0 copy-done.4
  5.1 1.4 %collective-permute-done.other_ref = bf16[128,1024]{1,0:T(8,128)(2,1)S(1)} collective-permute-done((bf16[128,1024]{1,0:T(8,128)(2,1)S(1)}, bf16[128,1024]{1,0:T(8,128)(2,1)S(1)}, u32[]{:S(2)}, u32[]{:S(2)}) %collective-permute-start) | collective-permute-done | bytes 262176 | tf_op jit(solution)/shard_map/ppermute | solution.py:228
  6.6 9.0 %all-gather = bf16[256,1024]{1,0:T(8,128)(2,1)S(1)} all-gather(bf16[128,1024]{1,0:T(8,128)(2,1)S(1)} %shard_map.78), channel_id=2, replica_groups=mesh['yh'=4,'yl'=2,'xh'=2,'zh'=6,'zl'=2,'xl'=2,'core'=2] {'xl'}, dimensions={0}, use_global_device_ids=true | all-gather | bytes 786432 | tf_op jit(solution)/shard_map/all_gather | solution.py:229
  15.6 0.2 multiply_reduce_fusion.1
  15.8 0.0 copy-done.2
  15.8 0.1 multiply_convert_fusion.1
  15.9 2.2 %all_gather.23.normed_ref = bf16[256,1024]{1,0:T(8,128)(2,1)S(1)} all-gather(bf16[128,1024]{1,0:T(8,128)(2,1)S(1)} %multiply_convert_fusion.1), channel_id=1, replica_groups=mesh['yh'=4,'yl'=2,'xh'=2,'zh'=6,'zl'=2,'xl'=2,'core'=2] {'core'}, dimensions={0}, use_global_device_ids=true | all-gather | bytes 786432 | tf_op jit(solution)/shard_map/all_gather | solution.py:232
  18.1 0.0 copy-done
  18.1 0.8 shard_map.79
  18.8 5.1 %all-gather.2 = f32[4,1,256]{2,1,0:T(1,128)S(1)} all-gather(f32[1,1,256]{2,1,0:T(1,128)S(1)} %bitcast.17), channel_id=1, replica_groups=mesh['yh'=4,'yl'=2,'xh'=2,'zh'=6,'zl'=2,'xl'=2,'core'=2] {'xl','core'}, dimensions={0}, use_global_device_ids=true | all-gather | bytes 5120 | tf_op jit(solution)/shard_map/all_gather | solution.py:237
  23.9 0.9 shard_map.80
  24.8 2.2 %collective-permute-start.1 = (bf16[128,1024]{1,0:T(8,128)(2,1)S(1)}, bf16[128,1024]{1,0:T(8,128)(2,1)S(1)}, u32[]{:S(2)}, u32[]{:S(2)}) collective-permute-start(bf16[128,1024]{1,0:T(8,128)(2,1)S(1)} %shard_map.80), channel_id=1, source_target_pairs={{0,1},{1,0},{2,3},{3,2},{4,5},{5,4},{6,7},{7,6},{8,9},{9,8},{10,11... | collective-permute-start | bytes 786440 | tf_op jit(solution)/shard_map/ppermute | solution.py:253
  27.0 2.6 %shard_map.81 = (f32[128,1024]{1,0:T(8,128)S(1)}, bf16[16,8,1024]{2,1,0:T(8,128)(2,1)S(1)}, bf16[4,96,1024]{2,1,0:T(8,128)(2,1)}) custom-call(s32[1]{0:T(128)} %bitcast.half_ref, f32[256,512]{1,0:T(8,128)S(1)} %get-tuple-element.21.exp_ref, f32[4,256]{1,0:T(4,128)S(1)} %bitcast.12, f32[1,256]{1,0:T(1,128)S(1)} %bitcast.16, f32[1,256]{1,0:T(1,128)S(1)} %bitcast.14, ...), custom_call_target="tpu_custom_call" | custom-call | tf_op jit(solution)/shard_map/pallas_call | solution.py:243
  29.6 0.0 collective-permute-done.1.other_ref
  29.6 12.9 %all-to-all-start = ((bf16[4,96,1024]{2,1,0:T(8,128)(2,1)}), bf16[4,96,1024]{2,1,0:T(8,128)(2,1)S(1)}, u32[]{:S(2)}, u32[]{:S(2)}) async-start(bf16[4,96,1024]{2,1,0:T(8,128)(2,1)} %get-tuple-element.27), calls=%async_computation | async-start | bytes 1572864 | tf_op jit(solution)/shard_map/all_to_all | solution.py:254
  42.6 0.0 copy-start.1
  42.6 8.9 %all-gather.1 = bf16[256,1024]{1,0:T(8,128)(2,1)S(1)} all-gather(bf16[128,1024]{1,0:T(8,128)(2,1)S(1)} %shard_map.82), channel_id=3, replica_groups=mesh['yh'=4,'yl'=2,'xh'=2,'zh'=6,'zl'=2,'xl'=2,'core'=2] {'xl'}, dimensions={0}, use_global_device_ids=true | all-gather | bytes 786432 | tf_op jit(solution)/shard_map/all_gather | solution.py:256
  51.6 0.3 multiply_reduce_fusion
  51.8 0.2 multiply_convert_fusion
  52.1 2.2 %all_gather.27.grad_ref = bf16[256,1024]{1,0:T(8,128)(2,1)S(1)} all-gather(bf16[128,1024]{1,0:T(8,128)(2,1)S(1)} %multiply_convert_fusion), channel_id=1, replica_groups=mesh['yh'=4,'yl'=2,'xh'=2,'zh'=6,'zl'=2,'xl'=2,'core'=2] {'core'}, dimensions={0}, use_global_device_ids=true | all-gather | bytes 786432 | tf_op jit(solution)/shard_map/all_gather | solution.py:258
  54.3 0.0 copy-done.1
  54.3 2.2 %shard_map.84 = bf16[8,144,1024]{2,1,0:T(8,128)(2,1)} custom-call(bf16[256,1024]{1,0:T(8,128)(2,1)S(1)} %copy-done.1, bf16[256,1024]{1,0:T(8,128)(2,1)S(1)} %all_gather.27.grad_ref, bf16[16,8,1024]{2,1,0:T(8,128)(2,1)S(1)} %get-tuple-element.26.head_ref), custom_call_target="tpu_custom_call" | custom-call | tf_op jit(solution)/shard_map/pallas_call | solution.py:260
  56.4 0.0 all-to-all-done.pieces_ref
  56.5 0.1 shard_map.85
  56.5 4.2 %all-to-all-start.1 = ((bf16[8,144,1024]{2,1,0:T(8,128)(2,1)}), bf16[8,144,1024]{2,1,0:T(8,128)(2,1)S(1)}, u32[]{:S(2)}, u32[]{:S(2)}) async-start(bf16[8,144,1024]{2,1,0:T(8,128)(2,1)} %shard_map.84), calls=%async_computation.1 | async-start | bytes 4718592 | tf_op jit(solution)/shard_map/all_to_all | solution.py:264
  60.8 4.9 %collective-permute-start.2 = (bf16[48,1024]{1,0:T(8,128)(2,1)S(1)}, bf16[48,1024]{1,0:T(8,128)(2,1)S(1)}, u32[]{:S(2)}, u32[]{:S(2)}) collective-permute-start(bf16[48,1024]{1,0:T(8,128)(2,1)S(1)} %get-tuple-element.31), channel_id=1, source_target_pairs={{0,48},{48,0},{1,49},{49,1},{2,50},{50,2},{3,51},{51,3},{4,52},{52... | collective-permute-start | bytes 294920 | tf_op jit(solution)/shard_map/ppermute | solution.py:265
  65.6 26.1 %collective-permute-done.2.other_ref = bf16[48,1024]{1,0:T(8,128)(2,1)S(1)} collective-permute-done((bf16[48,1024]{1,0:T(8,128)(2,1)S(1)}, bf16[48,1024]{1,0:T(8,128)(2,1)S(1)}, u32[]{:S(2)}, u32[]{:S(2)}) %collective-permute-start.2) | collective-permute-done | bytes 98336 | tf_op jit(solution)/shard_map/ppermute | solution.py:265
  91.8 0.0 all-to-all-done.1.pieces_ref
  91.8 1.1 shard_map.86
  92.8 13.5 %all-to-all-start.2 = ((bf16[24,8,1024]{2,1,0:T(8,128)(2,1)}), bf16[24,8,1024]{2,1,0:T(8,128)(2,1)S(1)}, u32[]{:S(2)}, u32[]{:S(2)}) async-start(bf16[24,8,1024]{2,1,0:T(8,128)(2,1)} %bitcast.6), calls=%async_computation.2 | async-start | bytes 786432 | tf_op jit(solution)/shard_map/all_to_all | solution.py:269
  106.3 3.7 %shard_map.83 = bf16[256,1024]{1,0:T(8,128)(2,1)} custom-call(bf16[256,1024]{1,0:T(8,128)(2,1)S(1)} %all_gather.27.grad_ref, bf16[1024,1024]{1,0:T(8,128)(2,1)} %b_hbm.3), custom_call_target="tpu_custom_call" | custom-call | flops 536870912 | bytes 3145728 | tf_op jit(solution)/shard_map/pallas_call | solution.py:273
  110.0 20.9 %all-to-all-done.2.pieces_ref = bf16[24,8,1024]{2,1,0:T(8,128)(2,1)S(1)} async-done(((bf16[24,8,1024]{2,1,0:T(8,128)(2,1)}), bf16[24,8,1024]{2,1,0:T(8,128)(2,1)S(1)}, u32[]{:S(2)}, u32[]{:S(2)}) %all-to-all-start.2) | async-done | bytes 393248 | tf_op jit(solution)/shard_map/all_to_all | solution.py:269
  130.9 0.7 shard_map.87
  (7 shorter events, 0.1 us)
Async XLA Ops:
  0.6 4.4 %copy-start.3 = (s32[256]{0:T(256)S(1)}, s32[256]{0:T(256)}, u32[]{:S(2)}) copy-start(s32[256]{0:T(256)} %param.11) | copy-start | bytes 3076
  0.6 4.4 %copy-start.4 = (s32[256]{0:T(256)S(1)}, s32[256]{0:T(256)}, u32[]{:S(2)}) copy-start(s32[256]{0:T(256)} %param.10) | copy-start | bytes 3076
  0.7 15.1 %copy-start.2 = (f32[1024]{0:T(1024)S(1)}, f32[1024]{0:T(1024)}, u32[]{:S(2)}) copy-start(f32[1024]{0:T(1024)} %param.8) | copy-start | bytes 12292
  2.9 15.1 %copy-start = (bf16[1024,512]{1,0:T(8,128)(2,1)S(1)}, bf16[1024,512]{1,0:T(8,128)(2,1)}, u32[]{:S(2)}) copy-start(bf16[1024,512]{1,0:T(8,128)(2,1)} %head_ref.5) | copy-start | bytes 3145732
  2.9 3.6 %collective-permute-start = (bf16[128,1024]{1,0:T(8,128)(2,1)S(1)}, bf16[128,1024]{1,0:T(8,128)(2,1)S(1)}, u32[]{:S(2)}, u32[]{:S(2)}) collective-permute-start(bf16[128,1024]{1,0:T(8,128)(2,1)S(1)} %get-tuple-element.18), channel_id=1, source_target_pairs={{0,1},{1,0},{2,3},{3,2},{4,5},{5,4},{6,7},{7,6},{8,9},{9,8},{10,11... | collective-permute-start | bytes 786440 | tf_op jit(solution)/shard_map/ppermute | solution.py:228
  24.8 4.8 %collective-permute-start.1 = (bf16[128,1024]{1,0:T(8,128)(2,1)S(1)}, bf16[128,1024]{1,0:T(8,128)(2,1)S(1)}, u32[]{:S(2)}, u32[]{:S(2)}) collective-permute-start(bf16[128,1024]{1,0:T(8,128)(2,1)S(1)} %shard_map.80), channel_id=1, source_target_pairs={{0,1},{1,0},{2,3},{3,2},{4,5},{5,4},{6,7},{7,6},{8,9},{9,8},{10,11... | collective-permute-start | bytes 786440 | tf_op jit(solution)/shard_map/ppermute | solution.py:253
  29.6 26.8 %all-to-all-start = ((bf16[4,96,1024]{2,1,0:T(8,128)(2,1)}), bf16[4,96,1024]{2,1,0:T(8,128)(2,1)S(1)}, u32[]{:S(2)}, u32[]{:S(2)}) async-start(bf16[4,96,1024]{2,1,0:T(8,128)(2,1)} %get-tuple-element.27), calls=%async_computation | async-start | bytes 1572864 | tf_op jit(solution)/shard_map/all_to_all | solution.py:254
  42.6 11.7 %copy-start.1 = (bf16[256,1024]{1,0:T(8,128)(2,1)S(1)}, bf16[256,1024]{1,0:T(8,128)(2,1)}, u32[]{:S(2)}) copy-start(bf16[256,1024]{1,0:T(8,128)(2,1)} %hidden_ref.1) | copy-start | bytes 1572868
  56.5 35.2 %all-to-all-start.1 = ((bf16[8,144,1024]{2,1,0:T(8,128)(2,1)}), bf16[8,144,1024]{2,1,0:T(8,128)(2,1)S(1)}, u32[]{:S(2)}, u32[]{:S(2)}) async-start(bf16[8,144,1024]{2,1,0:T(8,128)(2,1)} %shard_map.84), calls=%async_computation.1 | async-start | bytes 4718592 | tf_op jit(solution)/shard_map/all_to_all | solution.py:264
  60.8 31.0 %collective-permute-start.2 = (bf16[48,1024]{1,0:T(8,128)(2,1)S(1)}, bf16[48,1024]{1,0:T(8,128)(2,1)S(1)}, u32[]{:S(2)}, u32[]{:S(2)}) collective-permute-start(bf16[48,1024]{1,0:T(8,128)(2,1)S(1)} %get-tuple-element.31), channel_id=1, source_target_pairs={{0,48},{48,0},{1,49},{49,1},{2,50},{50,2},{3,51},{51,3},{4,52},{52... | collective-permute-start | bytes 294920 | tf_op jit(solution)/shard_map/ppermute | solution.py:265
  92.8 38.1 %all-to-all-start.2 = ((bf16[24,8,1024]{2,1,0:T(8,128)(2,1)}), bf16[24,8,1024]{2,1,0:T(8,128)(2,1)S(1)}, u32[]{:S(2)}, u32[]{:S(2)}) async-start(bf16[24,8,1024]{2,1,0:T(8,128)(2,1)} %bitcast.6), calls=%async_computation.2 | async-start | bytes 786432 | tf_op jit(solution)/shard_map/all_to_all | solution.py:269

commit v9 on v8

--- a/solution.py
+++ b/solution.py
@@ -116,13 +116,19 @@
     out_ref[...] = dot(dlogit, head_ref[...], 1, 1).astype(out_ref.dtype)
 
 
-def kept_grad(half_ref, exp_ref, totals_ref, code_ref, mask_ref, head_ref, normed_ref, out_ref, late_ref, early_ref):
-    rows = out_ref.shape[0]
-    start = pl.multiple_of(half_ref[0] * rows, rows)
-    dlogit = dlogit_rows(start, exp_ref, totals_ref, code_ref, mask_ref, rows)
-    out_ref[...] = dot(dlogit, head_ref[...], 1, 1)
-    whole = dlogit_rows(0, exp_ref, totals_ref, code_ref, mask_ref, exp_ref.shape[0])
-    grad = dot(normed_ref[...], whole, 0, 0).astype(bf16)
+def copy_out(source_ref, target_hbm, sems):
+    copies = [pltpu.make_async_copy(source_ref.at[i], target_hbm.at[i], sems.at[i]) for i in range(source_ref.shape[0])]
+    for copy in copies:
+        copy.start()
+    return copies
+
+
+def kept_grad(
+    half_ref, exp_ref, totals_ref, code_ref, mask_ref, head_ref, normed_ref,
+    out_ref, late_ref, early_hbm, dlogit_ref, early_ref, sems,
+):
+    dlogit_ref[...] = dlogit_rows(0, exp_ref, totals_ref, code_ref, mask_ref, exp_ref.shape[0])
+    grad = dot(normed_ref[...], dlogit_ref[...], 0, 0).astype(bf16)
     part = grad.shape[1]
     for i in range(BLOCKS - PROJ_BLOCKS):
         top, bottom = grad[16 * i : 16 * i + 8], grad[16 * i + 8 : 16 * i + 16]
@@ -134,9 +140,15 @@
             row = 8 * (xh * 6 + zh)
             early_ref[2 * yl + zl, row : row + 8, :part] = top
             early_ref[2 * yl + zl, row : row + 8, part:] = bottom
-
-
-def grad_blocks(hidden_ref, grad_ref, head_ref, out_ref):
+    copies = copy_out(early_ref, early_hbm, sems)
+    rows = out_ref.shape[0]
+    start = pl.multiple_of(half_ref[0] * rows, rows)
+    out_ref[...] = dot(dlogit_ref[pl.ds(start, rows), :], head_ref[...], 1, 1)
+    for copy in copies:
+        copy.wait()
+
+
+def grad_blocks(hidden_ref, grad_ref, head_ref, out_hbm, out_ref, sems):
     step = 16
     for first in range(0, LATE_BLOCKS, step):
         if first < PROJ_BLOCKS:
@@ -146,6 +158,8 @@
             row = 8 * (zh * 3 + yh)
             block = part[8 * i : 8 * i + 8] if first < PROJ_BLOCKS else head_ref[i]
             out_ref[(xh * 2 + yl) * 2 + zl, row : row + 8, :] = block
+    for copy in copy_out(out_ref, out_hbm, sems):
+        copy.wait()
 
 
 def early_sum(half_ref, pieces_ref, sent_ref, kept_ref):
@@ -240,15 +254,23 @@
     sent = in_vmem(sent_grad, shape((half, width), bf16), 5, 1)(other, *rest)
     exp_logits, sent = lax.optimization_barrier((exp_logits, sent))
     rest = (exp_logits, *rest[1:])
-    kept, late_head, early = in_vmem(
+    vmem = pl.BlockSpec(memory_space=pltpu.VMEM)
+    hbm = pl.BlockSpec(memory_space=pltpu.HBM)
+    kept, late_head, early = pl.pallas_call(
         kept_grad,
-        [
+        out_shape=[
             shape((half, width), f32),
             shape((LATE_BLOCKS - PROJ_BLOCKS, 8, width), bf16),
             shape((4, 96, width), bf16),
         ],
-        6,
-        1,
+        in_specs=[pl.BlockSpec(memory_space=pltpu.SMEM)] + [vmem] * 6,
+        out_specs=[vmem, vmem, hbm],
+        scratch_shapes=[
+            pltpu.VMEM((frames, vocab_part), bf16),
+            pltpu.VMEM((4, 96, width), bf16),
+            pltpu.SemaphoreType.DMA((4,)),
+        ],
+        compiler_params=pltpu.CompilerParams(vmem_limit_bytes=VMEM_BYTES),
     )(mine, *rest, normed)
     early, swapped = lax.optimization_barrier((early, lax.ppermute(sent, "core", SWAP)))
     early = lax.all_to_all(early, EARLY, 0, 0)
@@ -257,7 +279,17 @@
     centred = scaled_grad - unit_rows * jnp.mean(scaled_grad * unit_rows, axis=1, keepdims=True)
     row_grad = lax.all_gather((inv_rms * centred).astype(bf16), "core", tiled=True)
 
-    blocks = in_vmem(grad_blocks, shape((N_NEAR, LATE_BLOCKS, width), bf16), 3)(hidden, row_grad, late_head)
+    blocks = pl.pallas_call(
+        grad_blocks,
+        out_shape=shape((N_NEAR, LATE_BLOCKS, width), bf16),
+        in_specs=[vmem] * 3,
+        out_specs=hbm,
+        scratch_shapes=[
+            pltpu.VMEM((N_NEAR, LATE_BLOCKS, width), bf16),
+            pltpu.SemaphoreType.DMA((N_NEAR,)),
+        ],
+        compiler_params=pltpu.CompilerParams(vmem_limit_bytes=VMEM_BYTES),
+    )(hidden, row_grad, late_head)
     early_out = [shape((48, width), bf16), shape((48, width), f32)]
     early_sent, early_kept = in_vmem(early_sum, early_out, 1, 1)(lax.axis_index("xh").reshape(1), early)
     blocks, early_sent = lax.optimization_barrier((blocks, early_sent))

time: 132 us -> 132 us (level)
  no operation moved by 1% of the time
where the time goes in v9:
time: 132 us; the launch traced here: 131 us
  waiting for transfers between devices  48.4 us (37%)
  starting transfers between devices  39.8 us (30%)
  blocking collectives  27.4 us (21%)
  Pallas kernels  13.9 us (11%)
    ppermute x1, waiting for transfers between devices, local(): early_other = lax.ppermute(early_sent, 'xh', SWAP)  26.1 us
    all_to_all x1, waiting for transfers between devices, local(): far = lax.all_to_all(near.reshape(N_FAR, 8, width), FAR, 0, 0)  20.8 us
    all_to_all x1, starting transfers between devices, local(): far = lax.all_to_all(near.reshape(N_FAR, 8, width), FAR, 0, 0)  13.5 us
    all_to_all x1, starting transfers between devices, local(): early = lax.all_to_all(early, EARLY, 0, 0)  12.9 us
    all_gather x1, blocking collectives, local(): x = add_up(lax.all_gather(chip, 'xl'))  9.02 us
    all_gather x1, blocking collectives, local(): scaled_grad = add_up(lax.all_gather(chip, 'xl')) * gain  8.93 us
    all_gather x1, blocking collectives, local(): totals = lax.all_gather(sums, TP, tiled=True)  5.08 us
    ppermute x1, starting transfers between devices, local(): early_other = lax.ppermute(early_sent, 'xh', SWAP)  4.87 us
  transfers between devices with their start and end apart: 6, of which 3 were waited for; matrix products, arithmetic and copies ran while one was open for 0% of the time, Pallas kernels for 6%

profile of v9, /device:TPU:8, one launch (start us, length us, event | category | flops | bytes accessed | tf_op | source)
XLA Modules:
  0.0 131.1 jit_solution(4576459747582154088)
XLA Ops:
  0.6 0.0 copy-start.3
  0.6 0.0 copy-start.4
  0.7 0.0 copy-start.2
  0.7 2.3 %shard_map.77 = (bf16[128,1024]{1,0:T(8,128)(2,1)S(1)}, f32[128,1024]{1,0:T(8,128)S(1)}) custom-call(s32[1]{0:T(128)} %bitcast.half_ref, bf16[256,1024]{1,0:T(8,128)(2,1)} %hidden_ref.1, bf16[1024,1024]{1,0:T(8,128)(2,1)} %b_hbm.3), custom_call_target="tpu_custom_call" | custom-call | tf_op jit(solution)/shard_map/pallas_call | solution.py:230
  2.9 0.0 copy-start
  2.9 2.1 %collective-permute-start = (bf16[128,1024]{1,0:T(8,128)(2,1)S(1)}, bf16[128,1024]{1,0:T(8,128)(2,1)S(1)}, u32[]{:S(2)}, u32[]{:S(2)}) collective-permute-start(bf16[128,1024]{1,0:T(8,128)(2,1)S(1)} %get-tuple-element.18), channel_id=1, source_target_pairs={{0,1},{1,0},{2,3},{3,2},{4,5},{5,4},{6,7},{7,6},{8,9},{9,8},{10,11... | collective-permute-start | bytes 786440 | tf_op jit(solution)/shard_map/ppermute | solution.py:242
  5.0 0.0 copy-done.3
  5.0 0.0 copy-done.4
  5.1 1.4 %collective-permute-done.other_ref = bf16[128,1024]{1,0:T(8,128)(2,1)S(1)} collective-permute-done((bf16[128,1024]{1,0:T(8,128)(2,1)S(1)}, bf16[128,1024]{1,0:T(8,128)(2,1)S(1)}, u32[]{:S(2)}, u32[]{:S(2)}) %collective-permute-start) | collective-permute-done | bytes 262176 | tf_op jit(solution)/shard_map/ppermute | solution.py:242
  6.6 9.0 %all-gather = bf16[256,1024]{1,0:T(8,128)(2,1)S(1)} all-gather(bf16[128,1024]{1,0:T(8,128)(2,1)S(1)} %shard_map.78), channel_id=2, replica_groups=mesh['yh'=4,'yl'=2,'xh'=2,'zh'=6,'zl'=2,'xl'=2,'core'=2] {'xl'}, dimensions={0}, use_global_device_ids=true | all-gather | bytes 786432 | tf_op jit(solution)/shard_map/all_gather | solution.py:243
  15.6 0.2 multiply_reduce_fusion.1
  15.8 0.0 copy-done.2
  15.8 0.1 multiply_convert_fusion.1
  15.9 2.2 %all_gather.23.normed_ref = bf16[256,1024]{1,0:T(8,128)(2,1)S(1)} all-gather(bf16[128,1024]{1,0:T(8,128)(2,1)S(1)} %multiply_convert_fusion.1), channel_id=1, replica_groups=mesh['yh'=4,'yl'=2,'xh'=2,'zh'=6,'zl'=2,'xl'=2,'core'=2] {'core'}, dimensions={0}, use_global_device_ids=true | all-gather | bytes 786432 | tf_op jit(solution)/shard_map/all_gather | solution.py:246
  18.1 0.0 copy-done
  18.1 0.8 shard_map.79
  18.8 5.1 %all-gather.2 = f32[4,1,256]{2,1,0:T(1,128)S(1)} all-gather(f32[1,1,256]{2,1,0:T(1,128)S(1)} %bitcast.17), channel_id=1, replica_groups=mesh['yh'=4,'yl'=2,'xh'=2,'zh'=6,'zl'=2,'xl'=2,'core'=2] {'xl','core'}, dimensions={0}, use_global_device_ids=true | all-gather | bytes 5120 | tf_op jit(solution)/shard_map/all_gather | solution.py:251
  23.9 0.9 shard_map.80
  24.8 2.2 %collective-permute-start.1 = (bf16[128,1024]{1,0:T(8,128)(2,1)S(1)}, bf16[128,1024]{1,0:T(8,128)(2,1)S(1)}, u32[]{:S(2)}, u32[]{:S(2)}) collective-permute-start(bf16[128,1024]{1,0:T(8,128)(2,1)S(1)} %shard_map.80), channel_id=1, source_target_pairs={{0,1},{1,0},{2,3},{3,2},{4,5},{5,4},{6,7},{7,6},{8,9},{9,8},{10,11... | collective-permute-start | bytes 786440 | tf_op jit(solution)/shard_map/ppermute | solution.py:275
  27.0 2.1 %shard_map.81 = (f32[128,1024]{1,0:T(8,128)S(1)}, bf16[16,8,1024]{2,1,0:T(8,128)(2,1)S(1)}, bf16[4,96,1024]{2,1,0:T(8,128)(2,1)}) custom-call(s32[1]{0:T(128)} %bitcast.half_ref, f32[256,512]{1,0:T(8,128)S(1)} %get-tuple-element.21.exp_ref, f32[4,256]{1,0:T(4,128)S(1)} %bitcast.12, f32[1,256]{1,0:T(1,128)S(1)} %bitcast.16, f32[1,256]{1,0:T(1,128)S(1)} %bitcast.14, ...), custom_call_target="tpu_custom_call" | custom-call | tf_op jit(solution)/shard_map/pallas_call | solution.py:259
  29.1 0.0 collective-permute-done.1.other_ref
  29.2 12.9 %all-to-all-start = ((bf16[4,96,1024]{2,1,0:T(8,128)(2,1)}), bf16[4,96,1024]{2,1,0:T(8,128)(2,1)S(1)}, u32[]{:S(2)}, u32[]{:S(2)}) async-start(bf16[4,96,1024]{2,1,0:T(8,128)(2,1)} %get-tuple-element.27), calls=%async_computation | async-start | bytes 1572864 | tf_op jit(solution)/shard_map/all_to_all | solution.py:276
  42.1 0.0 copy-start.1
  42.1 8.9 %all-gather.1 = bf16[256,1024]{1,0:T(8,128)(2,1)S(1)} all-gather(bf16[128,1024]{1,0:T(8,128)(2,1)S(1)} %shard_map.82), channel_id=3, replica_groups=mesh['yh'=4,'yl'=2,'xh'=2,'zh'=6,'zl'=2,'xl'=2,'core'=2] {'xl'}, dimensions={0}, use_global_device_ids=true | all-gather | bytes 786432 | tf_op jit(solution)/shard_map/all_gather | solution.py:278
  51.1 0.3 multiply_reduce_fusion
  51.3 0.2 multiply_convert_fusion
  51.6 2.2 %all_gather.27.grad_ref = bf16[256,1024]{1,0:T(8,128)(2,1)S(1)} all-gather(bf16[128,1024]{1,0:T(8,128)(2,1)S(1)} %multiply_convert_fusion), channel_id=1, replica_groups=mesh['yh'=4,'yl'=2,'xh'=2,'zh'=6,'zl'=2,'xl'=2,'core'=2] {'core'}, dimensions={0}, use_global_device_ids=true | all-gather | bytes 786432 | tf_op jit(solution)/shard_map/all_gather | solution.py:280
  53.8 0.0 copy-done.1
  53.8 2.2 %shard_map.84 = bf16[8,144,1024]{2,1,0:T(8,128)(2,1)} custom-call(bf16[256,1024]{1,0:T(8,128)(2,1)S(1)} %copy-done.1, bf16[256,1024]{1,0:T(8,128)(2,1)S(1)} %all_gather.27.grad_ref, bf16[16,8,1024]{2,1,0:T(8,128)(2,1)S(1)} %get-tuple-element.26.head_ref), custom_call_target="tpu_custom_call" | custom-call | tf_op jit(solution)/shard_map/pallas_call | solution.py:282
  56.0 0.0 all-to-all-done.pieces_ref
  56.1 0.1 shard_map.85
  56.2 4.2 %all-to-all-start.1 = ((bf16[8,144,1024]{2,1,0:T(8,128)(2,1)}), bf16[8,144,1024]{2,1,0:T(8,128)(2,1)S(1)}, u32[]{:S(2)}, u32[]{:S(2)}) async-start(bf16[8,144,1024]{2,1,0:T(8,128)(2,1)} %shard_map.84), calls=%async_computation.1 | async-start | bytes 4718592 | tf_op jit(solution)/shard_map/all_to_all | solution.py:296
  60.4 4.9 %collective-permute-start.2 = (bf16[48,1024]{1,0:T(8,128)(2,1)S(1)}, bf16[48,1024]{1,0:T(8,128)(2,1)S(1)}, u32[]{:S(2)}, u32[]{:S(2)}) collective-permute-start(bf16[48,1024]{1,0:T(8,128)(2,1)S(1)} %get-tuple-element.31), channel_id=1, source_target_pairs={{0,48},{48,0},{1,49},{49,1},{2,50},{50,2},{3,51},{51,3},{4,52},{52... | collective-permute-start | bytes 294920 | tf_op jit(solution)/shard_map/ppermute | solution.py:297
  65.3 26.1 %collective-permute-done.2.other_ref = bf16[48,1024]{1,0:T(8,128)(2,1)S(1)} collective-permute-done((bf16[48,1024]{1,0:T(8,128)(2,1)S(1)}, bf16[48,1024]{1,0:T(8,128)(2,1)S(1)}, u32[]{:S(2)}, u32[]{:S(2)}) %collective-permute-start.2) | collective-permute-done | bytes 98336 | tf_op jit(solution)/shard_map/ppermute | solution.py:297
  91.4 0.0 all-to-all-done.1.pieces_ref
  91.4 1.1 shard_map.86
  92.4 13.5 %all-to-all-start.2 = ((bf16[24,8,1024]{2,1,0:T(8,128)(2,1)}), bf16[24,8,1024]{2,1,0:T(8,128)(2,1)S(1)}, u32[]{:S(2)}, u32[]{:S(2)}) async-start(bf16[24,8,1024]{2,1,0:T(8,128)(2,1)} %bitcast.6), calls=%async_computation.2 | async-start | bytes 786432 | tf_op jit(solution)/shard_map/all_to_all | solution.py:301
  105.9 3.7 %shard_map.83 = bf16[256,1024]{1,0:T(8,128)(2,1)} custom-call(bf16[256,1024]{1,0:T(8,128)(2,1)S(1)} %all_gather.27.grad_ref, bf16[1024,1024]{1,0:T(8,128)(2,1)} %b_hbm.3), custom_call_target="tpu_custom_call" | custom-call | flops 536870912 | bytes 3145728 | tf_op jit(solution)/shard_map/pallas_call | solution.py:305
  109.6 20.8 %all-to-all-done.2.pieces_ref = bf16[24,8,1024]{2,1,0:T(8,128)(2,1)S(1)} async-done(((bf16[24,8,1024]{2,1,0:T(8,128)(2,1)}), bf16[24,8,1024]{2,1,0:T(8,128)(2,1)S(1)}, u32[]{:S(2)}, u32[]{:S(2)}) %all-to-all-start.2) | async-done | bytes 393248 | tf_op jit(solution)/shard_map/all_to_all | solution.py:301
  130.5 0.7 shard_map.87
  (7 shorter events, 0.1 us)
Async XLA Ops:
  0.6 4.4 %copy-start.3 = (s32[256]{0:T(256)S(1)}, s32[256]{0:T(256)}, u32[]{:S(2)}) copy-start(s32[256]{0:T(256)} %param.11) | copy-start | bytes 3076
  0.6 4.4 %copy-start.4 = (s32[256]{0:T(256)S(1)}, s32[256]{0:T(256)}, u32[]{:S(2)}) copy-start(s32[256]{0:T(256)} %param.10) | copy-start | bytes 3076
  0.7 15.1 %copy-start.2 = (f32[1024]{0:T(1024)S(1)}, f32[1024]{0:T(1024)}, u32[]{:S(2)}) copy-start(f32[1024]{0:T(1024)} %param.8) | copy-start | bytes 12292
  2.9 15.1 %copy-start = (bf16[1024,512]{1,0:T(8,128)(2,1)S(1)}, bf16[1024,512]{1,0:T(8,128)(2,1)}, u32[]{:S(2)}) copy-start(bf16[1024,512]{1,0:T(8,128)(2,1)} %head_ref.5) | copy-start | bytes 3145732
  2.9 3.6 %collective-permute-start = (bf16[128,1024]{1,0:T(8,128)(2,1)S(1)}, bf16[128,1024]{1,0:T(8,128)(2,1)S(1)}, u32[]{:S(2)}, u32[]{:S(2)}) collective-permute-start(bf16[128,1024]{1,0:T(8,128)(2,1)S(1)} %get-tuple-element.18), channel_id=1, source_target_pairs={{0,1},{1,0},{2,3},{3,2},{4,5},{5,4},{6,7},{7,6},{8,9},{9,8},{10,11... | collective-permute-start | bytes 786440 | tf_op jit(solution)/shard_map/ppermute | solution.py:242
  24.8 4.3 %collective-permute-start.1 = (bf16[128,1024]{1,0:T(8,128)(2,1)S(1)}, bf16[128,1024]{1,0:T(8,128)(2,1)S(1)}, u32[]{:S(2)}, u32[]{:S(2)}) collective-permute-start(bf16[128,1024]{1,0:T(8,128)(2,1)S(1)} %shard_map.80), channel_id=1, source_target_pairs={{0,1},{1,0},{2,3},{3,2},{4,5},{5,4},{6,7},{7,6},{8,9},{9,8},{10,11... | collective-permute-start | bytes 786440 | tf_op jit(solution)/shard_map/ppermute | solution.py:275
  29.2 26.9 %all-to-all-start = ((bf16[4,96,1024]{2,1,0:T(8,128)(2,1)}), bf16[4,96,1024]{2,1,0:T(8,128)(2,1)S(1)}, u32[]{:S(2)}, u32[]{:S(2)}) async-start(bf16[4,96,1024]{2,1,0:T(8,128)(2,1)} %get-tuple-element.27), calls=%async_computation | async-start | bytes 1572864 | tf_op jit(solution)/shard_map/all_to_all | solution.py:276
  42.1 11.7 %copy-start.1 = (bf16[256,1024]{1,0:T(8,128)(2,1)S(1)}, bf16[256,1024]{1,0:T(8,128)(2,1)}, u32[]{:S(2)}) copy-start(bf16[256,1024]{1,0:T(8,128)(2,1)} %hidden_ref.1) | copy-start | bytes 1572868
  56.2 35.2 %all-to-all-start.1 = ((bf16[8,144,1024]{2,1,0:T(8,128)(2,1)}), bf16[8,144,1024]{2,1,0:T(8,128)(2,1)S(1)}, u32[]{:S(2)}, u32[]{:S(2)}) async-start(bf16[8,144,1024]{2,1,0:T(8,128)(2,1)} %shard_map.84), calls=%async_computation.1 | async-start | bytes 4718592 | tf_op jit(solution)/shard_map/all_to_all | solution.py:296
  60.4 31.0 %collective-permute-start.2 = (bf16[48,1024]{1,0:T(8,128)(2,1)S(1)}, bf16[48,1024]{1,0:T(8,128)(2,1)S(1)}, u32[]{:S(2)}, u32[]{:S(2)}) collective-permute-start(bf16[48,1024]{1,0:T(8,128)(2,1)S(1)} %get-tuple-element.31), channel_id=1, source_target_pairs={{0,48},{48,0},{1,49},{49,1},{2,50},{50,2},{3,51},{51,3},{4,52},{52... | collective-permute-start | bytes 294920 | tf_op jit(solution)/shard_map/ppermute | solution.py:297
  92.4 38.0 %all-to-all-start.2 = ((bf16[24,8,1024]{2,1,0:T(8,128)(2,1)}), bf16[24,8,1024]{2,1,0:T(8,128)(2,1)S(1)}, u32[]{:S(2)}, u32[]{:S(2)}) async-start(bf16[24,8,1024]{2,1,0:T(8,128)(2,1)} %bitcast.6), calls=%async_computation.2 | async-start | bytes 786432 | tf_op jit(solution)/shard_map/all_to_all | solution.py:301

commit v10 on v9

--- a/solution.py
+++ b/solution.py
@@ -97,22 +97,22 @@
     )
 
 
-def dlogit_rows(first, exp_ref, totals_ref, code_ref, mask_ref, rows):
+def dlogit_rows(first, column, exp_ref, totals_ref, code_ref, mask_ref, rows):
     window = pl.ds(first, rows)
-    total, code, weight = (spread(ref[:, window]) for ref in (totals_ref, code_ref, mask_ref))
+    total, code, weight = (spread(ref[:, window].astype(f32)) for ref in (totals_ref, code_ref, mask_ref))
     scale = weight / total
     parts = []
     for start in range(0, exp_ref.shape[1], 128):
-        columns = (lax.broadcasted_iota(jnp.int32, (rows, 128), 1) + start).astype(f32)
+        columns = (lax.broadcasted_iota(jnp.int32, (rows, 128), 1) + (column + start)).astype(f32)
         onehot = jnp.where(columns == code, weight, 0.0)
         parts.append((scale * exp_ref[window, start : start + 128] - onehot).astype(bf16))
     return jnp.concatenate(parts, axis=1)
 
 
-def sent_grad(half_ref, exp_ref, totals_ref, code_ref, mask_ref, head_ref, out_ref):
+def sent_grad(half_ref, column_ref, exp_ref, totals_ref, code_ref, mask_ref, head_ref, out_ref):
     rows = out_ref.shape[0]
     start = pl.multiple_of(half_ref[0] * rows, rows)
-    dlogit = dlogit_rows(start, exp_ref, totals_ref, code_ref, mask_ref, rows)
+    dlogit = dlogit_rows(start, column_ref[0], exp_ref, totals_ref, code_ref, mask_ref, rows)
     out_ref[...] = dot(dlogit, head_ref[...], 1, 1).astype(out_ref.dtype)
 
 
@@ -124,10 +124,10 @@
 
 
 def kept_grad(
-    half_ref, exp_ref, totals_ref, code_ref, mask_ref, head_ref, normed_ref,
+    half_ref, column_ref, exp_ref, totals_ref, code_ref, mask_ref, head_ref, normed_ref,
     out_ref, late_ref, early_hbm, dlogit_ref, early_ref, sems,
 ):
-    dlogit_ref[...] = dlogit_rows(0, exp_ref, totals_ref, code_ref, mask_ref, exp_ref.shape[0])
+    dlogit_ref[...] = dlogit_rows(0, column_ref[0], exp_ref, totals_ref, code_ref, mask_ref, exp_ref.shape[0])
     grad = dot(normed_ref[...], dlogit_ref[...], 0, 0).astype(bf16)
     part = grad.shape[1]
     for i in range(BLOCKS - PROJ_BLOCKS):
@@ -170,6 +170,10 @@
     kept_ref[...] = add_up(pieces_ref.at[:, mine])
 
 
+def chip_sum_of(half_ref, kept_ref, both_ref, out_ref):
+    out_ref[...] = (kept_ref[...] + both_ref[1 - half_ref[0]].astype(f32)).astype(out_ref.dtype)
+
+
 def chip_sum(kept_ref, other_ref, out_ref):
     out_ref[...] = (kept_ref[...] + other_ref[...].astype(f32)).astype(out_ref.dtype)
 
@@ -223,10 +227,10 @@
     gain = norm_gain[None, :]
     mine = lax.axis_index("core").reshape(1)
     other = 1 - mine
-    code = (code_ids - tp * vocab_part).astype(f32)[None, :]
-    mask = stream_mask.astype(f32)[None, :]
-
-    steps, inner = 4, hidden.shape[1]
+    code, mask = code_ids[None, :], stream_mask[None, :]
+    first_column = (tp * vocab_part).reshape(1)
+
+    steps, inner = 8, hidden.shape[1]
     sent, kept = pl.pallas_call(
         streamed_product,
         out_shape=[shape((half, width), bf16), shape((half, width), f32)],
@@ -239,7 +243,7 @@
         ],
         compiler_params=pltpu.CompilerParams(vmem_limit_bytes=VMEM_BYTES),
     )(mine, *(pltpu.with_memory_space_constraint(array, pltpu.HBM) for array in (hidden, in_proj)))
-    chip = in_vmem(chip_sum, shape((half, width), bf16), 2)(kept, lax.ppermute(sent, "core", SWAP))
+    chip = in_vmem(chip_sum_of, shape((half, width), bf16), 2, 1)(mine, kept, lax.all_gather(sent, "core"))
     x = add_up(lax.all_gather(chip, "xl"))
     inv_rms = lax.rsqrt(jnp.mean(x * x, axis=1, keepdims=True) + norm_eps)
     unit_rows = x * inv_rms
@@ -251,7 +255,7 @@
     totals = lax.all_gather(sums, TP, tiled=True)
 
     rest = (exp_logits, totals, code, mask, head_weight)
-    sent = in_vmem(sent_grad, shape((half, width), bf16), 5, 1)(other, *rest)
+    sent = in_vmem(sent_grad, shape((half, width), bf16), 5, 2)(other, first_column, *rest)
     exp_logits, sent = lax.optimization_barrier((exp_logits, sent))
     rest = (exp_logits, *rest[1:])
     vmem = pl.BlockSpec(memory_space=pltpu.VMEM)
@@ -263,7 +267,7 @@
             shape((LATE_BLOCKS - PROJ_BLOCKS, 8, width), bf16),
             shape((4, 96, width), bf16),
         ],
-        in_specs=[pl.BlockSpec(memory_space=pltpu.SMEM)] + [vmem] * 6,
+        in_specs=[pl.BlockSpec(memory_space=pltpu.SMEM)] * 2 + [vmem] * 6,
         out_specs=[vmem, vmem, hbm],
         scratch_shapes=[
             pltpu.VMEM((frames, vocab_part), bf16),
@@ -271,7 +275,7 @@
             pltpu.SemaphoreType.DMA((4,)),
         ],
         compiler_params=pltpu.CompilerParams(vmem_limit_bytes=VMEM_BYTES),
-    )(mine, *rest, normed)
+    )(mine, first_column, *rest, normed)
     early, swapped = lax.optimization_barrier((early, lax.ppermute(sent, "core", SWAP)))
     early = lax.all_to_all(early, EARLY, 0, 0)
     chip = in_vmem(chip_sum, shape((half, width), bf16), 2)(kept, swapped)

time: 132 us -> 132 us (level)
  waiting for transfers between devices: 48.4 us -> 45.4 us
  blocking collectives: 27.4 us -> 29.7 us
  starting transfers between devices: 39.8 us -> 37.8 us
  Pallas kernels: 13.9 us -> 15.8 us
    all_gather x0 -> x1, blocking collectives: none -> 2.31 us  [local(): lax.all_gather(sent, 'core')]
    ppermute x2 -> x1, starting transfers between devices: 4.28 us -> 2.23 us  [local(): lax.ppermute(sent, 'core', SWAP)]
    all_to_all x1, waiting for transfers between devices: 20.8 us -> 19.3 us  [local(): far = lax.all_to_all(near.reshape(N_FAR, 8, width), FAR, 0, 0)]
    pallas_call x1, Pallas kernels: 3.69 us -> 5.19 us  [local(): pl.pallas_call(hidden_rows, out_shape=shape((frames, inner), bf16), in_sp...]
    ppermute x2 -> x1, waiting for transfers between devices: 1.45 us -> 0.01 us  [local(): lax.ppermute(sent, 'core', SWAP)]
  transfers between devices with their start and end apart: 6 -> 5, of which waited for: 3 -> 2; matrix products, arithmetic and copies ran while one was open for 0% -> 1% of each run, Pallas kernels for 6% -> 7%
where the time goes in v10:
time: 132 us
  waiting for transfers between devices  45.4 us (34%)
  starting transfers between devices  37.8 us (29%)
  blocking collectives  29.7 us (22%)
  Pallas kernels  15.8 us (12%)
  other arithmetic  1.83 us (1%)
    ppermute x1, waiting for transfers between devices, local(): early_other = lax.ppermute(early_sent, 'xh', SWAP)  26.1 us
    all_to_all x1, waiting for transfers between devices, local(): far = lax.all_to_all(near.reshape(N_FAR, 8, width), FAR, 0, 0)  19.3 us
    all_to_all x1, starting transfers between devices, local(): far = lax.all_to_all(near.reshape(N_FAR, 8, width), FAR, 0, 0)  13.5 us
    all_to_all x1, starting transfers between devices, local(): early = lax.all_to_all(early, EARLY, 0, 0)  13.1 us
    all_gather x1, blocking collectives, local(): x = add_up(lax.all_gather(chip, 'xl'))  9.02 us
    all_gather x1, blocking collectives, local(): scaled_grad = add_up(lax.all_gather(chip, 'xl')) * gain  8.94 us
    pallas_call x1, Pallas kernels, local(): pl.pallas_call(hidden_rows, out_shape=shape((frames, inner), bf16), in_sp...  5.19 us
    all_gather x1, blocking collectives, local(): totals = lax.all_gather(sums, TP, tiled=True)  5.08 us
  transfers between devices with their start and end apart: 5, of which 2 were waited for; matrix products, arithmetic and copies ran while one was open for 1% of the time, Pallas kernels for 7%

profile of v10, /device:TPU:8, one launch (start us, length us, event | category | flops | bytes accessed | tf_op | source)
XLA Modules:
  0.0 131.9 jit_solution(8230260007152081210)
XLA Ops:
  0.6 2.7 %shard_map.77 = (bf16[128,1024]{1,0:T(8,128)(2,1)S(1)}, f32[128,1024]{1,0:T(8,128)S(1)}) custom-call(s32[1]{0:T(128)} %bitcast.half_ref, bf16[256,1024]{1,0:T(8,128)(2,1)} %hidden_ref.1, bf16[1024,1024]{1,0:T(8,128)(2,1)} %b_hbm.3), custom_call_target="tpu_custom_call" | custom-call | tf_op jit(solution)/shard_map/pallas_call | solution.py:234
  3.4 0.0 copy-start.6
  3.4 0.0 copy-start
  3.4 2.3 %all-gather = bf16[256,1024]{1,0:T(8,128)(2,1)S(1)} all-gather(bf16[128,1024]{1,0:T(8,128)(2,1)S(1)} %get-tuple-element.18), channel_id=2, replica_groups=mesh['yh'=4,'yl'=2,'xh'=2,'zh'=6,'zl'=2,'xl'=2,'core'=2] {'core'}, dimensions={0}, use_global_device_ids=true | all-gather | bytes 786432 | tf_op jit(solution)/shard_map/all_gather | solution.py:246
  5.7 0.0 copy-start.2
  5.8 0.0 copy-start.3
  5.8 9.0 %all-gather.1 = bf16[256,1024]{1,0:T(8,128)(2,1)S(1)} all-gather(bf16[128,1024]{1,0:T(8,128)(2,1)S(1)} %shard_map.78), channel_id=3, replica_groups=mesh['yh'=4,'yl'=2,'xh'=2,'zh'=6,'zl'=2,'xl'=2,'core'=2] {'xl'}, dimensions={0}, use_global_device_ids=true | all-gather | bytes 786432 | tf_op jit(solution)/shard_map/all_gather | solution.py:247
  14.8 0.0 copy-start.4
  14.8 0.2 multiply_reduce_fusion.1
  15.0 0.0 copy-done.6
  15.0 0.1 multiply_convert_fusion.1
  15.1 0.5 copy-done.4
  15.6 2.2 %all_gather.31.normed_ref = bf16[256,1024]{1,0:T(8,128)(2,1)S(1)} all-gather(bf16[128,1024]{1,0:T(8,128)(2,1)S(1)} %multiply_convert_fusion.1), channel_id=1, replica_groups=mesh['yh'=4,'yl'=2,'xh'=2,'zh'=6,'zl'=2,'xl'=2,'core'=2] {'core'}, dimensions={0}, use_global_device_ids=true | all-gather | bytes 786432 | tf_op jit(solution)/shard_map/all_gather | solution.py:250
  17.8 0.0 copy-done
  17.8 0.8 shard_map.79
  18.5 5.1 %all-gather.3 = f32[4,1,256]{2,1,0:T(1,128)S(1)} all-gather(f32[1,1,256]{2,1,0:T(1,128)S(1)} %bitcast.20), channel_id=1, replica_groups=mesh['yh'=4,'yl'=2,'xh'=2,'zh'=6,'zl'=2,'xl'=2,'core'=2] {'xl','core'}, dimensions={0}, use_global_device_ids=true | all-gather | bytes 5120 | tf_op jit(solution)/shard_map/all_gather | solution.py:255
  23.6 0.0 copy-done.2
  23.6 0.0 copy-done.3
  23.6 0.9 shard_map.80
  24.5 2.2 %collective-permute-start = (bf16[128,1024]{1,0:T(8,128)(2,1)S(1)}, bf16[128,1024]{1,0:T(8,128)(2,1)S(1)}, u32[]{:S(2)}, u32[]{:S(2)}) collective-permute-start(bf16[128,1024]{1,0:T(8,128)(2,1)S(1)} %shard_map.80), channel_id=1, source_target_pairs={{0,1},{1,0},{2,3},{3,2},{4,5},{5,4},{6,7},{7,6},{8,9},{9,8},{10,11... | collective-permute-start | bytes 786440 | tf_op jit(solution)/shard_map/ppermute | solution.py:279
  26.7 2.1 %shard_map.81 = (f32[128,1024]{1,0:T(8,128)S(1)}, bf16[16,8,1024]{2,1,0:T(8,128)(2,1)S(1)}, bf16[4,96,1024]{2,1,0:T(8,128)(2,1)}) custom-call(s32[1]{0:T(128)} %bitcast.half_ref, s32[1]{0:T(128)} %bitcast.2.column_ref, f32[256,512]{1,0:T(8,128)S(1)} %get-tuple-element.21.exp_ref, f32[4,256]{1,0:T(4,128)S(1)} %bitcast.15, s32[1,256]{1,0:T(1,128)S(1)} %bitcast.17, ...), custom_call_target="tpu_custom_call" | custom-call | tf_op jit(solution)/shard_map/pallas_call | solution.py:263
  28.8 0.0 copy-start.5
  28.8 0.0 collective-permute-done.other_ref
  28.9 13.1 %all-to-all-start = ((bf16[4,96,1024]{2,1,0:T(8,128)(2,1)}), bf16[4,96,1024]{2,1,0:T(8,128)(2,1)S(1)}, u32[]{:S(2)}, u32[]{:S(2)}) async-start(bf16[4,96,1024]{2,1,0:T(8,128)(2,1)} %get-tuple-element.27), calls=%async_computation | async-start | bytes 1572864 | tf_op jit(solution)/shard_map/all_to_all | solution.py:280
  41.9 0.0 copy-start.1
  42.0 8.9 %all-gather.2 = bf16[256,1024]{1,0:T(8,128)(2,1)S(1)} all-gather(bf16[128,1024]{1,0:T(8,128)(2,1)S(1)} %shard_map.82), channel_id=4, replica_groups=mesh['yh'=4,'yl'=2,'xh'=2,'zh'=6,'zl'=2,'xl'=2,'core'=2] {'xl'}, dimensions={0}, use_global_device_ids=true | all-gather | bytes 786432 | tf_op jit(solution)/shard_map/all_gather | solution.py:282
  50.9 1.3 multiply_reduce_fusion
  52.2 0.0 copy-done.5
  52.2 0.2 multiply_convert_fusion
  52.5 2.2 %all_gather.35.grad_ref = bf16[256,1024]{1,0:T(8,128)(2,1)S(1)} all-gather(bf16[128,1024]{1,0:T(8,128)(2,1)S(1)} %multiply_convert_fusion), channel_id=1, replica_groups=mesh['yh'=4,'yl'=2,'xh'=2,'zh'=6,'zl'=2,'xl'=2,'core'=2] {'core'}, dimensions={0}, use_global_device_ids=true | all-gather | bytes 786432 | tf_op jit(solution)/shard_map/all_gather | solution.py:284
  54.6 0.0 copy-done.1
  54.6 2.2 %shard_map.84 = bf16[8,144,1024]{2,1,0:T(8,128)(2,1)} custom-call(bf16[256,1024]{1,0:T(8,128)(2,1)S(1)} %copy-done.1, bf16[256,1024]{1,0:T(8,128)(2,1)S(1)} %all_gather.35.grad_ref, bf16[16,8,1024]{2,1,0:T(8,128)(2,1)S(1)} %get-tuple-element.26.head_ref), custom_call_target="tpu_custom_call" | custom-call | tf_op jit(solution)/shard_map/pallas_call | solution.py:286
  56.9 0.0 all-to-all-done.pieces_ref
  56.9 0.1 shard_map.85
  57.0 4.2 %all-to-all-start.1 = ((bf16[8,144,1024]{2,1,0:T(8,128)(2,1)}), bf16[8,144,1024]{2,1,0:T(8,128)(2,1)S(1)}, u32[]{:S(2)}, u32[]{:S(2)}) async-start(bf16[8,144,1024]{2,1,0:T(8,128)(2,1)} %shard_map.84), calls=%async_computation.1 | async-start | bytes 4718592 | tf_op jit(solution)/shard_map/all_to_all | solution.py:300
  61.2 4.9 %collective-permute-start.1 = (bf16[48,1024]{1,0:T(8,128)(2,1)S(1)}, bf16[48,1024]{1,0:T(8,128)(2,1)S(1)}, u32[]{:S(2)}, u32[]{:S(2)}) collective-permute-start(bf16[48,1024]{1,0:T(8,128)(2,1)S(1)} %get-tuple-element.31), channel_id=1, source_target_pairs={{0,48},{48,0},{1,49},{49,1},{2,50},{50,2},{3,51},{51,3},{4,52},{52... | collective-permute-start | bytes 294920 | tf_op jit(solution)/shard_map/ppermute | solution.py:301
  66.1 26.1 %collective-permute-done.1.other_ref = bf16[48,1024]{1,0:T(8,128)(2,1)S(1)} collective-permute-done((bf16[48,1024]{1,0:T(8,128)(2,1)S(1)}, bf16[48,1024]{1,0:T(8,128)(2,1)S(1)}, u32[]{:S(2)}, u32[]{:S(2)}) %collective-permute-start.1) | collective-permute-done | bytes 98336 | tf_op jit(solution)/shard_map/ppermute | solution.py:301
  92.2 0.0 all-to-all-done.1.pieces_ref
  92.2 1.1 shard_map.86
  93.3 13.5 %all-to-all-start.2 = ((bf16[24,8,1024]{2,1,0:T(8,128)(2,1)}), bf16[24,8,1024]{2,1,0:T(8,128)(2,1)S(1)}, u32[]{:S(2)}, u32[]{:S(2)}) async-start(bf16[24,8,1024]{2,1,0:T(8,128)(2,1)} %bitcast.8), calls=%async_computation.2 | async-start | bytes 786432 | tf_op jit(solution)/shard_map/all_to_all | solution.py:305
  106.8 5.2 %shard_map.83 = bf16[256,1024]{1,0:T(8,128)(2,1)} custom-call(bf16[256,1024]{1,0:T(8,128)(2,1)S(1)} %all_gather.35.grad_ref, bf16[1024,1024]{1,0:T(8,128)(2,1)} %b_hbm.3), custom_call_target="tpu_custom_call" | custom-call | flops 536870912 | bytes 3145728 | tf_op jit(solution)/shard_map/pallas_call | solution.py:309
  112.0 19.3 %all-to-all-done.2.pieces_ref = bf16[24,8,1024]{2,1,0:T(8,128)(2,1)S(1)} async-done(((bf16[24,8,1024]{2,1,0:T(8,128)(2,1)}), bf16[24,8,1024]{2,1,0:T(8,128)(2,1)S(1)}, u32[]{:S(2)}, u32[]{:S(2)}) %all-to-all-start.2) | async-done | bytes 393248 | tf_op jit(solution)/shard_map/all_to_all | solution.py:305
  131.3 0.7 shard_map.87
  (5 shorter events, 0.1 us)
Async XLA Ops:
  3.4 11.6 %copy-start.6 = (f32[1024]{0:T(1024)S(1)}, f32[1024]{0:T(1024)}, u32[]{:S(2)}) copy-start(f32[1024]{0:T(1024)} %param.8) | copy-start | bytes 12292
  3.4 14.4 %copy-start = (bf16[1024,512]{1,0:T(8,128)(2,1)S(1)}, bf16[1024,512]{1,0:T(8,128)(2,1)}, u32[]{:S(2)}) copy-start(bf16[1024,512]{1,0:T(8,128)(2,1)} %head_ref.5) | copy-start | bytes 3145732
  5.7 17.9 %copy-start.2 = (s32[256]{0:T(256)S(1)}, s32[256]{0:T(256)}, u32[]{:S(2)}) copy-start(s32[256]{0:T(256)} %param.10) | copy-start | bytes 3076
  5.8 17.8 %copy-start.3 = (s32[256]{0:T(256)S(1)}, s32[256]{0:T(256)}, u32[]{:S(2)}) copy-start(s32[256]{0:T(256)} %param.11) | copy-start | bytes 3076
  14.8 0.8 copy-start.4
  24.5 4.4 %collective-permute-start = (bf16[128,1024]{1,0:T(8,128)(2,1)S(1)}, bf16[128,1024]{1,0:T(8,128)(2,1)S(1)}, u32[]{:S(2)}, u32[]{:S(2)}) collective-permute-start(bf16[128,1024]{1,0:T(8,128)(2,1)S(1)} %shard_map.80), channel_id=1, source_target_pairs={{0,1},{1,0},{2,3},{3,2},{4,5},{5,4},{6,7},{7,6},{8,9},{9,8},{10,11... | collective-permute-start | bytes 786440 | tf_op jit(solution)/shard_map/ppermute | solution.py:279
  28.8 23.4 %copy-start.5 = (bf16[256,1024]{1,0:T(8,128)(2,1)S(1)}, bf16[256,1024]{1,0:T(8,128)(2,1)}, u32[]{:S(2)}) copy-start(bf16[256,1024]{1,0:T(8,128)(2,1)} %copy-done.4) | copy-start | bytes 1572868
  28.9 28.0 %all-to-all-start = ((bf16[4,96,1024]{2,1,0:T(8,128)(2,1)}), bf16[4,96,1024]{2,1,0:T(8,128)(2,1)S(1)}, u32[]{:S(2)}, u32[]{:S(2)}) async-start(bf16[4,96,1024]{2,1,0:T(8,128)(2,1)} %get-tuple-element.27), calls=%async_computation | async-start | bytes 1572864 | tf_op jit(solution)/shard_map/all_to_all | solution.py:280
  41.9 12.7 %copy-start.1 = (bf16[256,1024]{1,0:T(8,128)(2,1)S(1)}, bf16[256,1024]{1,0:T(8,128)(2,1)}, u32[]{:S(2)}) copy-start(bf16[256,1024]{1,0:T(8,128)(2,1)} %hidden_ref.1) | copy-start | bytes 1572868
  57.0 35.2 %all-to-all-start.1 = ((bf16[8,144,1024]{2,1,0:T(8,128)(2,1)}), bf16[8,144,1024]{2,1,0:T(8,128)(2,1)S(1)}, u32[]{:S(2)}, u32[]{:S(2)}) async-start(bf16[8,144,1024]{2,1,0:T(8,128)(2,1)} %shard_map.84), calls=%async_computation.1 | async-start | bytes 4718592 | tf_op jit(solution)/shard_map/all_to_all | solution.py:300
  61.2 31.0 %collective-permute-start.1 = (bf16[48,1024]{1,0:T(8,128)(2,1)S(1)}, bf16[48,1024]{1,0:T(8,128)(2,1)S(1)}, u32[]{:S(2)}, u32[]{:S(2)}) collective-permute-start(bf16[48,1024]{1,0:T(8,128)(2,1)S(1)} %get-tuple-element.31), channel_id=1, source_target_pairs={{0,48},{48,0},{1,49},{49,1},{2,50},{50,2},{3,51},{51,3},{4,52},{52... | collective-permute-start | bytes 294920 | tf_op jit(solution)/shard_map/ppermute | solution.py:301
  93.3 38.0 %all-to-all-start.2 = ((bf16[24,8,1024]{2,1,0:T(8,128)(2,1)}), bf16[24,8,1024]{2,1,0:T(8,128)(2,1)S(1)}, u32[]{:S(2)}, u32[]{:S(2)}) async-start(bf16[24,8,1024]{2,1,0:T(8,128)(2,1)} %bitcast.8), calls=%async_computation.2 | async-start | bytes 786432 | tf_op jit(solution)/shard_map/all_to_all | solution.py:305

commit v11 on v10

--- a/solution.py
+++ b/solution.py
@@ -162,6 +162,15 @@
         copy.wait()
 
 
+def norm_back(x_ref, grad_ref, gain_ref, out_ref):
+    x, grad = add_up(x_ref), add_up(grad_ref)
+    inv_rms = lax.rsqrt(jnp.mean(x * x, axis=1, keepdims=True) + norm_eps)
+    unit_rows = x * inv_rms
+    scaled_grad = grad * gain_ref[...]
+    centred = scaled_grad - unit_rows * jnp.mean(scaled_grad * unit_rows, axis=1, keepdims=True)
+    out_ref[...] = (inv_rms * centred).astype(out_ref.dtype)
+
+
 def early_sum(half_ref, pieces_ref, sent_ref, kept_ref):
     rows = sent_ref.shape[0]
     mine = pl.ds(pl.multiple_of(half_ref[0] * rows, rows), rows)
@@ -230,7 +239,7 @@
     code, mask = code_ids[None, :], stream_mask[None, :]
     first_column = (tp * vocab_part).reshape(1)
 
-    steps, inner = 8, hidden.shape[1]
+    steps, inner = 4, hidden.shape[1]
     sent, kept = pl.pallas_call(
         streamed_product,
         out_shape=[shape((half, width), bf16), shape((half, width), f32)],
@@ -244,7 +253,8 @@
         compiler_params=pltpu.CompilerParams(vmem_limit_bytes=VMEM_BYTES),
     )(mine, *(pltpu.with_memory_space_constraint(array, pltpu.HBM) for array in (hidden, in_proj)))
     chip = in_vmem(chip_sum_of, shape((half, width), bf16), 2, 1)(mine, kept, lax.all_gather(sent, "core"))
-    x = add_up(lax.all_gather(chip, "xl"))
+    pieces = lax.all_gather(chip, "xl")
+    x = add_up(pieces)
     inv_rms = lax.rsqrt(jnp.mean(x * x, axis=1, keepdims=True) + norm_eps)
     unit_rows = x * inv_rms
     normed = lax.all_gather((unit_rows * gain).astype(bf16), "core", tiled=True)
@@ -276,12 +286,11 @@
         ],
         compiler_params=pltpu.CompilerParams(vmem_limit_bytes=VMEM_BYTES),
     )(mine, first_column, *rest, normed)
-    early, swapped = lax.optimization_barrier((early, lax.ppermute(sent, "core", SWAP)))
+    chip = in_vmem(chip_sum, shape((half, width), bf16), 2)(kept, lax.ppermute(sent, "core", SWAP))
+    early, chip = lax.optimization_barrier((early, chip))
     early = lax.all_to_all(early, EARLY, 0, 0)
-    chip = in_vmem(chip_sum, shape((half, width), bf16), 2)(kept, swapped)
-    scaled_grad = add_up(lax.all_gather(chip, "xl")) * gain
-    centred = scaled_grad - unit_rows * jnp.mean(scaled_grad * unit_rows, axis=1, keepdims=True)
-    row_grad = lax.all_gather((inv_rms * centred).astype(bf16), "core", tiled=True)
+    own_grad = in_vmem(norm_back, shape((half, width), bf16), 3)(pieces, lax.all_gather(chip, "xl"), gain)
+    row_grad = lax.all_gather(own_grad, "core", tiled=True)
 
     blocks = pl.pallas_call(
         grad_blocks,

time: 132 us -> 130 us (0.985)
  Pallas kernels: 15.8 us -> 14.2 us
  other arithmetic: 1.83 us -> 0.29 us
  waiting for transfers between devices: 45.4 us -> 46.9 us
    all_to_all x1, waiting for transfers between devices: 19.3 us -> 20.8 us  [local(): far = lax.all_to_all(near.reshape(N_FAR, 8, width), FAR, 0, 0)]
    pallas_call x1, Pallas kernels: 5.19 us -> 3.69 us  [local(): pl.pallas_call(hidden_rows, out_shape=shape((frames, inner), bf16), in_sp...]
  transfers between devices with their start and end apart: 5 -> 5, of which waited for: 2 -> 2; matrix products, arithmetic and copies ran while one was open for 1% -> 0% of each run, Pallas kernels for 7% -> 6%
where the time goes in v11:
time: 130 us
  waiting for transfers between devices  46.9 us (36%)
  starting transfers between devices  37.8 us (29%)
  blocking collectives  29.6 us (23%)
  Pallas kernels  14.2 us (11%)
    ppermute x1, waiting for transfers between devices, local(): early_other = lax.ppermute(early_sent, 'xh', SWAP)  26.1 us
    all_to_all x1, waiting for transfers between devices, local(): far = lax.all_to_all(near.reshape(N_FAR, 8, width), FAR, 0, 0)  20.8 us
    all_to_all x1, starting transfers between devices, local(): far = lax.all_to_all(near.reshape(N_FAR, 8, width), FAR, 0, 0)  13.5 us
    all_to_all x1, starting transfers between devices, local(): early = lax.all_to_all(early, EARLY, 0, 0)  13.1 us
    all_gather x1, blocking collectives, local(): pieces = lax.all_gather(chip, 'xl')  9.02 us
    all_gather x1, blocking collectives, local(): lax.all_gather(chip, 'xl')  8.79 us
    all_gather x1, blocking collectives, local(): totals = lax.all_gather(sums, TP, tiled=True)  5.08 us
    ppermute x1, starting transfers between devices, local(): early_other = lax.ppermute(early_sent, 'xh', SWAP)  4.87 us
  transfers between devices with their start and end apart: 5, of which 2 were waited for; matrix products, arithmetic and copies ran while one was open for 0% of the time, Pallas kernels for 6%

profile of v11, /device:TPU:8, one launch (start us, length us, event | category | flops | bytes accessed | tf_op | source)
XLA Modules:
  0.0 129.7 jit_solution(1046628776485551908)
XLA Ops:
  0.6 2.2 %shard_map.77 = (bf16[128,1024]{1,0:T(8,128)(2,1)S(1)}, f32[128,1024]{1,0:T(8,128)S(1)}) custom-call(s32[1]{0:T(128)} %bitcast.half_ref, bf16[256,1024]{1,0:T(8,128)(2,1)} %hidden_ref.1, bf16[1024,1024]{1,0:T(8,128)(2,1)} %b_hbm.3), custom_call_target="tpu_custom_call" | custom-call | tf_op jit(solution)/shard_map/pallas_call | solution.py:243
  2.9 0.0 copy-start.2
  2.9 0.0 copy-start
  2.9 2.3 %all-gather = bf16[256,1024]{1,0:T(8,128)(2,1)S(1)} all-gather(bf16[128,1024]{1,0:T(8,128)(2,1)S(1)} %get-tuple-element.18), channel_id=2, replica_groups=mesh['yh'=4,'yl'=2,'xh'=2,'zh'=6,'zl'=2,'xl'=2,'core'=2] {'core'}, dimensions={0}, use_global_device_ids=true | all-gather | bytes 786432 | tf_op jit(solution)/shard_map/all_gather | solution.py:255
  5.3 0.0 copy-start.3
  5.3 0.0 copy-start.4
  5.3 9.0 %all-gather.1 = bf16[256,1024]{1,0:T(8,128)(2,1)S(1)} all-gather(bf16[128,1024]{1,0:T(8,128)(2,1)S(1)} %shard_map.78), channel_id=3, replica_groups=mesh['yh'=4,'yl'=2,'xh'=2,'zh'=6,'zl'=2,'xl'=2,'core'=2] {'xl'}, dimensions={0}, use_global_device_ids=true | all-gather | bytes 786432 | tf_op jit(solution)/shard_map/all_gather | solution.py:256
  14.3 0.2 multiply_reduce_fusion
  14.5 0.0 copy-done.2
  14.5 0.1 multiply_convert_fusion
  14.6 2.2 %all_gather.31.normed_ref = bf16[256,1024]{1,0:T(8,128)(2,1)S(1)} all-gather(bf16[128,1024]{1,0:T(8,128)(2,1)S(1)} %multiply_convert_fusion), channel_id=1, replica_groups=mesh['yh'=4,'yl'=2,'xh'=2,'zh'=6,'zl'=2,'xl'=2,'core'=2] {'core'}, dimensions={0}, use_global_device_ids=true | all-gather | bytes 786432 | tf_op jit(solution)/shard_map/all_gather | solution.py:260
  16.8 0.0 copy-done
  16.8 0.8 shard_map.79
  17.6 5.1 %all-gather.3 = f32[4,1,256]{2,1,0:T(1,128)S(1)} all-gather(f32[1,1,256]{2,1,0:T(1,128)S(1)} %bitcast.26), channel_id=1, replica_groups=mesh['yh'=4,'yl'=2,'xh'=2,'zh'=6,'zl'=2,'xl'=2,'core'=2] {'xl','core'}, dimensions={0}, use_global_device_ids=true | all-gather | bytes 5120 | tf_op jit(solution)/shard_map/all_gather | solution.py:265
  22.7 0.0 copy-done.3
  22.7 0.0 copy-done.4
  22.7 0.9 shard_map.80
  23.6 2.2 %collective-permute-start = (bf16[128,1024]{1,0:T(8,128)(2,1)S(1)}, bf16[128,1024]{1,0:T(8,128)(2,1)S(1)}, u32[]{:S(2)}, u32[]{:S(2)}) collective-permute-start(bf16[128,1024]{1,0:T(8,128)(2,1)S(1)} %shard_map.80), channel_id=1, source_target_pairs={{0,1},{1,0},{2,3},{3,2},{4,5},{5,4},{6,7},{7,6},{8,9},{9,8},{10,11... | collective-permute-start | bytes 786440 | tf_op jit(solution)/shard_map/ppermute | solution.py:289
  25.8 2.1 %shard_map.81 = (f32[128,1024]{1,0:T(8,128)S(1)}, bf16[16,8,1024]{2,1,0:T(8,128)(2,1)S(1)}, bf16[4,96,1024]{2,1,0:T(8,128)(2,1)}) custom-call(s32[1]{0:T(128)} %bitcast.half_ref, s32[1]{0:T(128)} %bitcast.3.column_ref, f32[256,512]{1,0:T(8,128)S(1)} %get-tuple-element.21.exp_ref, f32[4,256]{1,0:T(4,128)S(1)} %bitcast.20, s32[1,256]{1,0:T(1,128)S(1)} %bitcast.23, ...), custom_call_target="tpu_custom_call" | custom-call | tf_op jit(solution)/shard_map/pallas_call | solution.py:273
  27.9 0.0 collective-permute-done.other_ref
  27.9 0.1 shard_map.82
  28.0 0.0 copy-start.1
  28.0 13.1 %all-to-all-start = ((bf16[4,96,1024]{2,1,0:T(8,128)(2,1)}), bf16[4,96,1024]{2,1,0:T(8,128)(2,1)S(1)}, u32[]{:S(2)}, u32[]{:S(2)}) async-start(bf16[4,96,1024]{2,1,0:T(8,128)(2,1)} %get-tuple-element.27), calls=%async_computation | async-start | bytes 1572864 | tf_op jit(solution)/shard_map/all_to_all | solution.py:291
  41.1 8.8 %all-gather.2 = bf16[256,1024]{1,0:T(8,128)(2,1)S(1)} all-gather(bf16[128,1024]{1,0:T(8,128)(2,1)S(1)} %shard_map.82), channel_id=4, replica_groups=mesh['yh'=4,'yl'=2,'xh'=2,'zh'=6,'zl'=2,'xl'=2,'core'=2] {'xl'}, dimensions={0}, use_global_device_ids=true | all-gather | bytes 786432 | tf_op jit(solution)/shard_map/all_gather | solution.py:292
  49.8 0.3 shard_map.83
  50.1 2.2 %all_gather.35.grad_ref = bf16[256,1024]{1,0:T(8,128)(2,1)S(1)} all-gather(bf16[128,1024]{1,0:T(8,128)(2,1)S(1)} %shard_map.83), channel_id=1, replica_groups=mesh['yh'=4,'yl'=2,'xh'=2,'zh'=6,'zl'=2,'xl'=2,'core'=2] {'core'}, dimensions={0}, use_global_device_ids=true | all-gather | bytes 786432 | tf_op jit(solution)/shard_map/all_gather | solution.py:293
  52.3 0.0 copy-done.1
  52.3 2.3 %shard_map.85 = bf16[8,144,1024]{2,1,0:T(8,128)(2,1)} custom-call(bf16[256,1024]{1,0:T(8,128)(2,1)S(1)} %copy-done.1, bf16[256,1024]{1,0:T(8,128)(2,1)S(1)} %all_gather.35.grad_ref, bf16[16,8,1024]{2,1,0:T(8,128)(2,1)S(1)} %get-tuple-element.26.head_ref), custom_call_target="tpu_custom_call" | custom-call | tf_op jit(solution)/shard_map/pallas_call | solution.py:295
  54.6 0.0 all-to-all-done.pieces_ref
  54.6 0.1 shard_map.86
  54.7 4.2 %all-to-all-start.1 = ((bf16[8,144,1024]{2,1,0:T(8,128)(2,1)}), bf16[8,144,1024]{2,1,0:T(8,128)(2,1)S(1)}, u32[]{:S(2)}, u32[]{:S(2)}) async-start(bf16[8,144,1024]{2,1,0:T(8,128)(2,1)} %shard_map.85), calls=%async_computation.1 | async-start | bytes 4718592 | tf_op jit(solution)/shard_map/all_to_all | solution.py:309
  58.9 4.9 %collective-permute-start.1 = (bf16[48,1024]{1,0:T(8,128)(2,1)S(1)}, bf16[48,1024]{1,0:T(8,128)(2,1)S(1)}, u32[]{:S(2)}, u32[]{:S(2)}) collective-permute-start(bf16[48,1024]{1,0:T(8,128)(2,1)S(1)} %get-tuple-element.31), channel_id=1, source_target_pairs={{0,48},{48,0},{1,49},{49,1},{2,50},{50,2},{3,51},{51,3},{4,52},{52... | collective-permute-start | bytes 294920 | tf_op jit(solution)/shard_map/ppermute | solution.py:310
  63.8 26.1 %collective-permute-done.1.other_ref = bf16[48,1024]{1,0:T(8,128)(2,1)S(1)} collective-permute-done((bf16[48,1024]{1,0:T(8,128)(2,1)S(1)}, bf16[48,1024]{1,0:T(8,128)(2,1)S(1)}, u32[]{:S(2)}, u32[]{:S(2)}) %collective-permute-start.1) | collective-permute-done | bytes 98336 | tf_op jit(solution)/shard_map/ppermute | solution.py:310
  89.9 0.0 all-to-all-done.1.pieces_ref
  89.9 1.1 shard_map.87
  91.0 13.5 %all-to-all-start.2 = ((bf16[24,8,1024]{2,1,0:T(8,128)(2,1)}), bf16[24,8,1024]{2,1,0:T(8,128)(2,1)S(1)}, u32[]{:S(2)}, u32[]{:S(2)}) async-start(bf16[24,8,1024]{2,1,0:T(8,128)(2,1)} %bitcast.11), calls=%async_computation.2 | async-start | bytes 786432 | tf_op jit(solution)/shard_map/all_to_all | solution.py:314
  104.5 3.7 %shard_map.84 = bf16[256,1024]{1,0:T(8,128)(2,1)} custom-call(bf16[256,1024]{1,0:T(8,128)(2,1)S(1)} %all_gather.35.grad_ref, bf16[1024,1024]{1,0:T(8,128)(2,1)} %b_hbm.3), custom_call_target="tpu_custom_call" | custom-call | flops 536870912 | bytes 3145728 | tf_op jit(solution)/shard_map/pallas_call | solution.py:318
  108.2 20.8 %all-to-all-done.2.pieces_ref = bf16[24,8,1024]{2,1,0:T(8,128)(2,1)S(1)} async-done(((bf16[24,8,1024]{2,1,0:T(8,128)(2,1)}), bf16[24,8,1024]{2,1,0:T(8,128)(2,1)S(1)}, u32[]{:S(2)}, u32[]{:S(2)}) %all-to-all-start.2) | async-done | bytes 393248 | tf_op jit(solution)/shard_map/all_to_all | solution.py:314
  129.0 0.7 shard_map.88
  (3 shorter events, 0.1 us)
Async XLA Ops:
  2.9 11.6 %copy-start.2 = (f32[1024]{0:T(1024)S(1)}, f32[1024]{0:T(1024)}, u32[]{:S(2)}) copy-start(f32[1024]{0:T(1024)} %param.8) | copy-start | bytes 12292
  2.9 13.9 %copy-start = (bf16[1024,512]{1,0:T(8,128)(2,1)S(1)}, bf16[1024,512]{1,0:T(8,128)(2,1)}, u32[]{:S(2)}) copy-start(bf16[1024,512]{1,0:T(8,128)(2,1)} %head_ref.5) | copy-start | bytes 3145732
  5.3 17.4 %copy-start.3 = (s32[256]{0:T(256)S(1)}, s32[256]{0:T(256)}, u32[]{:S(2)}) copy-start(s32[256]{0:T(256)} %param.10) | copy-start | bytes 3076
  5.3 17.4 %copy-start.4 = (s32[256]{0:T(256)S(1)}, s32[256]{0:T(256)}, u32[]{:S(2)}) copy-start(s32[256]{0:T(256)} %param.11) | copy-start | bytes 3076
  23.6 4.3 %collective-permute-start = (bf16[128,1024]{1,0:T(8,128)(2,1)S(1)}, bf16[128,1024]{1,0:T(8,128)(2,1)S(1)}, u32[]{:S(2)}, u32[]{:S(2)}) collective-permute-start(bf16[128,1024]{1,0:T(8,128)(2,1)S(1)} %shard_map.80), channel_id=1, source_target_pairs={{0,1},{1,0},{2,3},{3,2},{4,5},{5,4},{6,7},{7,6},{8,9},{9,8},{10,11... | collective-permute-start | bytes 786440 | tf_op jit(solution)/shard_map/ppermute | solution.py:289
  28.0 24.4 %copy-start.1 = (bf16[256,1024]{1,0:T(8,128)(2,1)S(1)}, bf16[256,1024]{1,0:T(8,128)(2,1)}, u32[]{:S(2)}) copy-start(bf16[256,1024]{1,0:T(8,128)(2,1)} %hidden_ref.1) | copy-start | bytes 1572868
  28.0 26.6 %all-to-all-start = ((bf16[4,96,1024]{2,1,0:T(8,128)(2,1)}), bf16[4,96,1024]{2,1,0:T(8,128)(2,1)S(1)}, u32[]{:S(2)}, u32[]{:S(2)}) async-start(bf16[4,96,1024]{2,1,0:T(8,128)(2,1)} %get-tuple-element.27), calls=%async_computation | async-start | bytes 1572864 | tf_op jit(solution)/shard_map/all_to_all | solution.py:291
  54.7 35.2 %all-to-all-start.1 = ((bf16[8,144,1024]{2,1,0:T(8,128)(2,1)}), bf16[8,144,1024]{2,1,0:T(8,128)(2,1)S(1)}, u32[]{:S(2)}, u32[]{:S(2)}) async-start(bf16[8,144,1024]{2,1,0:T(8,128)(2,1)} %shard_map.85), calls=%async_computation.1 | async-start | bytes 4718592 | tf_op jit(solution)/shard_map/all_to_all | solution.py:309
  58.9 31.0 %collective-permute-start.1 = (bf16[48,1024]{1,0:T(8,128)(2,1)S(1)}, bf16[48,1024]{1,0:T(8,128)(2,1)S(1)}, u32[]{:S(2)}, u32[]{:S(2)}) collective-permute-start(bf16[48,1024]{1,0:T(8,128)(2,1)S(1)} %get-tuple-element.31), channel_id=1, source_target_pairs={{0,48},{48,0},{1,49},{49,1},{2,50},{50,2},{3,51},{51,3},{4,52},{52... | collective-permute-start | bytes 294920 | tf_op jit(solution)/shard_map/ppermute | solution.py:310
  91.0 38.0 %all-to-all-start.2 = ((bf16[24,8,1024]{2,1,0:T(8,128)(2,1)}), bf16[24,8,1024]{2,1,0:T(8,128)(2,1)S(1)}, u32[]{:S(2)}, u32[]{:S(2)}) async-start(bf16[24,8,1024]{2,1,0:T(8,128)(2,1)} %bitcast.11), calls=%async_computation.2 | async-start | bytes 786432 | tf_op jit(solution)/shard_map/all_to_all | solution.py:314

commit v12 on v11

--- a/solution.py
+++ b/solution.py
@@ -149,16 +149,24 @@
 
 
 def grad_blocks(hidden_ref, grad_ref, head_ref, out_hbm, out_ref, sems):
-    step = 16
+    step, copies = 16, []
     for first in range(0, LATE_BLOCKS, step):
         if first < PROJ_BLOCKS:
             part = dot(hidden_ref[:, 8 * first : 8 * (first + step)], grad_ref[...], 0, 0).astype(bf16)
         for i in range(step):
             yh, yl, xh, zh, zl = place(first + i)
-            row = 8 * (zh * 3 + yh)
+            row = 8 * (yh * 6 + zh)
             block = part[8 * i : 8 * i + 8] if first < PROJ_BLOCKS else head_ref[i]
             out_ref[(xh * 2 + yl) * 2 + zl, row : row + 8, :] = block
-    for copy in copy_out(out_ref, out_hbm, sems):
+        if (first + step) % 48 == 0:
+            done = first // 48
+            rows = slice(48 * done, 48 * done + 48)
+            for near in range(N_NEAR):
+                copies.append(
+                    pltpu.make_async_copy(out_ref.at[near, rows], out_hbm.at[near, rows], sems.at[N_NEAR * done + near])
+                )
+                copies[-1].start()
+    for copy in copies:
         copy.wait()
 
 
@@ -189,11 +197,12 @@
 
 def near_sum(pieces_ref, kept_ref, other_ref, out_ref):
     for zh in range(6):
-        window = slice(24 * zh, 24 * zh + 24)
-        out_ref[32 * zh : 32 * zh + 24] = add_up(pieces_ref.at[:, window]).astype(out_ref.dtype)
-        window = slice(8 * zh, 8 * zh + 8)
+        for yh in range(3):
+            first, row = 8 * (yh * 6 + zh), 8 * (zh * 4 + yh)
+            out_ref[row : row + 8] = add_up(pieces_ref.at[:, first : first + 8]).astype(out_ref.dtype)
+        window, row = slice(8 * zh, 8 * zh + 8), 8 * (zh * 4 + 3)
         early = kept_ref[window] + other_ref[window].astype(f32)
-        out_ref[32 * zh + 24 : 32 * zh + 32] = early.astype(out_ref.dtype)
+        out_ref[row : row + 8] = early.astype(out_ref.dtype)
 
 
 def far_sum(is_proj_ref, pieces_ref, out_ref):
@@ -299,7 +308,7 @@
         out_specs=hbm,
         scratch_shapes=[
             pltpu.VMEM((N_NEAR, LATE_BLOCKS, width), bf16),
-            pltpu.SemaphoreType.DMA((N_NEAR,)),
+            pltpu.SemaphoreType.DMA((3 * N_NEAR,)),
         ],
         compiler_params=pltpu.CompilerParams(vmem_limit_bytes=VMEM_BYTES),
     )(hidden, row_grad, late_head)

time: 130 us -> 130 us (level)
  no operation moved by 1% of the time
where the time goes in v12:
time: 130 us; the launch traced here: 129 us
  waiting for transfers between devices  46.9 us (36%)
  starting transfers between devices  37.8 us (29%)
  blocking collectives  29.6 us (23%)
  Pallas kernels  13.9 us (11%)
    ppermute x1, waiting for transfers between devices, local(): early_other = lax.ppermute(early_sent, 'xh', SWAP)  26.1 us
    all_to_all x1, waiting for transfers between devices, local(): far = lax.all_to_all(near.reshape(N_FAR, 8, width), FAR, 0, 0)  20.8 us
    all_to_all x1, starting transfers between devices, local(): far = lax.all_to_all(near.reshape(N_FAR, 8, width), FAR, 0, 0)  13.5 us
    all_to_all x1, starting transfers between devices, local(): early = lax.all_to_all(early, EARLY, 0, 0)  13.1 us
    all_gather x1, blocking collectives, local(): pieces = lax.all_gather(chip, 'xl')  9.02 us
    all_gather x1, blocking collectives, local(): lax.all_gather(chip, 'xl')  8.79 us
    all_gather x1, blocking collectives, local(): totals = lax.all_gather(sums, TP, tiled=True)  5.08 us
    ppermute x1, starting transfers between devices, local(): early_other = lax.ppermute(early_sent, 'xh', SWAP)  4.87 us
  transfers between devices with their start and end apart: 5, of which 2 were waited for; matrix products, arithmetic and copies ran while one was open for 0% of the time, Pallas kernels for 6%

profile of v12, /device:TPU:8, one launch (start us, length us, event | category | flops | bytes accessed | tf_op | source)
XLA Modules:
  0.0 129.4 jit_solution(1462154758100258195)
XLA Ops:
  0.6 2.2 %shard_map.77 = (bf16[128,1024]{1,0:T(8,128)(2,1)S(1)}, f32[128,1024]{1,0:T(8,128)S(1)}) custom-call(s32[1]{0:T(128)} %bitcast.half_ref, bf16[256,1024]{1,0:T(8,128)(2,1)} %hidden_ref.1, bf16[1024,1024]{1,0:T(8,128)(2,1)} %b_hbm.3), custom_call_target="tpu_custom_call" | custom-call | tf_op jit(solution)/shard_map/pallas_call | solution.py:252
  2.9 0.0 copy-start.2
  2.9 0.0 copy-start
  2.9 2.3 %all-gather = bf16[256,1024]{1,0:T(8,128)(2,1)S(1)} all-gather(bf16[128,1024]{1,0:T(8,128)(2,1)S(1)} %get-tuple-element.18), channel_id=2, replica_groups=mesh['yh'=4,'yl'=2,'xh'=2,'zh'=6,'zl'=2,'xl'=2,'core'=2] {'core'}, dimensions={0}, use_global_device_ids=true | all-gather | bytes 786432 | tf_op jit(solution)/shard_map/all_gather | solution.py:264
  5.3 0.0 copy-start.3
  5.3 0.0 copy-start.4
  5.3 9.0 %all-gather.1 = bf16[256,1024]{1,0:T(8,128)(2,1)S(1)} all-gather(bf16[128,1024]{1,0:T(8,128)(2,1)S(1)} %shard_map.78), channel_id=3, replica_groups=mesh['yh'=4,'yl'=2,'xh'=2,'zh'=6,'zl'=2,'xl'=2,'core'=2] {'xl'}, dimensions={0}, use_global_device_ids=true | all-gather | bytes 786432 | tf_op jit(solution)/shard_map/all_gather | solution.py:265
  14.3 0.2 multiply_reduce_fusion
  14.5 0.0 copy-done.2
  14.5 0.1 multiply_convert_fusion
  14.6 2.2 %all_gather.31.normed_ref = bf16[256,1024]{1,0:T(8,128)(2,1)S(1)} all-gather(bf16[128,1024]{1,0:T(8,128)(2,1)S(1)} %multiply_convert_fusion), channel_id=1, replica_groups=mesh['yh'=4,'yl'=2,'xh'=2,'zh'=6,'zl'=2,'xl'=2,'core'=2] {'core'}, dimensions={0}, use_global_device_ids=true | all-gather | bytes 786432 | tf_op jit(solution)/shard_map/all_gather | solution.py:269
  16.8 0.0 copy-done
  16.8 0.8 shard_map.79
  17.6 5.1 %all-gather.3 = f32[4,1,256]{2,1,0:T(1,128)S(1)} all-gather(f32[1,1,256]{2,1,0:T(1,128)S(1)} %bitcast.26), channel_id=1, replica_groups=mesh['yh'=4,'yl'=2,'xh'=2,'zh'=6,'zl'=2,'xl'=2,'core'=2] {'xl','core'}, dimensions={0}, use_global_device_ids=true | all-gather | bytes 5120 | tf_op jit(solution)/shard_map/all_gather | solution.py:274
  22.7 0.0 copy-done.3
  22.7 0.0 copy-done.4
  22.7 0.9 shard_map.80
  23.6 2.2 %collective-permute-start = (bf16[128,1024]{1,0:T(8,128)(2,1)S(1)}, bf16[128,1024]{1,0:T(8,128)(2,1)S(1)}, u32[]{:S(2)}, u32[]{:S(2)}) collective-permute-start(bf16[128,1024]{1,0:T(8,128)(2,1)S(1)} %shard_map.80), channel_id=1, source_target_pairs={{0,1},{1,0},{2,3},{3,2},{4,5},{5,4},{6,7},{7,6},{8,9},{9,8},{10,11... | collective-permute-start | bytes 786440 | tf_op jit(solution)/shard_map/ppermute | solution.py:298
  25.8 2.1 %shard_map.81 = (f32[128,1024]{1,0:T(8,128)S(1)}, bf16[16,8,1024]{2,1,0:T(8,128)(2,1)S(1)}, bf16[4,96,1024]{2,1,0:T(8,128)(2,1)}) custom-call(s32[1]{0:T(128)} %bitcast.half_ref, s32[1]{0:T(128)} %bitcast.3.column_ref, f32[256,512]{1,0:T(8,128)S(1)} %get-tuple-element.21.exp_ref, f32[4,256]{1,0:T(4,128)S(1)} %bitcast.20, s32[1,256]{1,0:T(1,128)S(1)} %bitcast.23, ...), custom_call_target="tpu_custom_call" | custom-call | tf_op jit(solution)/shard_map/pallas_call | solution.py:282
  27.9 0.0 collective-permute-done.other_ref
  27.9 0.1 shard_map.82
  28.0 0.0 copy-start.1
  28.0 13.1 %all-to-all-start = ((bf16[4,96,1024]{2,1,0:T(8,128)(2,1)}), bf16[4,96,1024]{2,1,0:T(8,128)(2,1)S(1)}, u32[]{:S(2)}, u32[]{:S(2)}) async-start(bf16[4,96,1024]{2,1,0:T(8,128)(2,1)} %get-tuple-element.27), calls=%async_computation | async-start | bytes 1572864 | tf_op jit(solution)/shard_map/all_to_all | solution.py:300
  41.1 8.8 %all-gather.2 = bf16[256,1024]{1,0:T(8,128)(2,1)S(1)} all-gather(bf16[128,1024]{1,0:T(8,128)(2,1)S(1)} %shard_map.82), channel_id=4, replica_groups=mesh['yh'=4,'yl'=2,'xh'=2,'zh'=6,'zl'=2,'xl'=2,'core'=2] {'xl'}, dimensions={0}, use_global_device_ids=true | all-gather | bytes 786432 | tf_op jit(solution)/shard_map/all_gather | solution.py:301
  49.8 0.3 shard_map.83
  50.1 2.2 %all_gather.35.grad_ref = bf16[256,1024]{1,0:T(8,128)(2,1)S(1)} all-gather(bf16[128,1024]{1,0:T(8,128)(2,1)S(1)} %shard_map.83), channel_id=1, replica_groups=mesh['yh'=4,'yl'=2,'xh'=2,'zh'=6,'zl'=2,'xl'=2,'core'=2] {'core'}, dimensions={0}, use_global_device_ids=true | all-gather | bytes 786432 | tf_op jit(solution)/shard_map/all_gather | solution.py:302
  52.3 0.0 copy-done.1
  52.3 2.0 %shard_map.85 = bf16[8,144,1024]{2,1,0:T(8,128)(2,1)} custom-call(bf16[256,1024]{1,0:T(8,128)(2,1)S(1)} %copy-done.1, bf16[256,1024]{1,0:T(8,128)(2,1)S(1)} %all_gather.35.grad_ref, bf16[16,8,1024]{2,1,0:T(8,128)(2,1)S(1)} %get-tuple-element.26.head_ref), custom_call_target="tpu_custom_call" | custom-call | tf_op jit(solution)/shard_map/pallas_call | solution.py:304
  54.4 0.0 all-to-all-done.pieces_ref
  54.4 0.1 shard_map.86
  54.5 4.2 %all-to-all-start.1 = ((bf16[8,144,1024]{2,1,0:T(8,128)(2,1)}), bf16[8,144,1024]{2,1,0:T(8,128)(2,1)S(1)}, u32[]{:S(2)}, u32[]{:S(2)}) async-start(bf16[8,144,1024]{2,1,0:T(8,128)(2,1)} %shard_map.85), calls=%async_computation.1 | async-start | bytes 4718592 | tf_op jit(solution)/shard_map/all_to_all | solution.py:318
  58.7 4.9 %collective-permute-start.1 = (bf16[48,1024]{1,0:T(8,128)(2,1)S(1)}, bf16[48,1024]{1,0:T(8,128)(2,1)S(1)}, u32[]{:S(2)}, u32[]{:S(2)}) collective-permute-start(bf16[48,1024]{1,0:T(8,128)(2,1)S(1)} %get-tuple-element.31), channel_id=1, source_target_pairs={{0,48},{48,0},{1,49},{49,1},{2,50},{50,2},{3,51},{51,3},{4,52},{52... | collective-permute-start | bytes 294920 | tf_op jit(solution)/shard_map/ppermute | solution.py:319
  63.6 26.1 %collective-permute-done.1.other_ref = bf16[48,1024]{1,0:T(8,128)(2,1)S(1)} collective-permute-done((bf16[48,1024]{1,0:T(8,128)(2,1)S(1)}, bf16[48,1024]{1,0:T(8,128)(2,1)S(1)}, u32[]{:S(2)}, u32[]{:S(2)}) %collective-permute-start.1) | collective-permute-done | bytes 98336 | tf_op jit(solution)/shard_map/ppermute | solution.py:319
  89.7 0.0 all-to-all-done.1.pieces_ref
  89.7 1.1 shard_map.87
  90.7 13.5 %all-to-all-start.2 = ((bf16[24,8,1024]{2,1,0:T(8,128)(2,1)}), bf16[24,8,1024]{2,1,0:T(8,128)(2,1)S(1)}, u32[]{:S(2)}, u32[]{:S(2)}) async-start(bf16[24,8,1024]{2,1,0:T(8,128)(2,1)} %bitcast.11), calls=%async_computation.2 | async-start | bytes 786432 | tf_op jit(solution)/shard_map/all_to_all | solution.py:323
  104.2 3.7 %shard_map.84 = bf16[256,1024]{1,0:T(8,128)(2,1)} custom-call(bf16[256,1024]{1,0:T(8,128)(2,1)S(1)} %all_gather.35.grad_ref, bf16[1024,1024]{1,0:T(8,128)(2,1)} %b_hbm.3), custom_call_target="tpu_custom_call" | custom-call | flops 536870912 | bytes 3145728 | tf_op jit(solution)/shard_map/pallas_call | solution.py:327
  107.9 20.8 %all-to-all-done.2.pieces_ref = bf16[24,8,1024]{2,1,0:T(8,128)(2,1)S(1)} async-done(((bf16[24,8,1024]{2,1,0:T(8,128)(2,1)}), bf16[24,8,1024]{2,1,0:T(8,128)(2,1)S(1)}, u32[]{:S(2)}, u32[]{:S(2)}) %all-to-all-start.2) | async-done | bytes 393248 | tf_op jit(solution)/shard_map/all_to_all | solution.py:323
  128.8 0.7 shard_map.88
  (3 shorter events, 0.1 us)
Async XLA Ops:
  2.9 11.6 %copy-start.2 = (f32[1024]{0:T(1024)S(1)}, f32[1024]{0:T(1024)}, u32[]{:S(2)}) copy-start(f32[1024]{0:T(1024)} %param.8) | copy-start | bytes 12292
  2.9 13.9 %copy-start = (bf16[1024,512]{1,0:T(8,128)(2,1)S(1)}, bf16[1024,512]{1,0:T(8,128)(2,1)}, u32[]{:S(2)}) copy-start(bf16[1024,512]{1,0:T(8,128)(2,1)} %head_ref.5) | copy-start | bytes 3145732
  5.3 17.4 %copy-start.3 = (s32[256]{0:T(256)S(1)}, s32[256]{0:T(256)}, u32[]{:S(2)}) copy-start(s32[256]{0:T(256)} %param.10) | copy-start | bytes 3076
  5.3 17.4 %copy-start.4 = (s32[256]{0:T(256)S(1)}, s32[256]{0:T(256)}, u32[]{:S(2)}) copy-start(s32[256]{0:T(256)} %param.11) | copy-start | bytes 3076
  23.6 4.3 %collective-permute-start = (bf16[128,1024]{1,0:T(8,128)(2,1)S(1)}, bf16[128,1024]{1,0:T(8,128)(2,1)S(1)}, u32[]{:S(2)}, u32[]{:S(2)}) collective-permute-start(bf16[128,1024]{1,0:T(8,128)(2,1)S(1)} %shard_map.80), channel_id=1, source_target_pairs={{0,1},{1,0},{2,3},{3,2},{4,5},{5,4},{6,7},{7,6},{8,9},{9,8},{10,11... | collective-permute-start | bytes 786440 | tf_op jit(solution)/shard_map/ppermute | solution.py:298
  28.0 24.4 %copy-start.1 = (bf16[256,1024]{1,0:T(8,128)(2,1)S(1)}, bf16[256,1024]{1,0:T(8,128)(2,1)}, u32[]{:S(2)}) copy-start(bf16[256,1024]{1,0:T(8,128)(2,1)} %hidden_ref.1) | copy-start | bytes 1572868
  28.0 26.4 %all-to-all-start = ((bf16[4,96,1024]{2,1,0:T(8,128)(2,1)}), bf16[4,96,1024]{2,1,0:T(8,128)(2,1)S(1)}, u32[]{:S(2)}, u32[]{:S(2)}) async-start(bf16[4,96,1024]{2,1,0:T(8,128)(2,1)} %get-tuple-element.27), calls=%async_computation | async-start | bytes 1572864 | tf_op jit(solution)/shard_map/all_to_all | solution.py:300
  54.5 35.2 %all-to-all-start.1 = ((bf16[8,144,1024]{2,1,0:T(8,128)(2,1)}), bf16[8,144,1024]{2,1,0:T(8,128)(2,1)S(1)}, u32[]{:S(2)}, u32[]{:S(2)}) async-start(bf16[8,144,1024]{2,1,0:T(8,128)(2,1)} %shard_map.85), calls=%async_computation.1 | async-start | bytes 4718592 | tf_op jit(solution)/shard_map/all_to_all | solution.py:318
  58.7 31.0 %collective-permute-start.1 = (bf16[48,1024]{1,0:T(8,128)(2,1)S(1)}, bf16[48,1024]{1,0:T(8,128)(2,1)S(1)}, u32[]{:S(2)}, u32[]{:S(2)}) collective-permute-start(bf16[48,1024]{1,0:T(8,128)(2,1)S(1)} %get-tuple-element.31), channel_id=1, source_target_pairs={{0,48},{48,0},{1,49},{49,1},{2,50},{50,2},{3,51},{51,3},{4,52},{52... | collective-permute-start | bytes 294920 | tf_op jit(solution)/shard_map/ppermute | solution.py:319
  90.7 38.0 %all-to-all-start.2 = ((bf16[24,8,1024]{2,1,0:T(8,128)(2,1)}), bf16[24,8,1024]{2,1,0:T(8,128)(2,1)S(1)}, u32[]{:S(2)}, u32[]{:S(2)}) async-start(bf16[24,8,1024]{2,1,0:T(8,128)(2,1)} %bitcast.11), calls=%async_computation.2 | async-start | bytes 786432 | tf_op jit(solution)/shard_map/all_to_all | solution.py:323

commit v13 on v12

--- a/solution.py
+++ b/solution.py
@@ -248,7 +248,7 @@
     code, mask = code_ids[None, :], stream_mask[None, :]
     first_column = (tp * vocab_part).reshape(1)
 
-    steps, inner = 4, hidden.shape[1]
+    steps, inner = 2, hidden.shape[1]
     sent, kept = pl.pallas_call(
         streamed_product,
         out_shape=[shape((half, width), bf16), shape((half, width), f32)],

time: 130 us -> 130 us (level)
  no operation moved by 1% of the time
where the time goes in v13:
time: 130 us
  waiting for transfers between devices  47.7 us (37%)
  starting transfers between devices  37.8 us (29%)
  blocking collectives  29.6 us (23%)
  Pallas kernels  13.5 us (10%)
    ppermute x1, waiting for transfers between devices, local(): early_other = lax.ppermute(early_sent, 'xh', SWAP)  26.1 us
    all_to_all x1, waiting for transfers between devices, local(): far = lax.all_to_all(near.reshape(N_FAR, 8, width), FAR, 0, 0)  21.6 us
    all_to_all x1, starting transfers between devices, local(): far = lax.all_to_all(near.reshape(N_FAR, 8, width), FAR, 0, 0)  13.5 us
    all_to_all x1, starting transfers between devices, local(): early = lax.all_to_all(early, EARLY, 0, 0)  13.1 us
    all_gather x1, blocking collectives, local(): pieces = lax.all_gather(chip, 'xl')  9.02 us
    all_gather x1, blocking collectives, local(): lax.all_gather(chip, 'xl')  8.78 us
    all_gather x1, blocking collectives, local(): totals = lax.all_gather(sums, TP, tiled=True)  5.08 us
    ppermute x1, starting transfers between devices, local(): early_other = lax.ppermute(early_sent, 'xh', SWAP)  4.87 us
  transfers between devices with their start and end apart: 5, of which 2 were waited for; matrix products, arithmetic and copies ran while one was open for 0% of the time, Pallas kernels for 6%

profile of v13, /device:TPU:8, one launch (start us, length us, event | category | flops | bytes accessed | tf_op | source)
XLA Modules:
  0.0 129.7 jit_solution(17790599545795587741)
XLA Ops:
  0.6 2.5 %shard_map.77 = (bf16[128,1024]{1,0:T(8,128)(2,1)S(1)}, f32[128,1024]{1,0:T(8,128)S(1)}) custom-call(s32[1]{0:T(128)} %bitcast.half_ref, bf16[256,1024]{1,0:T(8,128)(2,1)} %hidden_ref.1, bf16[1024,1024]{1,0:T(8,128)(2,1)} %b_hbm.3), custom_call_target="tpu_custom_call" | custom-call | tf_op jit(solution)/shard_map/pallas_call | solution.py:252
  3.1 0.0 copy-start.2
  3.1 0.0 copy-start
  3.1 2.3 %all-gather = bf16[256,1024]{1,0:T(8,128)(2,1)S(1)} all-gather(bf16[128,1024]{1,0:T(8,128)(2,1)S(1)} %get-tuple-element.18), channel_id=2, replica_groups=mesh['yh'=4,'yl'=2,'xh'=2,'zh'=6,'zl'=2,'xl'=2,'core'=2] {'core'}, dimensions={0}, use_global_device_ids=true | all-gather | bytes 786432 | tf_op jit(solution)/shard_map/all_gather | solution.py:264
  5.5 0.0 copy-start.3
  5.5 0.0 copy-start.4
  5.5 9.0 %all-gather.1 = bf16[256,1024]{1,0:T(8,128)(2,1)S(1)} all-gather(bf16[128,1024]{1,0:T(8,128)(2,1)S(1)} %shard_map.78), channel_id=3, replica_groups=mesh['yh'=4,'yl'=2,'xh'=2,'zh'=6,'zl'=2,'xl'=2,'core'=2] {'xl'}, dimensions={0}, use_global_device_ids=true | all-gather | bytes 786432 | tf_op jit(solution)/shard_map/all_gather | solution.py:265
  14.5 0.2 multiply_reduce_fusion
  14.7 0.0 copy-done.2
  14.7 0.1 multiply_convert_fusion
  14.8 2.2 %all_gather.31.normed_ref = bf16[256,1024]{1,0:T(8,128)(2,1)S(1)} all-gather(bf16[128,1024]{1,0:T(8,128)(2,1)S(1)} %multiply_convert_fusion), channel_id=1, replica_groups=mesh['yh'=4,'yl'=2,'xh'=2,'zh'=6,'zl'=2,'xl'=2,'core'=2] {'core'}, dimensions={0}, use_global_device_ids=true | all-gather | bytes 786432 | tf_op jit(solution)/shard_map/all_gather | solution.py:269
  17.0 0.0 copy-done
  17.0 0.8 shard_map.79
  17.8 5.1 %all-gather.3 = f32[4,1,256]{2,1,0:T(1,128)S(1)} all-gather(f32[1,1,256]{2,1,0:T(1,128)S(1)} %bitcast.26), channel_id=1, replica_groups=mesh['yh'=4,'yl'=2,'xh'=2,'zh'=6,'zl'=2,'xl'=2,'core'=2] {'xl','core'}, dimensions={0}, use_global_device_ids=true | all-gather | bytes 5120 | tf_op jit(solution)/shard_map/all_gather | solution.py:274
  22.9 0.0 copy-done.3
  22.9 0.0 copy-done.4
  22.9 0.9 shard_map.80
  23.8 2.2 %collective-permute-start = (bf16[128,1024]{1,0:T(8,128)(2,1)S(1)}, bf16[128,1024]{1,0:T(8,128)(2,1)S(1)}, u32[]{:S(2)}, u32[]{:S(2)}) collective-permute-start(bf16[128,1024]{1,0:T(8,128)(2,1)S(1)} %shard_map.80), channel_id=1, source_target_pairs={{0,1},{1,0},{2,3},{3,2},{4,5},{5,4},{6,7},{7,6},{8,9},{9,8},{10,11... | collective-permute-start | bytes 786440 | tf_op jit(solution)/shard_map/ppermute | solution.py:298
  26.0 2.1 %shard_map.81 = (f32[128,1024]{1,0:T(8,128)S(1)}, bf16[16,8,1024]{2,1,0:T(8,128)(2,1)S(1)}, bf16[4,96,1024]{2,1,0:T(8,128)(2,1)}) custom-call(s32[1]{0:T(128)} %bitcast.half_ref, s32[1]{0:T(128)} %bitcast.3.column_ref, f32[256,512]{1,0:T(8,128)S(1)} %get-tuple-element.21.exp_ref, f32[4,256]{1,0:T(4,128)S(1)} %bitcast.20, s32[1,256]{1,0:T(1,128)S(1)} %bitcast.23, ...), custom_call_target="tpu_custom_call" | custom-call | tf_op jit(solution)/shard_map/pallas_call | solution.py:282
  28.1 0.0 collective-permute-done.other_ref
  28.1 0.1 shard_map.82
  28.2 0.0 copy-start.1
  28.2 13.1 %all-to-all-start = ((bf16[4,96,1024]{2,1,0:T(8,128)(2,1)}), bf16[4,96,1024]{2,1,0:T(8,128)(2,1)S(1)}, u32[]{:S(2)}, u32[]{:S(2)}) async-start(bf16[4,96,1024]{2,1,0:T(8,128)(2,1)} %get-tuple-element.27), calls=%async_computation | async-start | bytes 1572864 | tf_op jit(solution)/shard_map/all_to_all | solution.py:300
  41.3 8.8 %all-gather.2 = bf16[256,1024]{1,0:T(8,128)(2,1)S(1)} all-gather(bf16[128,1024]{1,0:T(8,128)(2,1)S(1)} %shard_map.82), channel_id=4, replica_groups=mesh['yh'=4,'yl'=2,'xh'=2,'zh'=6,'zl'=2,'xl'=2,'core'=2] {'xl'}, dimensions={0}, use_global_device_ids=true | all-gather | bytes 786432 | tf_op jit(solution)/shard_map/all_gather | solution.py:301
  50.0 0.3 shard_map.83
  50.3 2.2 %all_gather.35.grad_ref = bf16[256,1024]{1,0:T(8,128)(2,1)S(1)} all-gather(bf16[128,1024]{1,0:T(8,128)(2,1)S(1)} %shard_map.83), channel_id=1, replica_groups=mesh['yh'=4,'yl'=2,'xh'=2,'zh'=6,'zl'=2,'xl'=2,'core'=2] {'core'}, dimensions={0}, use_global_device_ids=true | all-gather | bytes 786432 | tf_op jit(solution)/shard_map/all_gather | solution.py:302
  52.5 0.0 copy-done.1
  52.5 2.0 %shard_map.85 = bf16[8,144,1024]{2,1,0:T(8,128)(2,1)} custom-call(bf16[256,1024]{1,0:T(8,128)(2,1)S(1)} %copy-done.1, bf16[256,1024]{1,0:T(8,128)(2,1)S(1)} %all_gather.35.grad_ref, bf16[16,8,1024]{2,1,0:T(8,128)(2,1)S(1)} %get-tuple-element.26.head_ref), custom_call_target="tpu_custom_call" | custom-call | tf_op jit(solution)/shard_map/pallas_call | solution.py:304
  54.6 0.0 all-to-all-done.pieces_ref
  54.6 0.1 shard_map.86
  54.7 4.2 %all-to-all-start.1 = ((bf16[8,144,1024]{2,1,0:T(8,128)(2,1)}), bf16[8,144,1024]{2,1,0:T(8,128)(2,1)S(1)}, u32[]{:S(2)}, u32[]{:S(2)}) async-start(bf16[8,144,1024]{2,1,0:T(8,128)(2,1)} %shard_map.85), calls=%async_computation.1 | async-start | bytes 4718592 | tf_op jit(solution)/shard_map/all_to_all | solution.py:318
  58.9 4.9 %collective-permute-start.1 = (bf16[48,1024]{1,0:T(8,128)(2,1)S(1)}, bf16[48,1024]{1,0:T(8,128)(2,1)S(1)}, u32[]{:S(2)}, u32[]{:S(2)}) collective-permute-start(bf16[48,1024]{1,0:T(8,128)(2,1)S(1)} %get-tuple-element.31), channel_id=1, source_target_pairs={{0,48},{48,0},{1,49},{49,1},{2,50},{50,2},{3,51},{51,3},{4,52},{52... | collective-permute-start | bytes 294920 | tf_op jit(solution)/shard_map/ppermute | solution.py:319
  63.8 26.1 %collective-permute-done.1.other_ref = bf16[48,1024]{1,0:T(8,128)(2,1)S(1)} collective-permute-done((bf16[48,1024]{1,0:T(8,128)(2,1)S(1)}, bf16[48,1024]{1,0:T(8,128)(2,1)S(1)}, u32[]{:S(2)}, u32[]{:S(2)}) %collective-permute-start.1) | collective-permute-done | bytes 98336 | tf_op jit(solution)/shard_map/ppermute | solution.py:319
  89.9 0.0 all-to-all-done.1.pieces_ref
  89.9 1.1 shard_map.87
  91.0 13.5 %all-to-all-start.2 = ((bf16[24,8,1024]{2,1,0:T(8,128)(2,1)}), bf16[24,8,1024]{2,1,0:T(8,128)(2,1)S(1)}, u32[]{:S(2)}, u32[]{:S(2)}) async-start(bf16[24,8,1024]{2,1,0:T(8,128)(2,1)} %bitcast.11), calls=%async_computation.2 | async-start | bytes 786432 | tf_op jit(solution)/shard_map/all_to_all | solution.py:323
  104.5 3.0 %shard_map.84 = bf16[256,1024]{1,0:T(8,128)(2,1)} custom-call(bf16[256,1024]{1,0:T(8,128)(2,1)S(1)} %all_gather.35.grad_ref, bf16[1024,1024]{1,0:T(8,128)(2,1)} %b_hbm.3), custom_call_target="tpu_custom_call" | custom-call | flops 536870912 | bytes 3145728 | tf_op jit(solution)/shard_map/pallas_call | solution.py:327
  107.4 21.6 %all-to-all-done.2.pieces_ref = bf16[24,8,1024]{2,1,0:T(8,128)(2,1)S(1)} async-done(((bf16[24,8,1024]{2,1,0:T(8,128)(2,1)}), bf16[24,8,1024]{2,1,0:T(8,128)(2,1)S(1)}, u32[]{:S(2)}, u32[]{:S(2)}) %all-to-all-start.2) | async-done | bytes 393248 | tf_op jit(solution)/shard_map/all_to_all | solution.py:323
  129.0 0.7 shard_map.88
  (3 shorter events, 0.1 us)
Async XLA Ops:
  3.1 11.6 %copy-start.2 = (f32[1024]{0:T(1024)S(1)}, f32[1024]{0:T(1024)}, u32[]{:S(2)}) copy-start(f32[1024]{0:T(1024)} %param.8) | copy-start | bytes 12292
  3.1 13.9 %copy-start = (bf16[1024,512]{1,0:T(8,128)(2,1)S(1)}, bf16[1024,512]{1,0:T(8,128)(2,1)}, u32[]{:S(2)}) copy-start(bf16[1024,512]{1,0:T(8,128)(2,1)} %head_ref.5) | copy-start | bytes 3145732
  5.5 17.4 %copy-start.3 = (s32[256]{0:T(256)S(1)}, s32[256]{0:T(256)}, u32[]{:S(2)}) copy-start(s32[256]{0:T(256)} %param.10) | copy-start | bytes 3076
  5.5 17.4 %copy-start.4 = (s32[256]{0:T(256)S(1)}, s32[256]{0:T(256)}, u32[]{:S(2)}) copy-start(s32[256]{0:T(256)} %param.11) | copy-start | bytes 3076
  23.8 4.3 %collective-permute-start = (bf16[128,1024]{1,0:T(8,128)(2,1)S(1)}, bf16[128,1024]{1,0:T(8,128)(2,1)S(1)}, u32[]{:S(2)}, u32[]{:S(2)}) collective-permute-start(bf16[128,1024]{1,0:T(8,128)(2,1)S(1)} %shard_map.80), channel_id=1, source_target_pairs={{0,1},{1,0},{2,3},{3,2},{4,5},{5,4},{6,7},{7,6},{8,9},{9,8},{10,11... | collective-permute-start | bytes 786440 | tf_op jit(solution)/shard_map/ppermute | solution.py:298
  28.2 24.4 %copy-start.1 = (bf16[256,1024]{1,0:T(8,128)(2,1)S(1)}, bf16[256,1024]{1,0:T(8,128)(2,1)}, u32[]{:S(2)}) copy-start(bf16[256,1024]{1,0:T(8,128)(2,1)} %hidden_ref.1) | copy-start | bytes 1572868
  28.2 26.4 %all-to-all-start = ((bf16[4,96,1024]{2,1,0:T(8,128)(2,1)}), bf16[4,96,1024]{2,1,0:T(8,128)(2,1)S(1)}, u32[]{:S(2)}, u32[]{:S(2)}) async-start(bf16[4,96,1024]{2,1,0:T(8,128)(2,1)} %get-tuple-element.27), calls=%async_computation | async-start | bytes 1572864 | tf_op jit(solution)/shard_map/all_to_all | solution.py:300
  54.7 35.2 %all-to-all-start.1 = ((bf16[8,144,1024]{2,1,0:T(8,128)(2,1)}), bf16[8,144,1024]{2,1,0:T(8,128)(2,1)S(1)}, u32[]{:S(2)}, u32[]{:S(2)}) async-start(bf16[8,144,1024]{2,1,0:T(8,128)(2,1)} %shard_map.85), calls=%async_computation.1 | async-start | bytes 4718592 | tf_op jit(solution)/shard_map/all_to_all | solution.py:318
  58.9 31.0 %collective-permute-start.1 = (bf16[48,1024]{1,0:T(8,128)(2,1)S(1)}, bf16[48,1024]{1,0:T(8,128)(2,1)S(1)}, u32[]{:S(2)}, u32[]{:S(2)}) collective-permute-start(bf16[48,1024]{1,0:T(8,128)(2,1)S(1)} %get-tuple-element.31), channel_id=1, source_target_pairs={{0,48},{48,0},{1,49},{49,1},{2,50},{50,2},{3,51},{51,3},{4,52},{52... | collective-permute-start | bytes 294920 | tf_op jit(solution)/shard_map/ppermute | solution.py:319
  91.0 38.1 %all-to-all-start.2 = ((bf16[24,8,1024]{2,1,0:T(8,128)(2,1)}), bf16[24,8,1024]{2,1,0:T(8,128)(2,1)S(1)}, u32[]{:S(2)}, u32[]{:S(2)}) async-start(bf16[24,8,1024]{2,1,0:T(8,128)(2,1)} %bitcast.11), calls=%async_computation.2 | async-start | bytes 786432 | tf_op jit(solution)/shard_map/all_to_all | solution.py:323
